TPU v7x, 256 devices: a whole 4x4x8 slice. The times are simulated.
256 devices in a mesh: dp: 16 (over z, core), mp: 16 (over y, x).
Axes of the slice: x: 4, y: 4, z: 8, core: 2. Of those that a mesh axis runs over, the one named last changes fastest.
Arguments:
- candidates: bfloat16 [4096, 4096], P('dp', 'mp'), may hold values from -6 to 6
- hold_gate: bfloat16 [4096, 8192], P(None, 'mp'), may hold values from -0.09375 to 0.09375
- hold_up: bfloat16 [4096, 8192], P(None, 'mp'), may hold values from -0.09375 to 0.09375
- probe: float32 [8192], P('mp'), as said below
- chosen: int32 [16, 192], replicated, may hold values from 0 to 4095, as said below
- counts: int32 [16], replicated, may hold values from 24 to 192, as said below
- gate_w: bfloat16 [4096, 14336], P('dp', 'mp'), may hold values from -0.09375 to 0.09375
- up_w: bfloat16 [4096, 14336], P('dp', 'mp'), may hold values from -0.09375 to 0.09375
- cotangent: bfloat16 [3072, 14336], P('dp', 'mp'), may hold values from -6 to 6
Outputs:
- grad_gate: bfloat16 [4096, 14336], P('dp', 'mp')
- grad_up: bfloat16 [4096, 14336], P('dp', 'mp')
- hidden: bfloat16 [3072, 14336], P('dp', 'mp')
- cand_weight: float32 [4096], P('dp')
Inputs may be any that keep to these rules, and one draw needn't show every extreme that they name: `chosen`: all entries are distinct candidate indices. `counts`: exactly one training shard uses all 192 slots in every draw. `probe`: magnitudes at most 12 / sqrt(8192).
All inputs are finite; a program needn't handle non-finite values.
Results may differ from a plain program's by a relative error of at most 0.0057.
Values may be sent and summed in bfloat16 or wider, within the bound.
A program may use at most 128 MiB of HBM per device.

v0:
```python
import jax
import jax.numpy as jnp
from jax import lax
from jax.sharding import PartitionSpec as P


def on_device(candidates, hold_gate, hold_up, probe, chosen, counts, gate_w, up_w, cotangent):
    width_mp = candidates.shape[1]
    cand_dev = candidates.shape[0]
    incoming = lax.all_gather(candidates, "mp", axis=1, tiled=True)
    hold_g = jnp.dot(incoming, hold_gate, preferred_element_type=jnp.float32)
    hold_u = jnp.dot(incoming, hold_up, preferred_element_type=jnp.float32)
    partial_score = jnp.sum(jax.nn.silu(hold_g) * hold_u * probe[None, :], axis=1)
    score = lax.psum(partial_score, "mp")
    cand_weight = jax.nn.sigmoid(score)
    shards = chosen.shape[0]
    slots = chosen.shape[1]
    own_index = lax.axis_index("dp")
    source = chosen // cand_dev
    local_row = (chosen % cand_dev).reshape(-1)
    usable = (jnp.arange(slots, dtype=jnp.int32)[None, :] < counts[:, None]) & (source == own_index)
    picked = jnp.take(candidates, local_row, axis=0).reshape(shards, slots, width_mp)
    picked = jnp.where(usable[:, :, None], picked, jnp.zeros_like(picked))
    picked_weight = jnp.where(
        usable, jnp.take(cand_weight, local_row).reshape(shards, slots), 0.0
    ).astype(jnp.bfloat16)
    arrived, arrived_weight = (
        lax.all_to_all(picked, "dp", split_axis=0, concat_axis=0, tiled=True),
        lax.all_to_all(picked_weight, "dp", split_axis=0, concat_axis=0, tiled=True),
    )
    row_slab = jnp.sum(arrived.astype(jnp.float32), axis=0).astype(jnp.bfloat16)
    row_weight = jnp.sum(arrived_weight.astype(jnp.float32), axis=0)
    row_x = lax.all_gather(row_slab, "mp", axis=1, tiled=True)
    row_slices = lax.all_to_all(row_x, "dp", split_axis=1, concat_axis=0, tiled=True)
    incoming = (
        lax.all_gather(gate_w, "dp", axis=0, tiled=True),
        lax.all_gather(up_w, "dp", axis=0, tiled=True),
    )
    gate = jnp.dot(row_x, incoming[0], preferred_element_type=jnp.float32)
    up = jnp.dot(row_x, incoming[1], preferred_element_type=jnp.float32)
    hidden = (jax.nn.silu(gate) * up).astype(jnp.bfloat16)
    back = cotangent.astype(jnp.float32) * row_weight[:, None]
    sig = jax.nn.sigmoid(gate)
    d_up = (back * gate * sig).astype(jnp.bfloat16)
    d_gate = (back * up * sig * (1.0 + gate * (1.0 - sig))).astype(jnp.bfloat16)
    contract_rows = (((0,), (0,)), ((), ()))
    incoming = (
        lax.all_gather(d_gate, "dp", axis=0, tiled=True),
        lax.all_gather(d_up, "dp", axis=0, tiled=True),
    )
    grad_g = lax.dot_general(
        row_slices, incoming[0], contract_rows, preferred_element_type=jnp.float32
    )
    grad_u = lax.dot_general(
        row_slices, incoming[1], contract_rows, preferred_element_type=jnp.float32
    )
    return (grad_g.astype(jnp.bfloat16), grad_u.astype(jnp.bfloat16), hidden, cand_weight)


def solution(mesh):
    placed = (
        P("dp", "mp"),
        P(None, "mp"),
        P(None, "mp"),
        P("mp"),
        P(),
        P(),
        P("dp", "mp"),
        P("dp", "mp"),
        P("dp", "mp"),
    )
    return jax.shard_map(
        on_device,
        mesh=mesh,
        in_specs=placed,
        out_specs=(P("dp", "mp"), P("dp", "mp"), P("dp", "mp"), P("dp")),
        check_vma=False,
    )
```

profile of v0, /device:TPU:1, one launch (start us, length us, event | category | flops | bytes accessed | tf_op | source)
XLA Modules:
  0.0 458.5 jit_solution(4822329651751449593)
XLA Ops:
  7.2 0.7 all-gather.9.cloned.1.call-update
  8.0 0.7 add_select_fusion
  8.7 0.1 reshape.63
  8.8 11.1 %gather_fusion = bf16[3072,256]{1,0:T(8,128)(2,1)S(1)} fusion(bf16[256,256]{1,0:T(8,128)(2,1)S(1)} %copy-done.1, s32[3072]{0:T(1024)S(1)} %broadcast_clamp_fusion), kind=kCustom, calls=%fused_computation | custom fusion | bytes 3158016 | tf_op jit(solution)/shard_map/jit(_take)/gather | solution.py:22
  19.9 44.7 %all-gather.9.cloned.1.call-done = bf16[256,4096]{1,0:T(8,128)(2,1)} async-done(((bf16[256,256]{1,0:T(8,128)(2,1)}), bf16[256,4096]{1,0:T(8,128)(2,1)}) %all-gather.9.cloned.1.call-update) | async-done | bytes 2097168 | tf_op jit(solution)/shard_map/all_gather | solution.py:10
  64.6 4.2 fusion.8
  68.9 0.5 copy-done.6
  69.3 1.4 fusion.1
  70.7 30.9 %psum.7 = f32[256]{0:T(256)S(1)} all-reduce(f32[256]{0:T(256)S(1)} %fusion.1), channel_id=1, replica_groups=mesh['dp'=16,'mp'=16] {'mp'}, use_global_device_ids=true, to_apply=%region_2.3 | all-reduce | flops 256 | bytes 2048 | tf_op jit(solution)/shard_map/psum | solution.py:14
  101.6 19.3 %gather_fusion.1 = bf16[3072]{0:T(1024)(128)(2,1)S(1)} fusion(f32[256]{0:T(256)S(1)} %add_divide_fusion.1, s32[3072]{0:T(1024)S(1)} %broadcast_clamp_fusion), kind=kCustom, calls=%fused_computation.1 | custom fusion | bytes 24576 | tf_op jit(solution)/shard_map/jit(_take)/gather | solution.py:25
  120.9 0.1 gather.15
  121.0 0.1 fusion.6
  121.1 1.2 select_select_fusion
  122.4 56.0 %all_to_all.33 = bf16[16,192,256]{2,1,0:T(8,128)(2,1)S(1)} all-to-all(bf16[16,192,256]{2,1,0:T(8,128)(2,1)S(1)} %select_select_fusion), channel_id=1, replica_groups=mesh['dp'=16,'mp'=16] {'dp'}, dimensions={0} | all-to-all | bytes 3145728 | tf_op jit(solution)/shard_map/all_to_all | solution.py:28
  178.4 0.9 reduce_sum.30
  179.2 0.0 all-gather.13.cloned.1.call-start
  179.3 0.7 all-gather.13.cloned.1.call-update
  180.0 0.5 all-gather.11.cloned.1.call-update
  180.6 10.1 %all_to_all.34 = bf16[16,1,192]{2,1,0:T(2,128)(2,1)S(1)} all-to-all(bf16[16,1,192]{2,1,0:T(2,128)(2,1)S(1)} %copy.16), channel_id=1, replica_groups=mesh['dp'=16,'mp'=16] {'dp'}, dimensions={0} | all-to-all | bytes 12288 | tf_op jit(solution)/shard_map/all_to_all | solution.py:29
  190.8 28.7 %all-gather.7.cloned.1.call-done = bf16[192,4096]{1,0:T(8,128)(2,1)} async-done(((bf16[192,256]{1,0:T(8,128)(2,1)}), bf16[192,4096]{1,0:T(8,128)(2,1)}) %all-gather.7.cloned.1.call-update) | async-done | bytes 1572880 | tf_op jit(solution)/shard_map/all_gather | solution.py:33
  219.5 54.2 %all-gather.13.cloned.1.call-done = bf16[4096,896]{1,0:T(8,128)(2,1)} async-done(((bf16[256,896]{1,0:T(8,128)(2,1)}), bf16[4096,896]{1,0:T(8,128)(2,1)}) %all-gather.13.cloned.1.call-update) | async-done | bytes 7340048 | tf_op jit(solution)/shard_map/all_gather | solution.py:36
  273.7 5.4 %fusion.9 = f32[192,896]{1,0:T(8,128)S(1)} fusion(bf16[192,4096]{1,0:T(8,128)(2,1)} %all-gather.7.cloned.1.call-done, bf16[4096,896]{1,0:T(8,128)(2,1)} %all-gather.13.cloned.1.call-done), kind=kOutput, calls=%fused_computation.34 | convolution fusion | flops 1409286144 | bytes 9601024 | tf_op jit(solution)/shard_map/dot_general | solution.py:39
  279.1 45.8 %all-gather.11.cloned.1.call-done = bf16[4096,896]{1,0:T(8,128)(2,1)} async-done(((bf16[256,896]{1,0:T(8,128)(2,1)}), bf16[4096,896]{1,0:T(8,128)(2,1)}) %all-gather.11.cloned.1.call-update) | async-done | bytes 7340048 | tf_op jit(solution)/shard_map/all_gather | solution.py:37
  324.9 6.0 %multiply_convert_fusion = (bf16[192,896]{1,0:T(8,128)(2,1)}, bf16[192,896]{1,0:T(8,128)(2,1)}, bf16[192,896]{1,0:T(8,128)(2,1)}) fusion(f32[192,896]{1,0:T(8,128)S(1)} %fusion.9, f32[192]{0:T(256)S(1)} %convert_reduce_fusion, bf16[192,896]{1,0:T(8,128)(2,1)S(1)} %copy-done.7, bf16[192,4096]{1,0:T(8,128)(2,1)S(1)} %copy-done.2, ...), kind=kOutput, calls=%fused_computation.9 | convolution fusion | flops 1412382720 | bytes 10978048 | tf_op jit(solution)/shard_map/dot_general | solution.py:40
  330.9 0.0 all-gather.15.cloned.1.call-start
  331.0 0.5 all-gather.15.cloned.1.call-update
  331.5 0.1 copy.19
  331.6 58.1 %all_to_all.35 = bf16[192,16,256]{2,0,1:T(8,128)(2,1)S(1)} all-to-all(bf16[192,16,256]{2,0,1:T(8,128)(2,1)S(1)} %bitcast.24), channel_id=1, replica_groups=mesh['dp'=16,'mp'=16] {'dp'}, dimensions={1} | all-to-all | bytes 3145728 | tf_op jit(solution)/shard_map/all_to_all | solution.py:34
  389.8 12.2 %all-gather.17.cloned.1.call-done = bf16[3072,896]{1,0:T(8,128)(2,1)} async-done(((bf16[192,896]{1,0:T(8,128)(2,1)}), bf16[3072,896]{1,0:T(8,128)(2,1)}) %all-gather.17.cloned.1.call-update) | async-done | bytes 5505040 | tf_op jit(solution)/shard_map/all_gather | solution.py:49
  402.0 5.2 %convolution_convert_fusion = bf16[256,896]{1,0:T(8,128)(2,1)} fusion(bf16[3072,256]{1,0:T(8,128)(2,1)S(1)} %bitcast.26, bf16[3072,896]{1,0:T(8,128)(2,1)} %all-gather.17.cloned.1.call-done), kind=kOutput, calls=%fused_computation.4 | convolution fusion | flops 1409515520 | bytes 7536640 | tf_op jit(solution)/shard_map/dot_general | solution.py:54
  407.1 39.4 %all-gather.15.cloned.1.call-done = bf16[3072,896]{1,0:T(8,128)(2,1)} async-done(((bf16[192,896]{1,0:T(8,128)(2,1)}), bf16[3072,896]{1,0:T(8,128)(2,1)}) %all-gather.15.cloned.1.call-update) | async-done | bytes 5505040 | tf_op jit(solution)/shard_map/all_gather | solution.py:48
  446.5 5.2 %convolution_convert_fusion.1 = bf16[256,896]{1,0:T(8,128)(2,1)} fusion(bf16[3072,256]{1,0:T(8,128)(2,1)S(1)} %bitcast.27, bf16[3072,896]{1,0:T(8,128)(2,1)} %all-gather.15.cloned.1.call-done), kind=kOutput, calls=%fused_computation.5 | convolution fusion | flops 1409515520 | bytes 7536640 | tf_op jit(solution)/shard_map/dot_general | solution.py:51
  (28 shorter events, 0.3 us)
Async XLA Ops:
  7.2 1.6 copy-start.1
  7.2 57.4 %all-gather.9.cloned.1.call-start = ((), (), s32[]{:S(2)}) async-start(), calls=%async_computation.4 | async-start | bytes 2228224 | tf_op jit(solution)/shard_map/all_gather | solution.py:10
  7.9 211.6 %all-gather.7.cloned.1.call-start = ((), (), s32[]{:S(2)}) async-start(), calls=%async_computation.3 | async-start | bytes 1671168 | tf_op jit(solution)/shard_map/all_gather | solution.py:33
  19.9 49.0 %copy-start.8 = (f32[512]{0:T(512)S(1)}, f32[512]{0:T(512)}, u32[]{:S(2)}) copy-start(f32[512]{0:T(512)} %param.12) | copy-start | bytes 6148
  64.6 4.2 copy-start.5
  64.6 4.7 %copy-start.6 = (bf16[256,4096]{1,0:T(8,128)(2,1)S(1)}, bf16[256,4096]{1,0:T(8,128)(2,1)}, u32[]{:S(2)}) copy-start(bf16[256,4096]{1,0:T(8,128)(2,1)} %all-gather.9.cloned.1.call-done) | copy-start | bytes 6291460
  101.6 19.4 %copy-start = (f32[256]{0:T(256)}, f32[256]{0:T(256)S(1)}, u32[]{:S(2)}) copy-start(f32[256]{0:T(256)S(1)} %add_divide_fusion.1) | copy-start | bytes 3076
  101.6 19.4 %copy-start.3 = (s32[16,192]{1,0:T(8,128)S(1)}, s32[16,192]{1,0:T(8,128)}, u32[]{:S(2)}) copy-start(s32[16,192]{1,0:T(8,128)} %param.13) | copy-start | bytes 36868
  101.6 19.4 %copy-start.4 = (s32[16]{0:T(128)S(1)}, s32[16]{0:T(128)}, u32[]{:S(2)}) copy-start(s32[16]{0:T(128)} %param.14) | copy-start | bytes 196
  179.2 94.4 %all-gather.13.cloned.1.call-start = ((), (), s32[]{:S(2)}) async-start(), calls=%async_computation.6 | async-start | bytes 7798784 | tf_op jit(solution)/shard_map/all_gather | solution.py:36
  180.0 144.9 %all-gather.11.cloned.1.call-start = ((), (), s32[]{:S(2)}) async-start(), calls=%async_computation.5 | async-start | bytes 7798784 | tf_op jit(solution)/shard_map/all_gather | solution.py:37
  180.6 221.4 %all-gather.17.cloned.1.call-start = ((), (), s32[]{:S(2)}) async-start(), calls=%async_computation.8 | async-start | bytes 5849088 | tf_op jit(solution)/shard_map/all_gather | solution.py:49
  190.8 134.1 %copy-start.7 = (bf16[192,896]{1,0:T(8,128)(2,1)S(1)}, bf16[192,896]{1,0:T(8,128)(2,1)}, u32[]{:S(2)}) copy-start(bf16[192,896]{1,0:T(8,128)(2,1)} %param.17) | copy-start | bytes 1032196
  219.5 105.4 %copy-start.2 = (bf16[192,4096]{1,0:T(8,128)(2,1)S(1)}, bf16[192,4096]{1,0:T(8,128)(2,1)}, u32[]{:S(2)}) copy-start(bf16[192,4096]{1,0:T(8,128)(2,1)} %all-gather.7.cloned.1.call-done) | copy-start | bytes 4718596
  330.9 115.6 %all-gather.15.cloned.1.call-start = ((), (), s32[]{:S(2)}) async-start(), calls=%async_computation.7 | async-start | bytes 5849088 | tf_op jit(solution)/shard_map/all_gather | solution.py:48
Sparse Core Ops, SparseCore 0:
  10.4 54.1 all-gather.8
  179.4 40.0 all-gather.6
  221.3 52.3 all-gather.12
  275.4 49.4 all-gather.10
  331.0 70.8 all-gather.16
  404.2 42.2 all-gather.14
where the time goes:
time: 459 us; the launch traced here: 458 us
  waiting for transfers between devices  227 us (49%)
  blocking collectives  155 us (34%)
  local copies, waits for them, and re-layouts  31.2 us (7%)
  matrix products  27.3 us (6%)
  between operations  14.3 us (3%)
    all_to_all x1, blocking collectives, on_device(): lax.all_to_all(row_x, 'dp', split_axis=1, concat_axis=0, tiled=True)  58.1 us
    all_to_all x1, blocking collectives, on_device(): lax.all_to_all(picked, 'dp', split_axis=0, concat_axis=0, tiled=True)  56 us
    all_gather x1, waiting for transfers between devices, on_device(): lax.all_gather(gate_w, 'dp', axis=0, tiled=True)  54.2 us
    all_gather x1, waiting for transfers between devices, on_device(): lax.all_gather(up_w, 'dp', axis=0, tiled=True)  45.8 us
    all_gather x1, waiting for transfers between devices, on_device(): incoming = lax.all_gather(candidates, 'mp', axis=1, tiled=True)  44.7 us
    all_gather x1, waiting for transfers between devices, on_device(): lax.all_gather(d_gate, 'dp', axis=0, tiled=True)  39.4 us
    psum x1, blocking collectives, on_device(): score = lax.psum(partial_score, 'mp')  30.9 us
    all_gather x1, waiting for transfers between devices, on_device(): row_x = lax.all_gather(row_slab, 'mp', axis=1, tiled=True)  28.7 us
  transfers between devices with their start and end apart: 6, of which 6 were waited for; matrix products, arithmetic and copies ran while one was open for 5% of the time, Pallas kernels for 0%

commit v1 on v0

v1 whole, which is shorter than its diff:
```python
import jax
import jax.numpy as jnp
from jax import lax
from jax.sharding import PartitionSpec as P


def gather_by_a2a(x, axis_name, axis):
    parts = lax.psum(1, axis_name)
    stacked = lax.all_to_all(
        jnp.broadcast_to(x[None], (parts,) + x.shape), axis_name, split_axis=0, concat_axis=0, tiled=True
    )
    stacked = jnp.moveaxis(stacked, 0, axis)
    shape = list(x.shape)
    shape[axis] *= parts
    return stacked.reshape(shape)


def on_device(candidates, hold_gate, hold_up, probe, chosen, counts, gate_w, up_w, cotangent):
    cand_dev = candidates.shape[0]
    shards = chosen.shape[0]
    slots = chosen.shape[1]
    full_w = (
        lax.all_gather(gate_w, "dp", axis=0, tiled=True),
        lax.all_gather(up_w, "dp", axis=0, tiled=True),
    )
    own_index = lax.axis_index("dp")
    source = chosen // cand_dev
    local_row = (chosen % cand_dev).reshape(-1)
    usable = ((jnp.arange(slots, dtype=jnp.int32)[None, :] < counts[:, None]) & (source == own_index)).reshape(-1)
    onehot = (
        (local_row[:, None] == jnp.arange(cand_dev, dtype=jnp.int32)[None, :]) & usable[:, None]
    ).astype(jnp.bfloat16)
    picked = jnp.dot(onehot, candidates, preferred_element_type=jnp.float32).astype(jnp.bfloat16)
    picked = picked.reshape(shards, slots, candidates.shape[1])
    arrived = lax.all_to_all(picked, "dp", split_axis=0, concat_axis=0, tiled=True)
    row_slab = jnp.sum(arrived.astype(jnp.float32), axis=0).astype(jnp.bfloat16)
    row_x = gather_by_a2a(row_slab, "mp", 1)
    row_slices = lax.all_to_all(row_x, "dp", split_axis=1, concat_axis=0, tiled=True)

    incoming = lax.all_gather(candidates, "mp", axis=1, tiled=True)
    hold_g = jnp.dot(incoming, hold_gate, preferred_element_type=jnp.float32)
    hold_u = jnp.dot(incoming, hold_up, preferred_element_type=jnp.float32)
    partial_score = jnp.sum(jax.nn.silu(hold_g) * hold_u * probe[None, :], axis=1)
    score = lax.psum(partial_score, "mp")
    cand_weight = jax.nn.sigmoid(score)
    picked_weight = jnp.dot(
        onehot, cand_weight.astype(jnp.bfloat16)[:, None], preferred_element_type=jnp.float32
    ).astype(jnp.bfloat16).reshape(shards, slots)
    arrived_weight = lax.all_to_all(picked_weight, "dp", split_axis=0, concat_axis=0, tiled=True)
    row_weight = jnp.sum(arrived_weight.astype(jnp.float32), axis=0)

    gate = jnp.dot(row_x, full_w[0], preferred_element_type=jnp.float32)
    up = jnp.dot(row_x, full_w[1], preferred_element_type=jnp.float32)
    hidden = (jax.nn.silu(gate) * up).astype(jnp.bfloat16)
    back = cotangent.astype(jnp.float32) * row_weight[:, None]
    sig = jax.nn.sigmoid(gate)
    d_up = (back * gate * sig).astype(jnp.bfloat16)
    d_gate = (back * up * sig * (1.0 + gate * (1.0 - sig))).astype(jnp.bfloat16)
    contract_rows = (((0,), (0,)), ((), ()))
    incoming = (
        lax.all_gather(d_gate, "dp", axis=0, tiled=True),
        lax.all_gather(d_up, "dp", axis=0, tiled=True),
    )
    grad_g = lax.dot_general(
        row_slices, incoming[0], contract_rows, preferred_element_type=jnp.float32
    )
    grad_u = lax.dot_general(
        row_slices, incoming[1], contract_rows, preferred_element_type=jnp.float32
    )
    return (grad_g.astype(jnp.bfloat16), grad_u.astype(jnp.bfloat16), hidden, cand_weight)


def solution(mesh):
    placed = (
        P("dp", "mp"),
        P(None, "mp"),
        P(None, "mp"),
        P("mp"),
        P(),
        P(),
        P("dp", "mp"),
        P("dp", "mp"),
        P("dp", "mp"),
    )
    return jax.shard_map(
        on_device,
        mesh=mesh,
        in_specs=placed,
        out_specs=(P("dp", "mp"), P("dp", "mp"), P("dp", "mp"), P("dp")),
        check_vma=False,
    )
```

time: 459 us -> 304 us (0.66)
  waiting for transfers between devices: 227 us -> 130 us
  blocking collectives: 155 us -> 89.7 us
  starting transfers between devices: 0.24 us -> 29.8 us
  local copies, waits for them, and re-layouts: 31.2 us -> 2.84 us
  matrix products: 27.3 us -> 34.8 us
    all_to_all x2 -> x0, blocking collectives: 66.1 us -> none  [the longest x1 56 us: on_device(): lax.all_to_all(picked, 'dp', split_axis=0, concat_axis=0, tiled=True)]
    all_gather x1, waiting for transfers between devices: 54.2 us -> 0.02 us  [on_device(): lax.all_gather(gate_w, 'dp', axis=0, tiled=True)]
    all_gather x1, waiting for transfers between devices: 45.8 us -> 4.96 us  [on_device(): lax.all_gather(up_w, 'dp', axis=0, tiled=True)]
    all_to_all x0 -> x3, waiting for transfers between devices: none -> 32 us  [the longest x1 24.8 us: gather_by_a2a(): lax.all_to_all(jnp.broadcast_to(x[None], (parts,) + x.shape), axis_name,...]
    gather x3 -> x0, local copies, waits for them, and re-layouts: 30.5 us -> none  [the longest x2 19.4 us: on_device(): jnp.take(cand_weight, local_row).reshape(shards, slots)]
    all_to_all x0 -> x3, starting transfers between devices: none -> 29.6 us  [the longest x1 15.9 us: on_device(): lax.all_to_all(picked_weight, 'dp', split_axis=0, concat_axis=0, tiled=True)]
    all_gather x1 -> x0, waiting for transfers between devices: 28.7 us -> none  [on_device(): row_x = lax.all_gather(row_slab, 'mp', axis=1, tiled=True)]
    dot_general x2 -> x4, matrix products: 11.4 us -> 18.9 us  [the longest x1 6.14 us: on_device(): up = jnp.dot(row_x, full_w[1], preferred_element_type=jnp.float32)]
  transfers between devices with their start and end apart: 6 -> 8, of which waited for: 6 -> 6; matrix products, arithmetic and copies ran while one was open for 5% -> 9% of each run, Pallas kernels for 0% -> 0%
where the time goes in v1:
time: 304 us
  waiting for transfers between devices  130 us (43%)
  blocking collectives  89.7 us (30%)
  matrix products  34.8 us (11%)
  starting transfers between devices  29.8 us (10%)
  between operations  13.9 us (5%)
    all_to_all x1, blocking collectives, on_device(): lax.all_to_all(row_x, 'dp', split_axis=1, concat_axis=0, tiled=True)  58.2 us
    all_gather x1, waiting for transfers between devices, on_device(): lax.all_gather(d_gate, 'dp', axis=0, tiled=True)  39.4 us
    all_gather x1, waiting for transfers between devices, on_device(): incoming = lax.all_gather(candidates, 'mp', axis=1, tiled=True)  39.2 us
    psum x1, blocking collectives, on_device(): score = lax.psum(partial_score, 'mp')  31.5 us
    all_to_all x1, waiting for transfers between devices, gather_by_a2a(): lax.all_to_all(jnp.broadcast_to(x[None], (parts,) + x.shape), axis_name,...  24.8 us
    all_to_all x1, starting transfers between devices, on_device(): lax.all_to_all(picked_weight, 'dp', split_axis=0, concat_axis=0, tiled=True)  15.9 us
    all_gather x1, waiting for transfers between devices, on_device(): lax.all_gather(d_up, 'dp', axis=0, tiled=True)  12.1 us
    all_to_all x1, starting transfers between devices, on_device(): lax.all_to_all(picked, 'dp', split_axis=0, concat_axis=0, tiled=True)  9.97 us
  transfers between devices with their start and end apart: 8, of which 6 were waited for; matrix products, arithmetic and copies ran while one was open for 9% of the time, Pallas kernels for 0%

profile of v1, /device:TPU:1, one launch (start us, length us, event | category | flops | bytes accessed | tf_op | source)
XLA Modules:
  0.0 303.6 jit_solution(10809270662762904430)
XLA Ops:
  7.2 0.7 all-gather.6.cloned.1.call-update
  7.9 0.7 all-gather.10.cloned.1.call-update
  8.7 0.7 all-gather.8.cloned.1.call-update
  9.4 0.7 add_select_fusion.1
  10.2 0.8 fusion.11
  11.0 0.1 and.27
  11.1 4.3 %convolution_convert_fusion = bf16[3072,256]{1,0:T(8,128)(2,1)} fusion(bf16[256,256]{1,0:T(8,128)(2,1)} %param.9, s32[3072]{0:T(1024)S(1)} %eq.23, pred[3072]{0:T(1024)(128)(4,1)S(1)} %and.27), kind=kOutput, calls=%fused_computation | convolution fusion | flops 405012480 | bytes 1719296 | tf_op jit(solution)/shard_map/dot_general | solution.py:33
  15.4 10.0 %all-to-all-start = ((bf16[16,192,256]{2,1,0:T(8,128)(2,1)}), bf16[16,192,256]{2,1,0:T(8,128)(2,1)S(1)}, u32[]{:S(2)}, u32[]{:S(2)}) async-start(bf16[16,192,256]{2,1,0:T(8,128)(2,1)} %bitcast), calls=%async_computation | async-start | bytes 3145728 | tf_op jit(solution)/shard_map/all_to_all | solution.py:35
  25.4 39.2 %all-gather.6.cloned.1.call-done = bf16[256,4096]{1,0:T(8,128)(2,1)} async-done(((bf16[256,256]{1,0:T(8,128)(2,1)}), bf16[256,4096]{1,0:T(8,128)(2,1)}) %all-gather.6.cloned.1.call-update) | async-done | bytes 2097168 | tf_op jit(solution)/shard_map/all_gather | solution.py:40
  64.6 4.2 %fusion.15 = f32[256,512]{1,0:T(8,128)S(1)} fusion(bf16[256,4096]{1,0:T(8,128)(2,1)} %all-gather.6.cloned.1.call-done, bf16[4096,512]{1,0:T(8,128)(2,1)} %param.10), kind=kOutput, calls=%fused_computation.32 | convolution fusion | flops 1073741824 | bytes 6815744 | tf_op jit(solution)/shard_map/dot_general | solution.py:41
  68.8 0.5 copy-done.1
  69.3 1.4 fusion.9
  70.7 31.5 %psum.7 = f32[256]{0:T(256)S(1)} all-reduce(f32[256]{0:T(256)S(1)} %fusion.9), channel_id=1, replica_groups=mesh['dp'=16,'mp'=16] {'mp'}, use_global_device_ids=true, to_apply=%region_2.3 | all-reduce | flops 256 | bytes 2048 | tf_op jit(solution)/shard_map/psum | solution.py:44
  102.2 0.6 fusion.14
  102.7 2.5 fusion.1
  105.2 0.7 all_to_all.31
  106.0 15.9 %all-to-all-start.3 = ((bf16[16,1,192]{2,1,0:T(2,128)(2,1)}), bf16[16,1,192]{2,1,0:T(2,128)(2,1)S(1)}, u32[]{:S(2)}, u32[]{:S(2)}) async-start(bf16[16,1,192]{2,1,0:T(2,128)(2,1)} %all_to_all.31), calls=%async_computation.3 | async-start | bytes 32768 | tf_op jit(solution)/shard_map/all_to_all | solution.py:49
  121.9 0.2 reduce_sum.30
  122.1 7.1 %all-to-all-done.3 = bf16[16,1,192]{2,1,0:T(2,128)(2,1)S(1)} async-done(((bf16[16,1,192]{2,1,0:T(2,128)(2,1)}), bf16[16,1,192]{2,1,0:T(2,128)(2,1)S(1)}, u32[]{:S(2)}, u32[]{:S(2)}) %all-to-all-start.3) | async-done | bytes 6176 | tf_op jit(solution)/shard_map/all_to_all | solution.py:49
  129.2 1.3 broadcast_in_dim.2
  130.5 3.7 %all-to-all-start.1 = ((bf16[16,192,256]{2,1,0:T(8,128)(2,1)}), bf16[16,192,256]{2,1,0:T(8,128)(2,1)S(1)}, u32[]{:S(2)}, u32[]{:S(2)}) async-start(bf16[16,192,256]{2,1,0:T(8,128)(2,1)} %broadcast_in_dim.2), calls=%async_computation.1 | async-start | bytes 3145728 | tf_op jit(solution)/shard_map/all_to_all | solution.py:9
  134.3 24.8 %all-to-all-done.1 = bf16[16,192,256]{2,1,0:T(8,128)(2,1)S(1)} async-done(((bf16[16,192,256]{2,1,0:T(8,128)(2,1)}), bf16[16,192,256]{2,1,0:T(8,128)(2,1)S(1)}, u32[]{:S(2)}, u32[]{:S(2)}) %all-to-all-start.1) | async-done | bytes 1572896 | tf_op jit(solution)/shard_map/all_to_all | solution.py:9
  159.2 0.2 copy.16
  159.4 6.0 %fusion.16 = f32[192,896]{1,0:T(8,128)} fusion(bf16[192,4096]{1,0:T(8,128)(2,1)S(1)} %bitcast.24, bf16[4096,896]{1,0:T(8,128)(2,1)} %all-gather.10.cloned.1.call-done), kind=kOutput, calls=%fused_computation.33 | convolution fusion | flops 1409286144 | bytes 9601024 | tf_op jit(solution)/shard_map/dot_general | solution.py:52
  165.4 5.0 %all-gather.8.cloned.1.call-done = bf16[4096,896]{1,0:T(8,128)(2,1)} async-done(((bf16[256,896]{1,0:T(8,128)(2,1)}), bf16[4096,896]{1,0:T(8,128)(2,1)}) %all-gather.8.cloned.1.call-update) | async-done | bytes 7340048 | tf_op jit(solution)/shard_map/all_gather | solution.py:24
  170.3 6.1 %multiply_convert_fusion = (bf16[192,896]{1,0:T(8,128)(2,1)}, bf16[192,896]{1,0:T(8,128)(2,1)}, bf16[192,896]{1,0:T(8,128)(2,1)}) fusion(f32[192,896]{1,0:T(8,128)} %fusion.16, f32[192]{0:T(256)S(1)} %convert_reduce_fusion, bf16[192,896]{1,0:T(8,128)(2,1)S(1)} %copy-done.2, bf16[192,4096]{1,0:T(8,128)(2,1)S(1)} %bitcast.25, ...), kind=kOutput, calls=%fused_computation.13 | convolution fusion | flops 1412382720 | bytes 10978048 | tf_op jit(solution)/shard_map/dot_general | solution.py:53
  176.5 0.5 all-gather.12.cloned.1.call-update
  177.1 58.2 %all_to_all.36 = bf16[192,16,256]{2,0,1:T(8,128)(2,1)S(1)} all-to-all(bf16[192,16,256]{2,0,1:T(8,128)(2,1)S(1)} %bitcast.23), channel_id=1, replica_groups=mesh['dp'=16,'mp'=16] {'dp'}, dimensions={1} | all-to-all | bytes 3145728 | tf_op jit(solution)/shard_map/all_to_all | solution.py:38
  235.3 12.1 %all-gather.14.cloned.1.call-done = bf16[3072,896]{1,0:T(8,128)(2,1)} async-done(((bf16[192,896]{1,0:T(8,128)(2,1)}), bf16[3072,896]{1,0:T(8,128)(2,1)}) %all-gather.14.cloned.1.call-update) | async-done | bytes 5505040 | tf_op jit(solution)/shard_map/all_gather | solution.py:62
  247.4 5.2 %convolution_convert_fusion.1 = bf16[256,896]{1,0:T(8,128)(2,1)} fusion(bf16[3072,256]{1,0:T(8,128)(2,1)S(1)} %bitcast.26, bf16[3072,896]{1,0:T(8,128)(2,1)} %all-gather.14.cloned.1.call-done), kind=kOutput, calls=%fused_computation.8 | convolution fusion | flops 1409515520 | bytes 7536640 | tf_op jit(solution)/shard_map/dot_general | solution.py:67
  252.5 39.4 %all-gather.12.cloned.1.call-done = bf16[3072,896]{1,0:T(8,128)(2,1)} async-done(((bf16[192,896]{1,0:T(8,128)(2,1)}), bf16[3072,896]{1,0:T(8,128)(2,1)}) %all-gather.12.cloned.1.call-update) | async-done | bytes 5505040 | tf_op jit(solution)/shard_map/all_gather | solution.py:61
  291.9 5.2 %convolution_convert_fusion.2 = bf16[256,896]{1,0:T(8,128)(2,1)} fusion(bf16[3072,256]{1,0:T(8,128)(2,1)S(1)} %bitcast.27, bf16[3072,896]{1,0:T(8,128)(2,1)} %all-gather.12.cloned.1.call-done), kind=kOutput, calls=%fused_computation.9 | convolution fusion | flops 1409515520 | bytes 7536640 | tf_op jit(solution)/shard_map/dot_general | solution.py:64
  (19 shorter events, 0.4 us)
Async XLA Ops:
  7.2 57.4 %all-gather.6.cloned.1.call-start = ((), (), s32[]{:S(2)}) async-start(), calls=%async_computation.4 | async-start | bytes 2228224 | tf_op jit(solution)/shard_map/all_gather | solution.py:40
  7.9 151.5 %all-gather.10.cloned.1.call-start = ((), (), s32[]{:S(2)}) async-start(), calls=%async_computation.6 | async-start | bytes 7798784 | tf_op jit(solution)/shard_map/all_gather | solution.py:23
  8.6 161.7 %all-gather.8.cloned.1.call-start = ((), (), s32[]{:S(2)}) async-start(), calls=%async_computation.5 | async-start | bytes 7798784 | tf_op jit(solution)/shard_map/all_gather | solution.py:24
  15.4 90.6 %all-to-all-start = ((bf16[16,192,256]{2,1,0:T(8,128)(2,1)}), bf16[16,192,256]{2,1,0:T(8,128)(2,1)S(1)}, u32[]{:S(2)}, u32[]{:S(2)}) async-start(bf16[16,192,256]{2,1,0:T(8,128)(2,1)} %bitcast), calls=%async_computation | async-start | bytes 3145728 | tf_op jit(solution)/shard_map/all_to_all | solution.py:35
  25.4 43.5 %copy-start.3 = (f32[512]{0:T(512)S(1)}, f32[512]{0:T(512)}, u32[]{:S(2)}) copy-start(f32[512]{0:T(512)} %param.12) | copy-start | bytes 6148
  64.6 4.2 %copy-start = (bf16[4096,512]{1,0:T(8,128)(2,1)S(1)}, bf16[4096,512]{1,0:T(8,128)(2,1)}, u32[]{:S(2)}) copy-start(bf16[4096,512]{1,0:T(8,128)(2,1)} %param.11) | copy-start | bytes 12582916
  64.6 4.7 %copy-start.1 = (bf16[256,4096]{1,0:T(8,128)(2,1)S(1)}, bf16[256,4096]{1,0:T(8,128)(2,1)}, u32[]{:S(2)}) copy-start(bf16[256,4096]{1,0:T(8,128)(2,1)} %all-gather.6.cloned.1.call-done) | copy-start | bytes 6291460
  106.0 23.3 %all-to-all-start.3 = ((bf16[16,1,192]{2,1,0:T(2,128)(2,1)}), bf16[16,1,192]{2,1,0:T(2,128)(2,1)S(1)}, u32[]{:S(2)}, u32[]{:S(2)}) async-start(bf16[16,1,192]{2,1,0:T(2,128)(2,1)} %all_to_all.31), calls=%async_computation.3 | async-start | bytes 32768 | tf_op jit(solution)/shard_map/all_to_all | solution.py:49
  130.5 28.6 %all-to-all-start.1 = ((bf16[16,192,256]{2,1,0:T(8,128)(2,1)}), bf16[16,192,256]{2,1,0:T(8,128)(2,1)S(1)}, u32[]{:S(2)}, u32[]{:S(2)}) async-start(bf16[16,192,256]{2,1,0:T(8,128)(2,1)} %broadcast_in_dim.2), calls=%async_computation.1 | async-start | bytes 3145728 | tf_op jit(solution)/shard_map/all_to_all | solution.py:9
  134.3 113.1 %all-gather.14.cloned.1.call-start = ((), (), s32[]{:S(2)}) async-start(), calls=%async_computation.8 | async-start | bytes 5849088 | tf_op jit(solution)/shard_map/all_gather | solution.py:62
  159.4 10.9 %copy-start.2 = (bf16[192,896]{1,0:T(8,128)(2,1)S(1)}, bf16[192,896]{1,0:T(8,128)(2,1)}, u32[]{:S(2)}) copy-start(bf16[192,896]{1,0:T(8,128)(2,1)} %param.17) | copy-start | bytes 1032196
  176.5 115.4 %all-gather.12.cloned.1.call-start = ((), (), s32[]{:S(2)}) async-start(), calls=%async_computation.7 | async-start | bytes 5849088 | tf_op jit(solution)/shard_map/all_gather | solution.py:61
Sparse Core Ops, SparseCore 0:
  10.4 54.1 all-gather.5
  66.4 52.3 all-gather.9
  120.6 49.6 all-gather.7
  176.6 70.7 all-gather.13
  249.6 42.2 all-gather.11

commit v2 on v1

--- a/solution.py
+++ b/solution.py
@@ -15,15 +15,21 @@
     return stacked.reshape(shape)
 
 
+def gather_rows(x):
+    by_z = lax.all_gather(x, "z", axis=0)
+    both = lax.all_gather(by_z, "core", axis=1)
+    return both.reshape((-1,) + x.shape[1:])
+
+
 def on_device(candidates, hold_gate, hold_up, probe, chosen, counts, gate_w, up_w, cotangent):
     cand_dev = candidates.shape[0]
     shards = chosen.shape[0]
     slots = chosen.shape[1]
     full_w = (
-        lax.all_gather(gate_w, "dp", axis=0, tiled=True),
-        lax.all_gather(up_w, "dp", axis=0, tiled=True),
+        gather_rows(gate_w),
+        gather_rows(up_w),
     )
-    own_index = lax.axis_index("dp")
+    own_index = lax.axis_index("z") * lax.psum(1, "core") + lax.axis_index("core")
     source = chosen // cand_dev
     local_row = (chosen % cand_dev).reshape(-1)
     usable = ((jnp.arange(slots, dtype=jnp.int32)[None, :] < counts[:, None]) & (source == own_index)).reshape(-1)
@@ -32,12 +38,12 @@
     ).astype(jnp.bfloat16)
     picked = jnp.dot(onehot, candidates, preferred_element_type=jnp.float32).astype(jnp.bfloat16)
     picked = picked.reshape(shards, slots, candidates.shape[1])
-    arrived = lax.all_to_all(picked, "dp", split_axis=0, concat_axis=0, tiled=True)
+    arrived = lax.all_to_all(picked, DP, split_axis=0, concat_axis=0, tiled=True)
     row_slab = jnp.sum(arrived.astype(jnp.float32), axis=0).astype(jnp.bfloat16)
     row_x = gather_by_a2a(row_slab, "mp", 1)
-    row_slices = lax.all_to_all(row_x, "dp", split_axis=1, concat_axis=0, tiled=True)
+    row_slices = lax.all_to_all(row_x, DP, split_axis=1, concat_axis=0, tiled=True)
 
-    incoming = lax.all_gather(candidates, "mp", axis=1, tiled=True)
+    incoming = gather_by_a2a(candidates, "mp", 1)
     hold_g = jnp.dot(incoming, hold_gate, preferred_element_type=jnp.float32)
     hold_u = jnp.dot(incoming, hold_up, preferred_element_type=jnp.float32)
     partial_score = jnp.sum(jax.nn.silu(hold_g) * hold_u * probe[None, :], axis=1)
@@ -46,7 +52,7 @@
     picked_weight = jnp.dot(
         onehot, cand_weight.astype(jnp.bfloat16)[:, None], preferred_element_type=jnp.float32
     ).astype(jnp.bfloat16).reshape(shards, slots)
-    arrived_weight = lax.all_to_all(picked_weight, "dp", split_axis=0, concat_axis=0, tiled=True)
+    arrived_weight = lax.all_to_all(picked_weight, DP, split_axis=0, concat_axis=0, tiled=True)
     row_weight = jnp.sum(arrived_weight.astype(jnp.float32), axis=0)
 
     gate = jnp.dot(row_x, full_w[0], preferred_element_type=jnp.float32)
@@ -58,8 +64,8 @@
     d_gate = (back * up * sig * (1.0 + gate * (1.0 - sig))).astype(jnp.bfloat16)
     contract_rows = (((0,), (0,)), ((), ()))
     incoming = (
-        lax.all_gather(d_gate, "dp", axis=0, tiled=True),
-        lax.all_gather(d_up, "dp", axis=0, tiled=True),
+        gather_rows(d_gate),
+        gather_rows(d_up),
     )
     grad_g = lax.dot_general(
         row_slices, incoming[0], contract_rows, preferred_element_type=jnp.float32
@@ -70,22 +76,29 @@
     return (grad_g.astype(jnp.bfloat16), grad_u.astype(jnp.bfloat16), hidden, cand_weight)
 
 
+DP = ("z", "core")
+
+
 def solution(mesh):
+    cores = 2
+    mesh = jax.sharding.Mesh(
+        mesh.devices.reshape(mesh.devices.shape[0] // cores, cores, mesh.devices.shape[1]), ("z", "core", "mp")
+    )
     placed = (
-        P("dp", "mp"),
+        P(DP, "mp"),
         P(None, "mp"),
         P(None, "mp"),
         P("mp"),
         P(),
         P(),
-        P("dp", "mp"),
-        P("dp", "mp"),
-        P("dp", "mp"),
+        P(DP, "mp"),
+        P(DP, "mp"),
+        P(DP, "mp"),
     )
     return jax.shard_map(
         on_device,
         mesh=mesh,
         in_specs=placed,
-        out_specs=(P("dp", "mp"), P("dp", "mp"), P("dp", "mp"), P("dp")),
+        out_specs=(P(DP, "mp"), P(DP, "mp"), P(DP, "mp"), P(DP)),
         check_vma=False,
     )

time: 304 us -> 407 us (1.34)
  waiting for transfers between devices: 130 us -> 241 us
  blocking collectives: 89.7 us -> 79.1 us
    all_gather x5 -> x8, waiting for transfers between devices: 95.7 us -> 181 us  [the longest x4 181 us: gather_rows(): by_z = lax.all_gather(x, 'z', axis=0)]
    all_to_all x1 -> x2, waiting for transfers between devices: 24.8 us -> 51.3 us  [gather_by_a2a(): lax.all_to_all(jnp.broadcast_to(x[None], (parts,) + x.shape), axis_name,...]
    all_to_all x1, blocking collectives: 58.2 us -> 47.2 us  [on_device(): lax.all_to_all(row_x, DP, split_axis=1, concat_axis=0, tiled=True)]
    all_to_all x1 -> x2, starting transfers between devices: 3.71 us -> 10.2 us  [gather_by_a2a(): lax.all_to_all(jnp.broadcast_to(x[None], (parts,) + x.shape), axis_name,...]
    all_to_all x2, starting transfers between devices: 25.9 us -> 20.3 us  [the longest x1 13.7 us: on_device(): lax.all_to_all(picked_weight, DP, split_axis=0, concat_axis=0, tiled=True)]
  transfers between devices with their start and end apart: 8 -> 12, of which waited for: 6 -> 7; matrix products, arithmetic and copies ran while one was open for 9% -> 7% of each run, Pallas kernels for 0% -> 0%
where the time goes in v2:
time: 407 us; the launch traced here: 406 us
  waiting for transfers between devices  241 us (59%)
  blocking collectives  79.1 us (19%)
  matrix products  33.9 us (8%)
  starting transfers between devices  30.9 us (8%)
  between operations  14.3 us (4%)
  local copies, waits for them, and re-layouts  5.83 us (1%)
    all_gather x4, waiting for transfers between devices, gather_rows(): by_z = lax.all_gather(x, 'z', axis=0)  181 us
    all_to_all x2, waiting for transfers between devices, gather_by_a2a(): lax.all_to_all(jnp.broadcast_to(x[None], (parts,) + x.shape), axis_name,...  51.3 us
    all_to_all x1, blocking collectives, on_device(): lax.all_to_all(row_x, DP, split_axis=1, concat_axis=0, tiled=True)  47.2 us
    psum x1, blocking collectives, on_device(): score = lax.psum(partial_score, 'mp')  31.8 us
    all_to_all x1, starting transfers between devices, on_device(): lax.all_to_all(picked_weight, DP, split_axis=0, concat_axis=0, tiled=True)  13.7 us
    all_to_all x2, starting transfers between devices, gather_by_a2a(): lax.all_to_all(jnp.broadcast_to(x[None], (parts,) + x.shape), axis_name,...  10.2 us
  transfers between devices with their start and end apart: 12, of which 7 were waited for; matrix products, arithmetic and copies ran while one was open for 7% of the time, Pallas kernels for 0%

profile of v2, /device:TPU:1, one launch (start us, length us, event | category | flops | bytes accessed | tf_op | source)
XLA Modules:
  0.0 406.3 jit_solution(17809317110289626407)
XLA Ops:
  7.2 0.7 all-gather.21.cloned.1.call-update
  7.9 0.7 all-gather.17.cloned.1.call-update
  8.7 54.6 %all-gather.21.cloned.1.call-done = bf16[2048,896]{1,0:T(8,128)(2,1)} async-done(((bf16[256,896]{1,0:T(8,128)(2,1)}), bf16[2048,896]{1,0:T(8,128)(2,1)}) %all-gather.21.cloned.1.call-update) | async-done | bytes 3670032 | tf_op jit(solution)/shard_map/all_gather | solution.py:19
  63.3 50.2 %all-gather.17.cloned.1.call-done = bf16[2048,896]{1,0:T(8,128)(2,1)} async-done(((bf16[256,896]{1,0:T(8,128)(2,1)}), bf16[2048,896]{1,0:T(8,128)(2,1)}) %all-gather.17.cloned.1.call-update) | async-done | bytes 3670032 | tf_op jit(solution)/shard_map/all_gather | solution.py:19
  113.7 1.5 broadcast_in_dim.5
  115.2 6.5 %all-to-all-start.3 = ((bf16[16,256,256]{1,2,0:T(8,128)(2,1)}), bf16[16,256,256]{1,2,0:T(8,128)(2,1)S(1)}, u32[]{:S(2)}, u32[]{:S(2)}) async-start(bf16[16,256,256]{1,2,0:T(8,128)(2,1)} %broadcast_in_dim.5), calls=%async_computation.3 | async-start | bytes 4194304 | tf_op jit(solution)/shard_map/all_to_all | solution.py:9
  122.0 3.5 convolution_convert_fusion
  125.5 26.5 %all-to-all-done.3 = bf16[16,256,256]{1,2,0:T(8,128)(2,1)S(1)} async-done(((bf16[16,256,256]{1,2,0:T(8,128)(2,1)}), bf16[16,256,256]{1,2,0:T(8,128)(2,1)S(1)}, u32[]{:S(2)}, u32[]{:S(2)}) %all-to-all-start.3) | async-done | bytes 2097184 | tf_op jit(solution)/shard_map/all_to_all | solution.py:9
  152.0 1.3 copy-done
  153.3 6.6 %all-to-all-start = ((bf16[16,192,256]{2,1,0:T(8,128)(2,1)}), bf16[16,192,256]{2,1,0:T(8,128)(2,1)S(1)}, u32[]{:S(2)}, u32[]{:S(2)}) async-start(bf16[16,192,256]{2,1,0:T(8,128)(2,1)} %bitcast.41), calls=%async_computation | async-start | bytes 3145728 | tf_op jit(solution)/shard_map/all_to_all | solution.py:41
  159.9 4.3 %fusion.15 = f32[256,512]{1,0:T(8,128)S(1)} fusion(bf16[256,4096]{0,1:T(8,128)(2,1)} %bitcast.39, bf16[4096,512]{1,0:T(8,128)(2,1)} %param.10), kind=kOutput, calls=%fused_computation.32 | convolution fusion | flops 1073741824 | bytes 6815744 | tf_op jit(solution)/shard_map/dot_general | solution.py:47
  164.2 0.5 copy-done.5
  164.6 1.4 fusion.9
  166.0 31.8 %psum.7 = f32[256]{0:T(256)S(1)} all-reduce(f32[256]{0:T(256)S(1)} %fusion.9), channel_id=1, replica_groups=mesh['z'=8,'core'=2,'mp'=16] {'mp'}, use_global_device_ids=true, to_apply=%region_2.3 | all-reduce | flops 256 | bytes 2048 | tf_op jit(solution)/shard_map/psum | solution.py:50
  197.8 0.6 fusion.14
  198.4 2.5 fusion.1
  200.9 0.7 all_to_all.35
  201.6 13.7 %all-to-all-start.4 = ((bf16[16,1,192]{2,1,0:T(2,128)(2,1)}), bf16[16,1,192]{2,1,0:T(2,128)(2,1)S(1)}, u32[]{:S(2)}, u32[]{:S(2)}) async-start(bf16[16,1,192]{2,1,0:T(2,128)(2,1)} %all_to_all.35), calls=%async_computation.4 | async-start | bytes 32768 | tf_op jit(solution)/shard_map/all_to_all | solution.py:55
  215.4 0.2 reduce_sum.30
  215.6 7.1 %all-to-all-done.4 = bf16[16,1,192]{2,1,0:T(2,128)(2,1)S(1)} async-done(((bf16[16,1,192]{2,1,0:T(2,128)(2,1)}), bf16[16,1,192]{2,1,0:T(2,128)(2,1)S(1)}, u32[]{:S(2)}, u32[]{:S(2)}) %all-to-all-start.4) | async-done | bytes 6176 | tf_op jit(solution)/shard_map/all_to_all | solution.py:55
  222.7 1.3 broadcast_in_dim.4
  224.0 3.7 all-to-all-start.1
  227.8 24.8 %all-to-all-done.1 = bf16[16,192,256]{2,1,0:T(8,128)(2,1)S(1)} async-done(((bf16[16,192,256]{2,1,0:T(8,128)(2,1)}), bf16[16,192,256]{2,1,0:T(8,128)(2,1)S(1)}, u32[]{:S(2)}, u32[]{:S(2)}) %all-to-all-start.1) | async-done | bytes 1572896 | tf_op jit(solution)/shard_map/all_to_all | solution.py:9
  252.7 0.2 copy.19
  252.9 5.8 %fusion.16 = f32[192,896]{1,0:T(8,128)} fusion(bf16[192,4096]{1,0:T(8,128)(2,1)S(1)} %bitcast.42, bf16[4096,896]{1,0:T(8,128)(2,1)} %bitcast.47), kind=kOutput, calls=%fused_computation.33 | convolution fusion | flops 1409286144 | bytes 9601024 | tf_op jit(solution)/shard_map/dot_general | solution.py:58
  258.7 6.1 %multiply_convert_fusion = (bf16[192,896]{1,0:T(8,128)(2,1)}, bf16[192,896]{1,0:T(8,128)(2,1)}, bf16[192,896]{1,0:T(8,128)(2,1)}) fusion(f32[192,896]{1,0:T(8,128)} %fusion.16, f32[192]{0:T(256)S(1)} %convert_reduce_fusion, bf16[192,896]{1,0:T(8,128)(2,1)S(1)} %copy-done.6, bf16[192,4096]{1,0:T(8,128)(2,1)S(1)} %bitcast.43, bf16[4096,896]{1,0:T(8,128)(2,1)} %bitcast.48), kind=kOutput, calls=%fused_computation.13 | convolution fusion | flops 1412382720 | bytes 10978048 | tf_op jit(solution)/shard_map/dot_general | solution.py:59
  264.9 0.5 all-gather.25.cloned.1.call-update
  265.5 32.7 %all-gather.29.cloned.1.call-done = bf16[1536,896]{1,0:T(8,128)(2,1)} async-done(((bf16[192,896]{1,0:T(8,128)(2,1)}), bf16[1536,896]{1,0:T(8,128)(2,1)}) %all-gather.29.cloned.1.call-update) | async-done | bytes 2752528 | tf_op jit(solution)/shard_map/all_gather | solution.py:19
  298.3 43.6 %all-gather.25.cloned.1.call-done = bf16[1536,896]{1,0:T(8,128)(2,1)} async-done(((bf16[192,896]{1,0:T(8,128)(2,1)}), bf16[1536,896]{1,0:T(8,128)(2,1)}) %all-gather.25.cloned.1.call-update) | async-done | bytes 2752528 | tf_op jit(solution)/shard_map/all_gather | solution.py:19
  341.9 47.2 %all_to_all.41 = bf16[192,16,256]{2,0,1:T(8,128)(2,1)S(1)} all-to-all(bf16[192,16,256]{2,0,1:T(8,128)(2,1)S(1)} %bitcast.34), channel_id=1, replica_groups=mesh['z'=8,'core'=2,'mp'=16] {'z','core'}, dimensions={1} | all-to-all | bytes 3145728 | tf_op jit(solution)/shard_map/all_to_all | solution.py:44
  389.1 5.2 %convolution_convert_fusion.1 = bf16[256,896]{1,0:T(8,128)(2,1)} fusion(bf16[3072,256]{1,0:T(8,128)(2,1)S(1)} %bitcast.44, bf16[3072,896]{1,0:T(8,128)(2,1)} %bitcast.49), kind=kOutput, calls=%fused_computation.8 | convolution fusion | flops 1409515520 | bytes 7536640 | tf_op jit(solution)/shard_map/dot_general | solution.py:73
  394.3 5.2 %convolution_convert_fusion.2 = bf16[256,896]{1,0:T(8,128)(2,1)} fusion(bf16[3072,256]{1,0:T(8,128)(2,1)S(1)} %bitcast.45, bf16[3072,896]{1,0:T(8,128)(2,1)} %bitcast.50), kind=kOutput, calls=%fused_computation.9 | convolution fusion | flops 1409515520 | bytes 7536640 | tf_op jit(solution)/shard_map/dot_general | solution.py:70
  (40 shorter events, 0.9 us)
Async XLA Ops:
  7.2 56.1 %all-gather.21.cloned.1.call-start = ((), (), s32[]{:S(2)}) async-start(), calls=%async_computation.7 | async-start | bytes 4128768 | tf_op jit(solution)/shard_map/all_gather | solution.py:19
  7.9 105.6 %all-gather.17.cloned.1.call-start = ((), (), s32[]{:S(2)}) async-start(), calls=%async_computation.5 | async-start | bytes 4128768 | tf_op jit(solution)/shard_map/all_gather | solution.py:19
  8.6 244.2 %all-gather.23.cloned.1.call-start = ((), (), s32[]{:S(2)}) async-start(), calls=%async_computation.8 | async-start | bytes 11010048 | tf_op jit(solution)/shard_map/all_gather | solution.py:20
  63.3 50.3 %copy-start.2 = (bf16[256,256]{1,0:T(8,128)(2,1)S(1)}, bf16[256,256]{1,0:T(8,128)(2,1)}, u32[]{:S(2)}) copy-start(bf16[256,256]{1,0:T(8,128)(2,1)} %param.9) | copy-start | bytes 393220
  63.3 195.5 %all-gather.19.cloned.1.call-start = ((), (), s32[]{:S(2)}) async-start(), calls=%async_computation.6 | async-start | bytes 11010048 | tf_op jit(solution)/shard_map/all_gather | solution.py:20
  113.6 8.1 %copy-start.3 = (s32[16,192]{1,0:T(8,128)S(1)}, s32[16,192]{1,0:T(8,128)}, u32[]{:S(2)}) copy-start(s32[16,192]{1,0:T(8,128)} %param.13) | copy-start | bytes 36868
  113.7 8.1 %copy-start.4 = (s32[16]{0:T(128)S(1)}, s32[16]{0:T(128)}, u32[]{:S(2)}) copy-start(s32[16]{0:T(128)} %param.14) | copy-start | bytes 196
  115.2 36.8 %all-to-all-start.3 = ((bf16[16,256,256]{1,2,0:T(8,128)(2,1)}), bf16[16,256,256]{1,2,0:T(8,128)(2,1)S(1)}, u32[]{:S(2)}, u32[]{:S(2)}) async-start(bf16[16,256,256]{1,2,0:T(8,128)(2,1)} %broadcast_in_dim.5), calls=%async_computation.3 | async-start | bytes 4194304 | tf_op jit(solution)/shard_map/all_to_all | solution.py:9
  152.0 1.3 copy-start
  153.3 48.3 %all-to-all-start = ((bf16[16,192,256]{2,1,0:T(8,128)(2,1)}), bf16[16,192,256]{2,1,0:T(8,128)(2,1)S(1)}, u32[]{:S(2)}, u32[]{:S(2)}) async-start(bf16[16,192,256]{2,1,0:T(8,128)(2,1)} %bitcast.41), calls=%async_computation | async-start | bytes 3145728 | tf_op jit(solution)/shard_map/all_to_all | solution.py:41
  159.9 4.3 %copy-start.1 = (bf16[16,256,256]{1,2,0:T(8,128)(2,1)S(1)}, bf16[16,256,256]{1,2,0:T(8,128)(2,1)}, u32[]{:S(2)}) copy-start(bf16[16,256,256]{1,2,0:T(8,128)(2,1)} %copy-done) | copy-start | bytes 6291460
  159.9 4.8 %copy-start.5 = (bf16[4096,512]{1,0:T(8,128)(2,1)S(1)}, bf16[4096,512]{1,0:T(8,128)(2,1)}, u32[]{:S(2)}) copy-start(bf16[4096,512]{1,0:T(8,128)(2,1)} %param.11) | copy-start | bytes 12582916
  159.9 4.8 %copy-start.7 = (f32[512]{0:T(512)S(1)}, f32[512]{0:T(512)}, u32[]{:S(2)}) copy-start(f32[512]{0:T(512)} %param.12) | copy-start | bytes 6148
  201.6 21.1 %all-to-all-start.4 = ((bf16[16,1,192]{2,1,0:T(2,128)(2,1)}), bf16[16,1,192]{2,1,0:T(2,128)(2,1)S(1)}, u32[]{:S(2)}, u32[]{:S(2)}) async-start(bf16[16,1,192]{2,1,0:T(2,128)(2,1)} %all_to_all.35), calls=%async_computation.4 | async-start | bytes 32768 | tf_op jit(solution)/shard_map/all_to_all | solution.py:55
  224.0 28.6 %all-to-all-start.1 = ((bf16[16,192,256]{2,1,0:T(8,128)(2,1)}), bf16[16,192,256]{2,1,0:T(8,128)(2,1)S(1)}, u32[]{:S(2)}, u32[]{:S(2)}) async-start(bf16[16,192,256]{2,1,0:T(8,128)(2,1)} %broadcast_in_dim.4), calls=%async_computation.1 | async-start | bytes 3145728 | tf_op jit(solution)/shard_map/all_to_all | solution.py:9
  227.8 70.5 %all-gather.29.cloned.1.call-start = ((), (), s32[]{:S(2)}) async-start(), calls=%async_computation.11 | async-start | bytes 3096576 | tf_op jit(solution)/shard_map/all_gather | solution.py:19
  252.9 5.9 %copy-start.6 = (bf16[192,896]{1,0:T(8,128)(2,1)S(1)}, bf16[192,896]{1,0:T(8,128)(2,1)}, u32[]{:S(2)}) copy-start(bf16[192,896]{1,0:T(8,128)(2,1)} %param.17) | copy-start | bytes 1032196
  264.9 77.0 %all-gather.25.cloned.1.call-start = ((), (), s32[]{:S(2)}) async-start(), calls=%async_computation.9 | async-start | bytes 3096576 | tf_op jit(solution)/shard_map/all_gather | solution.py:19
  265.5 123.6 %all-gather.31.cloned.1.call-start = ((), (), s32[]{:S(2)}) async-start(), calls=%async_computation.12 | async-start | bytes 8257536 | tf_op jit(solution)/shard_map/all_gather | solution.py:20
  298.3 96.0 %all-gather.27.cloned.1.call-start = ((), (), s32[]{:S(2)}) async-start(), calls=%async_computation.10 | async-start | bytes 8257536 | tf_op jit(solution)/shard_map/all_gather | solution.py:20
Sparse Core Ops, SparseCore 0:
  9.8 53.4 all-gather.20
  65.0 48.4 all-gather.16
  115.3 23.1 all-gather.22
  140.1 25.0 all-gather.18
  265.0 33.1 all-gather.28
  300.4 41.3 all-gather.24
  343.6 23.0 all-gather.30
  368.5 22.2 all-gather.26

commit v3 on v1

--- a/solution.py
+++ b/solution.py
@@ -37,11 +37,11 @@
     row_x = gather_by_a2a(row_slab, "mp", 1)
     row_slices = lax.all_to_all(row_x, "dp", split_axis=1, concat_axis=0, tiled=True)
 
-    incoming = lax.all_gather(candidates, "mp", axis=1, tiled=True)
+    incoming = gather_by_a2a(candidates, "mp", 1)
     hold_g = jnp.dot(incoming, hold_gate, preferred_element_type=jnp.float32)
     hold_u = jnp.dot(incoming, hold_up, preferred_element_type=jnp.float32)
     partial_score = jnp.sum(jax.nn.silu(hold_g) * hold_u * probe[None, :], axis=1)
-    score = lax.psum(partial_score, "mp")
+    score = jnp.sum(gather_by_a2a(partial_score[None, :], "mp", 0), axis=0)
     cand_weight = jax.nn.sigmoid(score)
     picked_weight = jnp.dot(
         onehot, cand_weight.astype(jnp.bfloat16)[:, None], preferred_element_type=jnp.float32

time: 304 us -> 310 us (1.020)
  waiting for transfers between devices: 130 us -> 163 us
  blocking collectives: 89.7 us -> 60 us
    all_to_all x1, waiting for transfers between devices: 0.01 us -> 50 us  [on_device(): lax.all_to_all(picked, 'dp', split_axis=0, concat_axis=0, tiled=True)]
    all_gather x1 -> x0, waiting for transfers between devices: 39.2 us -> none  [on_device(): incoming = lax.all_gather(candidates, 'mp', axis=1, tiled=True)]
    all_to_all x1 -> x3, waiting for transfers between devices: 24.8 us -> 58.6 us  [gather_by_a2a(): lax.all_to_all(jnp.broadcast_to(x[None], (parts,) + x.shape), axis_name,...]
    psum x1 -> x0, blocking collectives: 31.5 us -> none  [on_device(): score = lax.psum(partial_score, 'mp')]
    all_to_all x1 -> x3, starting transfers between devices: 3.71 us -> 15.2 us  [gather_by_a2a(): lax.all_to_all(jnp.broadcast_to(x[None], (parts,) + x.shape), axis_name,...]
    all_to_all x1, starting transfers between devices: 15.9 us -> 5.92 us  [on_device(): lax.all_to_all(picked_weight, 'dp', split_axis=0, concat_axis=0, tiled=True)]
    all_gather x1, waiting for transfers between devices: 4.96 us -> 0.01 us  [on_device(): lax.all_gather(up_w, 'dp', axis=0, tiled=True)]
    all_gather x1, waiting for transfers between devices: 39.4 us -> 35.3 us  [on_device(): lax.all_gather(d_gate, 'dp', axis=0, tiled=True)]
  transfers between devices with their start and end apart: 8 -> 9, of which waited for: 6 -> 7; matrix products, arithmetic and copies ran while one was open for 9% -> 9% of each run, Pallas kernels for 0% -> 0%
where the time goes in v3:
time: 310 us; the launch traced here: 309 us
  waiting for transfers between devices  163 us (53%)
  blocking collectives  60 us (19%)
  matrix products  33.3 us (11%)
  starting transfers between devices  32.2 us (10%)
  between operations  13.9 us (4%)
  local copies, waits for them, and re-layouts  5.52 us (2%)
    all_to_all x1, blocking collectives, on_device(): lax.all_to_all(row_x, 'dp', split_axis=1, concat_axis=0, tiled=True)  60 us
    all_to_all x3, waiting for transfers between devices, gather_by_a2a(): lax.all_to_all(jnp.broadcast_to(x[None], (parts,) + x.shape), axis_name,...  58.6 us
    all_to_all x1, waiting for transfers between devices, on_device(): lax.all_to_all(picked, 'dp', split_axis=0, concat_axis=0, tiled=True)  50 us
    all_gather x1, waiting for transfers between devices, on_device(): lax.all_gather(d_gate, 'dp', axis=0, tiled=True)  35.3 us
    all_to_all x3, starting transfers between devices, gather_by_a2a(): lax.all_to_all(jnp.broadcast_to(x[None], (parts,) + x.shape), axis_name,...  15.2 us
    all_to_all x1, starting transfers between devices, on_device(): lax.all_to_all(picked, 'dp', split_axis=0, concat_axis=0, tiled=True)  10.9 us
    all_gather x1, waiting for transfers between devices, on_device(): lax.all_gather(d_up, 'dp', axis=0, tiled=True)  10.1 us
    all_to_all x1, waiting for transfers between devices, on_device(): lax.all_to_all(picked_weight, 'dp', split_axis=0, concat_axis=0, tiled=True)  7.33 us
  transfers between devices with their start and end apart: 9, of which 7 were waited for; matrix products, arithmetic and copies ran while one was open for 9% of the time, Pallas kernels for 0%

profile of v3, /device:TPU:1, one launch (start us, length us, event | category | flops | bytes accessed | tf_op | source)
XLA Modules:
  0.0 309.1 jit_solution(15480405777864478074)
XLA Ops:
  7.2 0.7 all-gather.7.cloned.1.call-update
  7.9 0.7 all-gather.5.cloned.1.call-update
  8.6 1.0 copy.22
  9.7 1.5 broadcast_in_dim.7
  11.2 7.6 %all-to-all-start.3 = ((bf16[16,256,256]{1,2,0:T(8,128)(2,1)}), bf16[16,256,256]{1,2,0:T(8,128)(2,1)S(1)}, u32[]{:S(2)}, u32[]{:S(2)}) async-start(bf16[16,256,256]{1,2,0:T(8,128)(2,1)} %broadcast_in_dim.7), calls=%async_computation.3 | async-start | bytes 4194304 | tf_op jit(solution)/shard_map/all_to_all | solution.py:9
  19.0 30.7 %all-to-all-done.3 = bf16[16,256,256]{1,2,0:T(8,128)(2,1)S(1)} async-done(((bf16[16,256,256]{1,2,0:T(8,128)(2,1)}), bf16[16,256,256]{1,2,0:T(8,128)(2,1)S(1)}, u32[]{:S(2)}, u32[]{:S(2)}) %all-to-all-start.3) | async-done | bytes 2097184 | tf_op jit(solution)/shard_map/all_to_all | solution.py:9
  49.7 3.7 %fusion.15 = f32[256,512]{1,0:T(8,128)S(1)} fusion(bf16[256,4096]{0,1:T(8,128)(2,1)S(1)} %bitcast.27, bf16[4096,512]{1,0:T(8,128)(2,1)} %param.10), kind=kOutput, calls=%fused_computation.32 | convolution fusion | flops 1073741824 | bytes 6815744 | tf_op jit(solution)/shard_map/dot_general | solution.py:41
  53.4 1.4 fusion.9
  54.8 0.6 broadcast_in_dim.8
  55.5 3.9 %all-to-all-start.4 = ((f32[16,1,256]{2,1,0:T(1,128)}), f32[16,1,256]{2,1,0:T(1,128)S(1)}, u32[]{:S(2)}, u32[]{:S(2)}) async-start(f32[16,1,256]{2,1,0:T(1,128)} %broadcast_in_dim.8), calls=%async_computation.4 | async-start | bytes 32768 | tf_op jit(solution)/shard_map/all_to_all | solution.py:9
  59.4 3.4 %convolution_convert_fusion = bf16[3072,256]{1,0:T(8,128)(2,1)} fusion(bf16[256,256]{1,0:T(8,128)(2,1)S(1)} %copy-done, s32[3072]{0:T(1024)S(1)} %eq.23, pred[3072]{0:T(1024)(128)(4,1)S(1)} %and.27), kind=kOutput, calls=%fused_computation | convolution fusion | flops 405012480 | bytes 1719296 | tf_op jit(solution)/shard_map/dot_general | solution.py:33
  62.8 3.0 all-to-all-done.4
  65.8 10.9 %all-to-all-start = ((bf16[16,192,256]{2,1,0:T(8,128)(2,1)}), bf16[16,192,256]{2,1,0:T(8,128)(2,1)S(1)}, u32[]{:S(2)}, u32[]{:S(2)}) async-start(bf16[16,192,256]{2,1,0:T(8,128)(2,1)} %bitcast), calls=%async_computation | async-start | bytes 3145728 | tf_op jit(solution)/shard_map/all_to_all | solution.py:35
  76.8 0.6 fusion.14
  77.4 2.5 fusion.1
  79.9 0.7 all_to_all.39
  80.6 50.0 %all-to-all-done = bf16[16,192,256]{2,1,0:T(8,128)(2,1)S(1)} async-done(((bf16[16,192,256]{2,1,0:T(8,128)(2,1)}), bf16[16,192,256]{2,1,0:T(8,128)(2,1)S(1)}, u32[]{:S(2)}, u32[]{:S(2)}) %all-to-all-start) | async-done | bytes 1572896 | tf_op jit(solution)/shard_map/all_to_all | solution.py:35
  130.6 5.9 %all-to-all-start.5 = ((bf16[16,1,192]{2,1,0:T(2,128)(2,1)}), bf16[16,1,192]{2,1,0:T(2,128)(2,1)S(1)}, u32[]{:S(2)}, u32[]{:S(2)}) async-start(bf16[16,1,192]{2,1,0:T(2,128)(2,1)} %all_to_all.39), calls=%async_computation.5 | async-start | bytes 32768 | tf_op jit(solution)/shard_map/all_to_all | solution.py:49
  136.5 0.2 reduce_sum.39
  136.7 7.3 %all-to-all-done.5 = bf16[16,1,192]{2,1,0:T(2,128)(2,1)S(1)} async-done(((bf16[16,1,192]{2,1,0:T(2,128)(2,1)}), bf16[16,1,192]{2,1,0:T(2,128)(2,1)S(1)}, u32[]{:S(2)}, u32[]{:S(2)}) %all-to-all-start.5) | async-done | bytes 6176 | tf_op jit(solution)/shard_map/all_to_all | solution.py:49
  144.1 1.3 broadcast_in_dim.6
  145.4 3.7 %all-to-all-start.1 = ((bf16[16,192,256]{2,1,0:T(8,128)(2,1)}), bf16[16,192,256]{2,1,0:T(8,128)(2,1)S(1)}, u32[]{:S(2)}, u32[]{:S(2)}) async-start(bf16[16,192,256]{2,1,0:T(8,128)(2,1)} %broadcast_in_dim.6), calls=%async_computation.1 | async-start | bytes 3145728 | tf_op jit(solution)/shard_map/all_to_all | solution.py:9
  149.2 24.9 %all-to-all-done.1 = bf16[16,192,256]{2,1,0:T(8,128)(2,1)S(1)} async-done(((bf16[16,192,256]{2,1,0:T(8,128)(2,1)}), bf16[16,192,256]{2,1,0:T(8,128)(2,1)S(1)}, u32[]{:S(2)}, u32[]{:S(2)}) %all-to-all-start.1) | async-done | bytes 1572896 | tf_op jit(solution)/shard_map/all_to_all | solution.py:9
  174.1 0.2 copy.27
  174.3 5.8 %fusion.16 = f32[192,896]{1,0:T(8,128)} fusion(bf16[192,4096]{1,0:T(8,128)(2,1)S(1)} %bitcast.29, bf16[4096,896]{1,0:T(8,128)(2,1)} %all-gather.7.cloned.1.call-done), kind=kOutput, calls=%fused_computation.33 | convolution fusion | flops 1409286144 | bytes 9601024 | tf_op jit(solution)/shard_map/dot_general | solution.py:52
  180.1 6.1 %multiply_convert_fusion = (bf16[192,896]{1,0:T(8,128)(2,1)}, bf16[192,896]{1,0:T(8,128)(2,1)}, bf16[192,896]{1,0:T(8,128)(2,1)}) fusion(f32[192,896]{1,0:T(8,128)} %fusion.16, f32[192]{0:T(256)S(1)} %convert_reduce_fusion, bf16[192,896]{1,0:T(8,128)(2,1)S(1)} %copy-done.4, bf16[192,4096]{1,0:T(8,128)(2,1)S(1)} %bitcast.30, ...), kind=kOutput, calls=%fused_computation.13 | convolution fusion | flops 1412382720 | bytes 10978048 | tf_op jit(solution)/shard_map/dot_general | solution.py:53
  186.3 0.5 all-gather.9.cloned.1.call-update
  186.9 60.0 %all_to_all.46 = bf16[192,16,256]{2,0,1:T(8,128)(2,1)S(1)} all-to-all(bf16[192,16,256]{2,0,1:T(8,128)(2,1)S(1)} %bitcast.26), channel_id=1, replica_groups=mesh['dp'=16,'mp'=16] {'dp'}, dimensions={1} | all-to-all | bytes 3145728 | tf_op jit(solution)/shard_map/all_to_all | solution.py:38
  246.9 10.1 %all-gather.11.cloned.1.call-done = bf16[3072,896]{1,0:T(8,128)(2,1)} async-done(((bf16[192,896]{1,0:T(8,128)(2,1)}), bf16[3072,896]{1,0:T(8,128)(2,1)}) %all-gather.11.cloned.1.call-update) | async-done | bytes 5505040 | tf_op jit(solution)/shard_map/all_gather | solution.py:62
  257.0 5.2 %convolution_convert_fusion.1 = bf16[256,896]{1,0:T(8,128)(2,1)} fusion(bf16[3072,256]{1,0:T(8,128)(2,1)S(1)} %bitcast.31, bf16[3072,896]{1,0:T(8,128)(2,1)} %all-gather.11.cloned.1.call-done), kind=kOutput, calls=%fused_computation.8 | convolution fusion | flops 1409515520 | bytes 7536640 | tf_op jit(solution)/shard_map/dot_general | solution.py:67
  262.1 35.3 %all-gather.9.cloned.1.call-done = bf16[3072,896]{1,0:T(8,128)(2,1)} async-done(((bf16[192,896]{1,0:T(8,128)(2,1)}), bf16[3072,896]{1,0:T(8,128)(2,1)}) %all-gather.9.cloned.1.call-update) | async-done | bytes 5505040 | tf_op jit(solution)/shard_map/all_gather | solution.py:61
  297.5 5.2 %convolution_convert_fusion.2 = bf16[256,896]{1,0:T(8,128)(2,1)} fusion(bf16[3072,256]{1,0:T(8,128)(2,1)S(1)} %bitcast.32, bf16[3072,896]{1,0:T(8,128)(2,1)} %all-gather.9.cloned.1.call-done), kind=kOutput, calls=%fused_computation.9 | convolution fusion | flops 1409515520 | bytes 7536640 | tf_op jit(solution)/shard_map/dot_general | solution.py:64
  (27 shorter events, 0.6 us)
Async XLA Ops:
  7.2 167.1 %all-gather.7.cloned.1.call-start = ((), (), s32[]{:S(2)}) async-start(), calls=%async_computation.7 | async-start | bytes 7798784 | tf_op jit(solution)/shard_map/all_gather | solution.py:23
  7.9 172.2 %all-gather.5.cloned.1.call-start = ((), (), s32[]{:S(2)}) async-start(), calls=%async_computation.6 | async-start | bytes 7798784 | tf_op jit(solution)/shard_map/all_gather | solution.py:24
  9.7 9.1 %copy-start.1 = (s32[16,192]{1,0:T(8,128)S(1)}, s32[16,192]{1,0:T(8,128)}, u32[]{:S(2)}) copy-start(s32[16,192]{1,0:T(8,128)} %param.13) | copy-start | bytes 36868
  9.7 9.2 %copy-start.2 = (s32[16]{0:T(128)S(1)}, s32[16]{0:T(128)}, u32[]{:S(2)}) copy-start(s32[16]{0:T(128)} %param.14) | copy-start | bytes 196
  11.2 38.5 %all-to-all-start.3 = ((bf16[16,256,256]{1,2,0:T(8,128)(2,1)}), bf16[16,256,256]{1,2,0:T(8,128)(2,1)S(1)}, u32[]{:S(2)}, u32[]{:S(2)}) async-start(bf16[16,256,256]{1,2,0:T(8,128)(2,1)} %broadcast_in_dim.7), calls=%async_computation.3 | async-start | bytes 4194304 | tf_op jit(solution)/shard_map/all_to_all | solution.py:9
  49.7 3.7 %copy-start.3 = (bf16[4096,512]{1,0:T(8,128)(2,1)S(1)}, bf16[4096,512]{1,0:T(8,128)(2,1)}, u32[]{:S(2)}) copy-start(bf16[4096,512]{1,0:T(8,128)(2,1)} %param.11) | copy-start | bytes 12582916
  49.7 3.7 %copy-start.5 = (f32[512]{0:T(512)S(1)}, f32[512]{0:T(512)}, u32[]{:S(2)}) copy-start(f32[512]{0:T(512)} %param.12) | copy-start | bytes 6148
  53.4 5.9 %copy-start = (bf16[256,256]{1,0:T(8,128)(2,1)S(1)}, bf16[256,256]{1,0:T(8,128)(2,1)}, u32[]{:S(2)}) copy-start(bf16[256,256]{1,0:T(8,128)(2,1)} %param.9) | copy-start | bytes 393220
  55.5 10.4 %all-to-all-start.4 = ((f32[16,1,256]{2,1,0:T(1,128)}), f32[16,1,256]{2,1,0:T(1,128)S(1)}, u32[]{:S(2)}, u32[]{:S(2)}) async-start(f32[16,1,256]{2,1,0:T(1,128)} %broadcast_in_dim.8), calls=%async_computation.4 | async-start | bytes 32768 | tf_op jit(solution)/shard_map/all_to_all | solution.py:9
  65.8 64.8 %all-to-all-start = ((bf16[16,192,256]{2,1,0:T(8,128)(2,1)}), bf16[16,192,256]{2,1,0:T(8,128)(2,1)S(1)}, u32[]{:S(2)}, u32[]{:S(2)}) async-start(bf16[16,192,256]{2,1,0:T(8,128)(2,1)} %bitcast), calls=%async_computation | async-start | bytes 3145728 | tf_op jit(solution)/shard_map/all_to_all | solution.py:35
  130.6 13.5 %all-to-all-start.5 = ((bf16[16,1,192]{2,1,0:T(2,128)(2,1)}), bf16[16,1,192]{2,1,0:T(2,128)(2,1)S(1)}, u32[]{:S(2)}, u32[]{:S(2)}) async-start(bf16[16,1,192]{2,1,0:T(2,128)(2,1)} %all_to_all.39), calls=%async_computation.5 | async-start | bytes 32768 | tf_op jit(solution)/shard_map/all_to_all | solution.py:49
  145.4 28.7 %all-to-all-start.1 = ((bf16[16,192,256]{2,1,0:T(8,128)(2,1)}), bf16[16,192,256]{2,1,0:T(8,128)(2,1)S(1)}, u32[]{:S(2)}, u32[]{:S(2)}) async-start(bf16[16,192,256]{2,1,0:T(8,128)(2,1)} %broadcast_in_dim.6), calls=%async_computation.1 | async-start | bytes 3145728 | tf_op jit(solution)/shard_map/all_to_all | solution.py:9
  149.1 107.9 %all-gather.11.cloned.1.call-start = ((), (), s32[]{:S(2)}) async-start(), calls=%async_computation.9 | async-start | bytes 5849088 | tf_op jit(solution)/shard_map/all_gather | solution.py:62
  174.3 5.9 %copy-start.4 = (bf16[192,896]{1,0:T(8,128)(2,1)S(1)}, bf16[192,896]{1,0:T(8,128)(2,1)}, u32[]{:S(2)}) copy-start(bf16[192,896]{1,0:T(8,128)(2,1)} %param.17) | copy-start | bytes 1032196
  186.3 111.2 %all-gather.9.cloned.1.call-start = ((), (), s32[]{:S(2)}) async-start(), calls=%async_computation.8 | async-start | bytes 5849088 | tf_op jit(solution)/shard_map/all_gather | solution.py:61
Sparse Core Ops, SparseCore 0:
  9.8 55.0 all-gather.6
  66.8 83.5 all-gather.4
  186.4 70.5 all-gather.10
  259.2 38.1 all-gather.8

commit v4 on v3

--- a/solution.py
+++ b/solution.py
@@ -23,17 +23,21 @@
         lax.all_gather(gate_w, "dp", axis=0, tiled=True),
         lax.all_gather(up_w, "dp", axis=0, tiled=True),
     )
+    all_cands = lax.all_gather(candidates, "dp", axis=0, tiled=True)
     own_index = lax.axis_index("dp")
     source = chosen // cand_dev
     local_row = (chosen % cand_dev).reshape(-1)
-    usable = ((jnp.arange(slots, dtype=jnp.int32)[None, :] < counts[:, None]) & (source == own_index)).reshape(-1)
+    valid = jnp.arange(slots, dtype=jnp.int32)[None, :] < counts[:, None]
+    usable = (valid & (source == own_index)).reshape(-1)
     onehot = (
         (local_row[:, None] == jnp.arange(cand_dev, dtype=jnp.int32)[None, :]) & usable[:, None]
     ).astype(jnp.bfloat16)
-    picked = jnp.dot(onehot, candidates, preferred_element_type=jnp.float32).astype(jnp.bfloat16)
-    picked = picked.reshape(shards, slots, candidates.shape[1])
-    arrived = lax.all_to_all(picked, "dp", split_axis=0, concat_axis=0, tiled=True)
-    row_slab = jnp.sum(arrived.astype(jnp.float32), axis=0).astype(jnp.bfloat16)
+    own_chosen = lax.dynamic_index_in_dim(chosen, own_index, 0, keepdims=False)
+    own_valid = lax.dynamic_index_in_dim(valid, own_index, 0, keepdims=False)
+    own_onehot = (
+        (own_chosen[:, None] == jnp.arange(all_cands.shape[0], dtype=jnp.int32)[None, :]) & own_valid[:, None]
+    ).astype(jnp.bfloat16)
+    row_slab = jnp.dot(own_onehot, all_cands, preferred_element_type=jnp.float32).astype(jnp.bfloat16)
     row_x = gather_by_a2a(row_slab, "mp", 1)
     row_slices = lax.all_to_all(row_x, "dp", split_axis=1, concat_axis=0, tiled=True)
 

time: 310 us -> 290 us (0.935)
  waiting for transfers between devices: 163 us -> 153 us
  starting transfers between devices: 32.2 us -> 26.3 us
    all_to_all x1 -> x0, waiting for transfers between devices: 50 us -> none  [on_device(): lax.all_to_all(picked, 'dp', split_axis=0, concat_axis=0, tiled=True)]
    all_gather x1, waiting for transfers between devices: 0.01 us -> 31.6 us  [on_device(): lax.all_gather(up_w, 'dp', axis=0, tiled=True)]
    all_to_all x1 -> x0, starting transfers between devices: 10.9 us -> none  [on_device(): lax.all_to_all(picked, 'dp', split_axis=0, concat_axis=0, tiled=True)]
    all_to_all x1, starting transfers between devices: 5.92 us -> 11 us  [on_device(): lax.all_to_all(picked_weight, 'dp', split_axis=0, concat_axis=0, tiled=True)]
    all_gather x1, waiting for transfers between devices: 35.3 us -> 39.4 us  [on_device(): lax.all_gather(d_gate, 'dp', axis=0, tiled=True)]
    all_to_all x3, waiting for transfers between devices: 58.6 us -> 61.8 us  [gather_by_a2a(): lax.all_to_all(jnp.broadcast_to(x[None], (parts,) + x.shape), axis_name,...]
where the time goes in v4:
time: 290 us
  waiting for transfers between devices  153 us (53%)
  blocking collectives  58.2 us (20%)
  matrix products  32.1 us (11%)
  starting transfers between devices  26.3 us (9%)
  between operations  13.9 us (5%)
  local copies, waits for them, and re-layouts  5.59 us (2%)
    all_to_all x3, waiting for transfers between devices, gather_by_a2a(): lax.all_to_all(jnp.broadcast_to(x[None], (parts,) + x.shape), axis_name,...  61.8 us
    all_to_all x1, blocking collectives, on_device(): lax.all_to_all(row_x, 'dp', split_axis=1, concat_axis=0, tiled=True)  58.2 us
    all_gather x1, waiting for transfers between devices, on_device(): lax.all_gather(d_gate, 'dp', axis=0, tiled=True)  39.4 us
    all_gather x1, waiting for transfers between devices, on_device(): lax.all_gather(up_w, 'dp', axis=0, tiled=True)  31.6 us
    all_to_all x3, starting transfers between devices, gather_by_a2a(): lax.all_to_all(jnp.broadcast_to(x[None], (parts,) + x.shape), axis_name,...  15.1 us
    all_gather x1, waiting for transfers between devices, on_device(): lax.all_gather(d_up, 'dp', axis=0, tiled=True)  12.1 us
    all_to_all x1, starting transfers between devices, on_device(): lax.all_to_all(picked_weight, 'dp', split_axis=0, concat_axis=0, tiled=True)  11 us
    dot_general x1, matrix products, on_device(): up = jnp.dot(row_x, full_w[1], preferred_element_type=jnp.float32)  6.14 us
  transfers between devices with their start and end apart: 9, of which 7 were waited for; matrix products, arithmetic and copies ran while one was open for 9% of the time, Pallas kernels for 0%

profile of v4, /device:TPU:1, one launch (start us, length us, event | category | flops | bytes accessed | tf_op | source)
XLA Modules:
  0.0 289.6 jit_solution(11017177416749902291)
XLA Ops:
  7.2 0.7 all-gather.6.cloned.1.call-update
  7.9 0.7 all-gather.10.cloned.1.call-update
  8.7 0.7 all-gather.8.cloned.1.call-update
  9.4 1.0 copy.22
  10.4 1.5 broadcast_in_dim.7
  12.0 7.6 %all-to-all-start.2 = ((bf16[16,256,256]{1,2,0:T(8,128)(2,1)}), bf16[16,256,256]{1,2,0:T(8,128)(2,1)S(1)}, u32[]{:S(2)}, u32[]{:S(2)}) async-start(bf16[16,256,256]{1,2,0:T(8,128)(2,1)} %broadcast_in_dim.7), calls=%async_computation.2 | async-start | bytes 4194304 | tf_op jit(solution)/shard_map/all_to_all | solution.py:9
  19.7 30.8 %all-to-all-done.2 = bf16[16,256,256]{1,2,0:T(8,128)(2,1)S(1)} async-done(((bf16[16,256,256]{1,2,0:T(8,128)(2,1)}), bf16[16,256,256]{1,2,0:T(8,128)(2,1)S(1)}, u32[]{:S(2)}, u32[]{:S(2)}) %all-to-all-start.2) | async-done | bytes 2097184 | tf_op jit(solution)/shard_map/all_to_all | solution.py:9
  50.5 3.6 %fusion.20 = f32[256,512]{1,0:T(8,128)S(1)} fusion(bf16[256,4096]{0,1:T(8,128)(2,1)S(1)} %bitcast.27, bf16[4096,512]{1,0:T(8,128)(2,1)} %param.10), kind=kOutput, calls=%fused_computation.37 | convolution fusion | flops 1073741824 | bytes 6815744 | tf_op jit(solution)/shard_map/dot_general | solution.py:45
  54.1 1.4 fusion.11
  55.5 0.6 broadcast_in_dim.8
  56.1 3.8 %all-to-all-start.3 = ((f32[16,1,256]{2,1,0:T(1,128)}), f32[16,1,256]{2,1,0:T(1,128)S(1)}, u32[]{:S(2)}, u32[]{:S(2)}) async-start(f32[16,1,256]{2,1,0:T(1,128)} %broadcast_in_dim.8), calls=%async_computation.3 | async-start | bytes 32768 | tf_op jit(solution)/shard_map/all_to_all | solution.py:9
  60.0 0.1 and.40
  60.2 6.2 %all-to-all-done.3 = f32[16,1,256]{2,1,0:T(1,128)S(1)} async-done(((f32[16,1,256]{2,1,0:T(1,128)}), f32[16,1,256]{2,1,0:T(1,128)S(1)}, u32[]{:S(2)}, u32[]{:S(2)}) %all-to-all-start.3) | async-done | bytes 16416 | tf_op jit(solution)/shard_map/all_to_all | solution.py:9
  66.4 0.6 fusion.19
  67.0 2.5 fusion.4
  69.5 0.7 all_to_all.35
  70.2 11.0 %all-to-all-start.4 = ((bf16[16,1,192]{2,1,0:T(2,128)(2,1)}), bf16[16,1,192]{2,1,0:T(2,128)(2,1)S(1)}, u32[]{:S(2)}, u32[]{:S(2)}) async-start(bf16[16,1,192]{2,1,0:T(2,128)(2,1)} %all_to_all.35), calls=%async_computation.4 | async-start | bytes 32768 | tf_op jit(solution)/shard_map/all_to_all | solution.py:53
  81.3 2.4 fusion.12
  83.7 5.1 %all-to-all-done.4 = bf16[16,1,192]{2,1,0:T(2,128)(2,1)S(1)} async-done(((bf16[16,1,192]{2,1,0:T(2,128)(2,1)}), bf16[16,1,192]{2,1,0:T(2,128)(2,1)S(1)}, u32[]{:S(2)}, u32[]{:S(2)}) %all-to-all-start.4) | async-done | bytes 6176 | tf_op jit(solution)/shard_map/all_to_all | solution.py:53
  88.8 1.3 broadcast_in_dim.6
  90.1 3.7 %all-to-all-start = ((bf16[16,192,256]{2,1,0:T(8,128)(2,1)}), bf16[16,192,256]{2,1,0:T(8,128)(2,1)S(1)}, u32[]{:S(2)}, u32[]{:S(2)}) async-start(bf16[16,192,256]{2,1,0:T(8,128)(2,1)} %broadcast_in_dim.6), calls=%async_computation | async-start | bytes 3145728 | tf_op jit(solution)/shard_map/all_to_all | solution.py:9
  93.9 24.8 %all-to-all-done = bf16[16,192,256]{2,1,0:T(8,128)(2,1)S(1)} async-done(((bf16[16,192,256]{2,1,0:T(8,128)(2,1)}), bf16[16,192,256]{2,1,0:T(8,128)(2,1)S(1)}, u32[]{:S(2)}, u32[]{:S(2)}) %all-to-all-start) | async-done | bytes 1572896 | tf_op jit(solution)/shard_map/all_to_all | solution.py:9
  118.7 0.2 copy.27
  118.9 5.8 %fusion.21 = f32[192,896]{1,0:T(8,128)} fusion(bf16[192,4096]{1,0:T(8,128)(2,1)S(1)} %bitcast.29, bf16[4096,896]{1,0:T(8,128)(2,1)} %all-gather.10.cloned.1.call-done), kind=kOutput, calls=%fused_computation.38 | convolution fusion | flops 1409286144 | bytes 9601024 | tf_op jit(solution)/shard_map/dot_general | solution.py:56
  124.8 31.6 %all-gather.8.cloned.1.call-done = bf16[4096,896]{1,0:T(8,128)(2,1)} async-done(((bf16[256,896]{1,0:T(8,128)(2,1)}), bf16[4096,896]{1,0:T(8,128)(2,1)}) %all-gather.8.cloned.1.call-update) | async-done | bytes 7340048 | tf_op jit(solution)/shard_map/all_gather | solution.py:24
  156.4 6.1 %multiply_convert_fusion = (bf16[192,896]{1,0:T(8,128)(2,1)}, bf16[192,896]{1,0:T(8,128)(2,1)}, bf16[192,896]{1,0:T(8,128)(2,1)}) fusion(f32[192,896]{1,0:T(8,128)} %fusion.21, f32[192]{0:T(256)S(1)} %convert_reduce_fusion, bf16[192,896]{1,0:T(8,128)(2,1)S(1)} %copy-done.3, bf16[192,4096]{1,0:T(8,128)(2,1)S(1)} %bitcast.30, ...), kind=kOutput, calls=%fused_computation.16 | convolution fusion | flops 1412382720 | bytes 10978048 | tf_op jit(solution)/shard_map/dot_general | solution.py:57
  162.6 0.5 all-gather.12.cloned.1.call-update
  163.1 58.2 %all_to_all.41 = bf16[192,16,256]{2,0,1:T(8,128)(2,1)S(1)} all-to-all(bf16[192,16,256]{2,0,1:T(8,128)(2,1)S(1)} %bitcast.26), channel_id=1, replica_groups=mesh['dp'=16,'mp'=16] {'dp'}, dimensions={1} | all-to-all | bytes 3145728 | tf_op jit(solution)/shard_map/all_to_all | solution.py:42
  221.3 12.1 %all-gather.14.cloned.1.call-done = bf16[3072,896]{1,0:T(8,128)(2,1)} async-done(((bf16[192,896]{1,0:T(8,128)(2,1)}), bf16[3072,896]{1,0:T(8,128)(2,1)}) %all-gather.14.cloned.1.call-update) | async-done | bytes 5505040 | tf_op jit(solution)/shard_map/all_gather | solution.py:66
  233.4 5.2 %convolution_convert_fusion = bf16[256,896]{1,0:T(8,128)(2,1)} fusion(bf16[3072,256]{1,0:T(8,128)(2,1)S(1)} %bitcast.31, bf16[3072,896]{1,0:T(8,128)(2,1)} %all-gather.14.cloned.1.call-done), kind=kOutput, calls=%fused_computation.10 | convolution fusion | flops 1409515520 | bytes 7536640 | tf_op jit(solution)/shard_map/dot_general | solution.py:71
  238.6 39.4 %all-gather.12.cloned.1.call-done = bf16[3072,896]{1,0:T(8,128)(2,1)} async-done(((bf16[192,896]{1,0:T(8,128)(2,1)}), bf16[3072,896]{1,0:T(8,128)(2,1)}) %all-gather.12.cloned.1.call-update) | async-done | bytes 5505040 | tf_op jit(solution)/shard_map/all_gather | solution.py:65
  277.9 5.2 %convolution_convert_fusion.1 = bf16[256,896]{1,0:T(8,128)(2,1)} fusion(bf16[3072,256]{1,0:T(8,128)(2,1)S(1)} %bitcast.32, bf16[3072,896]{1,0:T(8,128)(2,1)} %all-gather.12.cloned.1.call-done), kind=kOutput, calls=%fused_computation.11 | convolution fusion | flops 1409515520 | bytes 7536640 | tf_op jit(solution)/shard_map/dot_general | solution.py:68
  (27 shorter events, 0.6 us)
Async XLA Ops:
  7.2 74.1 %all-gather.6.cloned.1.call-start = ((), (), s32[]{:S(2)}) async-start(), calls=%async_computation.5 | async-start | bytes 2228224 | tf_op jit(solution)/shard_map/all_gather | solution.py:26
  7.9 111.0 %all-gather.10.cloned.1.call-start = ((), (), s32[]{:S(2)}) async-start(), calls=%async_computation.7 | async-start | bytes 7798784 | tf_op jit(solution)/shard_map/all_gather | solution.py:23
  8.6 147.7 %all-gather.8.cloned.1.call-start = ((), (), s32[]{:S(2)}) async-start(), calls=%async_computation.6 | async-start | bytes 7798784 | tf_op jit(solution)/shard_map/all_gather | solution.py:24
  10.4 9.2 %copy-start = (s32[16,192]{1,0:T(8,128)S(1)}, s32[16,192]{1,0:T(8,128)}, u32[]{:S(2)}) copy-start(s32[16,192]{1,0:T(8,128)} %param.13) | copy-start | bytes 36868
  10.4 9.2 %copy-start.1 = (s32[16]{0:T(128)S(1)}, s32[16]{0:T(128)}, u32[]{:S(2)}) copy-start(s32[16]{0:T(128)} %param.14) | copy-start | bytes 196
  12.0 38.5 %all-to-all-start.2 = ((bf16[16,256,256]{1,2,0:T(8,128)(2,1)}), bf16[16,256,256]{1,2,0:T(8,128)(2,1)S(1)}, u32[]{:S(2)}, u32[]{:S(2)}) async-start(bf16[16,256,256]{1,2,0:T(8,128)(2,1)} %broadcast_in_dim.7), calls=%async_computation.2 | async-start | bytes 4194304 | tf_op jit(solution)/shard_map/all_to_all | solution.py:9
  50.5 3.6 %copy-start.2 = (bf16[4096,512]{1,0:T(8,128)(2,1)S(1)}, bf16[4096,512]{1,0:T(8,128)(2,1)}, u32[]{:S(2)}) copy-start(bf16[4096,512]{1,0:T(8,128)(2,1)} %param.11) | copy-start | bytes 12582916
  50.5 3.6 %copy-start.4 = (f32[512]{0:T(512)S(1)}, f32[512]{0:T(512)}, u32[]{:S(2)}) copy-start(f32[512]{0:T(512)} %param.12) | copy-start | bytes 6148
  56.1 10.3 %all-to-all-start.3 = ((f32[16,1,256]{2,1,0:T(1,128)}), f32[16,1,256]{2,1,0:T(1,128)S(1)}, u32[]{:S(2)}, u32[]{:S(2)}) async-start(f32[16,1,256]{2,1,0:T(1,128)} %broadcast_in_dim.8), calls=%async_computation.3 | async-start | bytes 32768 | tf_op jit(solution)/shard_map/all_to_all | solution.py:9
  70.2 18.6 %all-to-all-start.4 = ((bf16[16,1,192]{2,1,0:T(2,128)(2,1)}), bf16[16,1,192]{2,1,0:T(2,128)(2,1)S(1)}, u32[]{:S(2)}, u32[]{:S(2)}) async-start(bf16[16,1,192]{2,1,0:T(2,128)(2,1)} %all_to_all.35), calls=%async_computation.4 | async-start | bytes 32768 | tf_op jit(solution)/shard_map/all_to_all | solution.py:53
  90.1 28.6 %all-to-all-start = ((bf16[16,192,256]{2,1,0:T(8,128)(2,1)}), bf16[16,192,256]{2,1,0:T(8,128)(2,1)S(1)}, u32[]{:S(2)}, u32[]{:S(2)}) async-start(bf16[16,192,256]{2,1,0:T(8,128)(2,1)} %broadcast_in_dim.6), calls=%async_computation | async-start | bytes 3145728 | tf_op jit(solution)/shard_map/all_to_all | solution.py:9
  93.8 139.6 %all-gather.14.cloned.1.call-start = ((), (), s32[]{:S(2)}) async-start(), calls=%async_computation.9 | async-start | bytes 5849088 | tf_op jit(solution)/shard_map/all_gather | solution.py:66
  118.9 37.5 %copy-start.3 = (bf16[192,896]{1,0:T(8,128)(2,1)S(1)}, bf16[192,896]{1,0:T(8,128)(2,1)}, u32[]{:S(2)}) copy-start(bf16[192,896]{1,0:T(8,128)(2,1)} %param.17) | copy-start | bytes 1032196
  162.5 115.4 %all-gather.12.cloned.1.call-start = ((), (), s32[]{:S(2)}) async-start(), calls=%async_computation.8 | async-start | bytes 5849088 | tf_op jit(solution)/shard_map/all_gather | solution.py:65
Sparse Core Ops, SparseCore 0:
  9.8 43.5 all-gather.5
  55.2 49.7 all-gather.9
  106.8 49.4 all-gather.7
  162.6 70.7 all-gather.13
  235.7 42.2 all-gather.11

commit v5 on v4

--- a/solution.py
+++ b/solution.py
@@ -19,11 +19,11 @@
     cand_dev = candidates.shape[0]
     shards = chosen.shape[0]
     slots = chosen.shape[1]
-    full_w = (
-        lax.all_gather(gate_w, "dp", axis=0, tiled=True),
-        lax.all_gather(up_w, "dp", axis=0, tiled=True),
-    )
-    all_cands = lax.all_gather(candidates, "dp", axis=0, tiled=True)
+    width = candidates.shape[1]
+    ff = gate_w.shape[1]
+    merged = lax.all_gather(jnp.concatenate([candidates, gate_w, up_w], axis=1), "dp", axis=0, tiled=True)
+    all_cands = merged[:, :width]
+    full_w = (merged[:, width:width + ff], merged[:, width + ff:])
     own_index = lax.axis_index("dp")
     source = chosen // cand_dev
     local_row = (chosen % cand_dev).reshape(-1)
@@ -39,7 +39,10 @@
     ).astype(jnp.bfloat16)
     row_slab = jnp.dot(own_onehot, all_cands, preferred_element_type=jnp.float32).astype(jnp.bfloat16)
     row_x = gather_by_a2a(row_slab, "mp", 1)
-    row_slices = lax.all_to_all(row_x, "dp", split_axis=1, concat_axis=0, tiled=True)
+    parts = lax.psum(1, "dp")
+    row_blocks = row_x.reshape(row_x.shape[0], parts, -1).transpose(1, 0, 2)
+    row_slices = lax.all_to_all(row_blocks, "dp", split_axis=0, concat_axis=0, tiled=True)
+    row_slices = row_slices.reshape(-1, row_blocks.shape[2])
 
     incoming = gather_by_a2a(candidates, "mp", 1)
     hold_g = jnp.dot(incoming, hold_gate, preferred_element_type=jnp.float32)
@@ -61,10 +64,8 @@
     d_up = (back * gate * sig).astype(jnp.bfloat16)
     d_gate = (back * up * sig * (1.0 + gate * (1.0 - sig))).astype(jnp.bfloat16)
     contract_rows = (((0,), (0,)), ((), ()))
-    incoming = (
-        lax.all_gather(d_gate, "dp", axis=0, tiled=True),
-        lax.all_gather(d_up, "dp", axis=0, tiled=True),
-    )
+    both_d = lax.all_gather(jnp.concatenate([d_gate, d_up], axis=1), "dp", axis=0, tiled=True)
+    incoming = (both_d[:, :ff], both_d[:, ff:])
     grad_g = lax.dot_general(
         row_slices, incoming[0], contract_rows, preferred_element_type=jnp.float32
     )

time: 290 us -> 269 us (0.928)
  waiting for transfers between devices: 153 us -> 126 us
  matrix products: 32.1 us -> 28.6 us
  other arithmetic: 0.75 us -> 3.96 us
  blocking collectives: 58.2 us -> 61.4 us
    all_gather x5 -> x2, waiting for transfers between devices: 83.1 us -> 64.3 us  [the longest x1 35.3 us: on_device(): lax.all_gather(jnp.concatenate([d_gate, d_up], axis=1), 'dp', axis=0, til...]
    all_to_all x1, waiting for transfers between devices: 5.13 us -> 0.01 us  [on_device(): lax.all_to_all(picked_weight, 'dp', split_axis=0, concat_axis=0, tiled=True)]
    concatenate x0 -> x2, other arithmetic: none -> 3.21 us  [the longest x1 2.31 us: on_device(): jnp.concatenate([candidates, gate_w, up_w], axis=1)]
    all_to_all x1, blocking collectives: 58.2 us -> 61.4 us  [on_device(): lax.all_to_all(row_blocks, 'dp', split_axis=0, concat_axis=0, tiled=True)]
    all_to_all x3, starting transfers between devices: 15.1 us -> 18.2 us  [gather_by_a2a(): lax.all_to_all(jnp.broadcast_to(x[None], (parts,) + x.shape), axis_name,...]
  transfers between devices with their start and end apart: 9 -> 6, of which waited for: 7 -> 5; matrix products, arithmetic and copies ran while one was open for 9% -> 5% of each run, Pallas kernels for 0% -> 0%
where the time goes in v5:
time: 269 us; the launch traced here: 268 us
  waiting for transfers between devices  126 us (47%)
  blocking collectives  61.4 us (23%)
  starting transfers between devices  29.1 us (11%)
  matrix products  28.6 us (11%)
  between operations  14.2 us (5%)
  local copies, waits for them, and re-layouts  5.3 us (2%)
  other arithmetic  3.96 us (1%)
    all_to_all x3, waiting for transfers between devices, gather_by_a2a(): lax.all_to_all(jnp.broadcast_to(x[None], (parts,) + x.shape), axis_name,...  61.6 us
    all_to_all x1, blocking collectives, on_device(): lax.all_to_all(row_blocks, 'dp', split_axis=0, concat_axis=0, tiled=True)  61.4 us
    all_gather x1, waiting for transfers between devices, on_device(): lax.all_gather(jnp.concatenate([d_gate, d_up], axis=1), 'dp', axis=0, til...  35.3 us
    all_gather x1, waiting for transfers between devices, on_device(): lax.all_gather(jnp.concatenate([candidates, gate_w, up_w], axis=1), 'dp',...  29 us
    all_to_all x3, starting transfers between devices, gather_by_a2a(): lax.all_to_all(jnp.broadcast_to(x[None], (parts,) + x.shape), axis_name,...  18.2 us
    all_to_all x1, starting transfers between devices, on_device(): lax.all_to_all(picked_weight, 'dp', split_axis=0, concat_axis=0, tiled=True)  10.9 us
    dot_general x1, matrix products, on_device(): up = jnp.dot(row_x, full_w[1], preferred_element_type=jnp.float32)  5.8 us
  transfers between devices with their start and end apart: 6, of which 5 were waited for; matrix products, arithmetic and copies ran while one was open for 5% of the time, Pallas kernels for 0%

profile of v5, /device:TPU:1, one launch (start us, length us, event | category | flops | bytes accessed | tf_op | source)
XLA Modules:
  0.0 268.5 jit_solution(9712265441364224894)
XLA Ops:
  7.2 2.3 pad_maximum_fusion
  9.6 0.1 copy.22
  9.7 1.5 broadcast_in_dim.7
  11.2 7.7 %all-to-all-start.2 = ((bf16[16,256,256]{1,2,0:T(8,128)(2,1)}), bf16[16,256,256]{1,2,0:T(8,128)(2,1)S(1)}, u32[]{:S(2)}, u32[]{:S(2)}) async-start(bf16[16,256,256]{1,2,0:T(8,128)(2,1)} %broadcast_in_dim.7), calls=%async_computation.2 | async-start | bytes 4194304 | tf_op jit(solution)/shard_map/all_to_all | solution.py:9
  19.0 0.1 fusion.34
  19.0 30.8 %all-to-all-done.2 = bf16[16,256,256]{1,2,0:T(8,128)(2,1)S(1)} async-done(((bf16[16,256,256]{1,2,0:T(8,128)(2,1)}), bf16[16,256,256]{1,2,0:T(8,128)(2,1)S(1)}, u32[]{:S(2)}, u32[]{:S(2)}) %all-to-all-start.2) | async-done | bytes 2097184 | tf_op jit(solution)/shard_map/all_to_all | solution.py:9
  49.9 3.7 %fusion.37 = f32[256,512]{1,0:T(8,128)S(1)} fusion(bf16[256,4096]{0,1:T(8,128)(2,1)S(1)} %bitcast.19, bf16[4096,512]{1,0:T(8,128)(2,1)} %param.10), kind=kOutput, calls=%fused_computation.48 | convolution fusion | flops 1073741824 | bytes 6815744 | tf_op jit(solution)/shard_map/dot_general | solution.py:48
  53.6 1.4 fusion.26
  55.0 0.6 broadcast_in_dim.8
  55.6 3.9 %all-to-all-start.3 = ((f32[16,1,256]{2,1,0:T(1,128)}), f32[16,1,256]{2,1,0:T(1,128)S(1)}, u32[]{:S(2)}, u32[]{:S(2)}) async-start(f32[16,1,256]{2,1,0:T(1,128)} %broadcast_in_dim.8), calls=%async_computation.3 | async-start | bytes 32768 | tf_op jit(solution)/shard_map/all_to_all | solution.py:9
  59.6 0.1 and.40
  59.7 0.1 eq.42
  59.8 6.2 %all-to-all-done.3 = f32[16,1,256]{2,1,0:T(1,128)S(1)} async-done(((f32[16,1,256]{2,1,0:T(1,128)}), f32[16,1,256]{2,1,0:T(1,128)S(1)}, u32[]{:S(2)}, u32[]{:S(2)}) %all-to-all-start.3) | async-done | bytes 16416 | tf_op jit(solution)/shard_map/all_to_all | solution.py:9
  66.0 0.6 fusion.36
  66.6 2.5 fusion.12
  69.1 0.7 all_to_all.24
  69.8 10.9 %all-to-all-start.4 = ((bf16[16,1,192]{2,1,0:T(2,128)(2,1)}), bf16[16,1,192]{2,1,0:T(2,128)(2,1)S(1)}, u32[]{:S(2)}, u32[]{:S(2)}) async-start(bf16[16,1,192]{2,1,0:T(2,128)(2,1)} %all_to_all.24), calls=%async_computation.4 | async-start | bytes 32768 | tf_op jit(solution)/shard_map/all_to_all | solution.py:56
  80.7 29.0 %all-gather.3.cloned.1.call-done = bf16[4096,2048]{1,0:T(8,128)(2,1)} async-done(((bf16[256,2048]{1,0:T(8,128)(2,1)}), bf16[4096,2048]{1,0:T(8,128)(2,1)}) %all-gather.3.cloned.1.call-update) | async-done | bytes 16777232 | tf_op jit(solution)/shard_map/all_gather | solution.py:24
  109.7 2.4 fusion.27
  112.1 1.3 broadcast_in_dim.6
  113.5 6.5 %all-to-all-start = ((bf16[16,192,256]{2,1,0:T(8,128)(2,1)}), bf16[16,192,256]{2,1,0:T(8,128)(2,1)S(1)}, u32[]{:S(2)}, u32[]{:S(2)}) async-start(bf16[16,192,256]{2,1,0:T(8,128)(2,1)} %broadcast_in_dim.6), calls=%async_computation | async-start | bytes 3145728 | tf_op jit(solution)/shard_map/all_to_all | solution.py:9
  120.0 0.0 all-gather.5.cloned.1.call-start
  120.1 24.5 %all-to-all-done = bf16[16,192,256]{2,1,0:T(8,128)(2,1)S(1)} async-done(((bf16[16,192,256]{2,1,0:T(8,128)(2,1)}), bf16[16,192,256]{2,1,0:T(8,128)(2,1)S(1)}, u32[]{:S(2)}, u32[]{:S(2)}) %all-to-all-start) | async-done | bytes 1572896 | tf_op jit(solution)/shard_map/all_to_all | solution.py:9
  144.6 0.2 copy.27
  144.8 5.0 %fusion = f32[192,896]{1,0:T(8,128)S(1)} fusion(bf16[192,4096]{1,0:T(8,128)(2,1)S(1)} %bitcast.23, bf16[4096,2048]{1,0:T(8,128)(2,1)} %all-gather.3.cloned.1.call-done), kind=kOutput, calls=%fused_computation | convolution fusion | flops 1409286144 | bytes 9601024 | tf_op jit(solution)/shard_map/dot_general | solution.py:59
  149.7 5.8 %multiply_convert_fusion = (bf16[192,896]{1,0:T(8,128)(2,1)}, bf16[192,896]{1,0:T(8,128)(2,1)S(1)}, bf16[192,896]{1,0:T(8,128)(2,1)S(1)}) fusion(f32[192,896]{1,0:T(8,128)S(1)} %fusion, f32[192]{0:T(256)S(1)} %convert_reduce_fusion, bf16[192,896]{1,0:T(8,128)(2,1)S(1)} %copy-done.5, bf16[192,4096]{1,0:T(8,128)(2,1)S(1)} %bitcast.24, ...), kind=kOutput, calls=%fused_computation.27 | convolution fusion | flops 1412382720 | bytes 10978048 | tf_op jit(solution)/shard_map/dot_general | solution.py:60
  155.5 0.9 pad_maximum_fusion.1
  156.5 61.4 %all_to_all.30 = bf16[16,192,256]{2,1,0:T(8,128)(2,1)S(1)} all-to-all(bf16[16,192,256]{2,1,0:T(8,128)(2,1)S(1)} %all-to-all-done), channel_id=1, replica_groups=mesh['dp'=16,'mp'=16] {'dp'}, dimensions={0} | all-to-all | bytes 3145728 | tf_op jit(solution)/shard_map/all_to_all | solution.py:44
  217.8 35.3 %all-gather.5.cloned.1.call-done = bf16[3072,1792]{1,0:T(8,128)(2,1)} async-done(((bf16[192,1792]{1,0:T(8,128)(2,1)}), bf16[3072,1792]{1,0:T(8,128)(2,1)}) %all-gather.5.cloned.1.call-update) | async-done | bytes 11010064 | tf_op jit(solution)/shard_map/all_gather | solution.py:67
  253.1 5.3 %fusion.22 = bf16[256,896]{1,0:T(8,128)(2,1)} fusion(bf16[3072,256]{1,0:T(8,128)(2,1)S(1)} %bitcast.21, bf16[3072,1792]{1,0:T(8,128)(2,1)} %all-gather.5.cloned.1.call-done), kind=kOutput, calls=%fused_computation.20 | convolution fusion | flops 1409515520 | bytes 7536640 | tf_op jit(solution)/shard_map/dot_general | solution.py:72
  258.4 0.6 copy-done.3
  259.0 2.6 fusion.19
  (24 shorter events, 0.2 us)
Async XLA Ops:
  7.2 2.4 copy-start
  7.2 102.6 %all-gather.3.cloned.1.call-start = ((), (), s32[]{:S(2)}) async-start(), calls=%async_computation.5 | async-start | bytes 17825792 | tf_op jit(solution)/shard_map/all_gather | solution.py:24
  11.2 7.7 %copy-start.1 = (s32[16,192]{1,0:T(8,128)S(1)}, s32[16,192]{1,0:T(8,128)}, u32[]{:S(2)}) copy-start(s32[16,192]{1,0:T(8,128)} %param.13) | copy-start | bytes 36868
  11.2 7.7 %copy-start.2 = (s32[16]{0:T(128)S(1)}, s32[16]{0:T(128)}, u32[]{:S(2)}) copy-start(s32[16]{0:T(128)} %param.14) | copy-start | bytes 196
  11.2 38.7 %all-to-all-start.2 = ((bf16[16,256,256]{1,2,0:T(8,128)(2,1)}), bf16[16,256,256]{1,2,0:T(8,128)(2,1)S(1)}, u32[]{:S(2)}, u32[]{:S(2)}) async-start(bf16[16,256,256]{1,2,0:T(8,128)(2,1)} %broadcast_in_dim.7), calls=%async_computation.2 | async-start | bytes 4194304 | tf_op jit(solution)/shard_map/all_to_all | solution.py:9
  49.9 3.7 %copy-start.4 = (bf16[4096,512]{1,0:T(8,128)(2,1)S(1)}, bf16[4096,512]{1,0:T(8,128)(2,1)}, u32[]{:S(2)}) copy-start(bf16[4096,512]{1,0:T(8,128)(2,1)} %param.11) | copy-start | bytes 12582916
  49.9 3.7 %copy-start.6 = (f32[512]{0:T(512)S(1)}, f32[512]{0:T(512)}, u32[]{:S(2)}) copy-start(f32[512]{0:T(512)} %param.12) | copy-start | bytes 6148
  55.6 10.4 %all-to-all-start.3 = ((f32[16,1,256]{2,1,0:T(1,128)}), f32[16,1,256]{2,1,0:T(1,128)S(1)}, u32[]{:S(2)}, u32[]{:S(2)}) async-start(f32[16,1,256]{2,1,0:T(1,128)} %broadcast_in_dim.8), calls=%async_computation.3 | async-start | bytes 32768 | tf_op jit(solution)/shard_map/all_to_all | solution.py:9
  69.8 42.3 %all-to-all-start.4 = ((bf16[16,1,192]{2,1,0:T(2,128)(2,1)}), bf16[16,1,192]{2,1,0:T(2,128)(2,1)S(1)}, u32[]{:S(2)}, u32[]{:S(2)}) async-start(bf16[16,1,192]{2,1,0:T(2,128)(2,1)} %all_to_all.24), calls=%async_computation.4 | async-start | bytes 32768 | tf_op jit(solution)/shard_map/all_to_all | solution.py:56
  113.5 31.1 %all-to-all-start = ((bf16[16,192,256]{2,1,0:T(8,128)(2,1)}), bf16[16,192,256]{2,1,0:T(8,128)(2,1)S(1)}, u32[]{:S(2)}, u32[]{:S(2)}) async-start(bf16[16,192,256]{2,1,0:T(8,128)(2,1)} %broadcast_in_dim.6), calls=%async_computation | async-start | bytes 3145728 | tf_op jit(solution)/shard_map/all_to_all | solution.py:9
  120.0 133.1 %all-gather.5.cloned.1.call-start = ((), (), s32[]{:S(2)}) async-start(), calls=%async_computation.6 | async-start | bytes 11698176 | tf_op jit(solution)/shard_map/all_gather | solution.py:67
  144.7 5.0 %copy-start.5 = (bf16[192,896]{1,0:T(8,128)(2,1)S(1)}, bf16[192,896]{1,0:T(8,128)(2,1)}, u32[]{:S(2)}) copy-start(bf16[192,896]{1,0:T(8,128)(2,1)} %param.17) | copy-start | bytes 1032196
  253.1 5.9 %copy-start.3 = (bf16[3072,1792]{1,0:T(8,128)(2,1)S(1)}, bf16[3072,1792]{1,0:T(8,128)(2,1)}, u32[]{:S(2)}) copy-start(bf16[3072,1792]{1,0:T(8,128)(2,1)} %all-gather.5.cloned.1.call-done) | copy-start | bytes 33030148
Sparse Core Ops, SparseCore 0:
  9.8 99.8 all-gather.2
  156.6 96.4 all-gather.4

commit v6 on v5

--- a/solution.py
+++ b/solution.py
@@ -39,12 +39,17 @@
     ).astype(jnp.bfloat16)
     row_slab = jnp.dot(own_onehot, all_cands, preferred_element_type=jnp.float32).astype(jnp.bfloat16)
     row_x = gather_by_a2a(row_slab, "mp", 1)
-    parts = lax.psum(1, "dp")
-    row_blocks = row_x.reshape(row_x.shape[0], parts, -1).transpose(1, 0, 2)
-    row_slices = lax.all_to_all(row_blocks, "dp", split_axis=0, concat_axis=0, tiled=True)
-    row_slices = row_slices.reshape(-1, row_blocks.shape[2])
 
     incoming = gather_by_a2a(candidates, "mp", 1)
+    parts = lax.psum(1, "dp")
+    by_feature = incoming.reshape(cand_dev, parts, -1).transpose(1, 0, 2)
+    by_feature = lax.all_to_all(by_feature, "dp", split_axis=0, concat_axis=0, tiled=True)
+    by_feature = by_feature.reshape(-1, by_feature.shape[2])
+    all_onehot = (
+        (chosen.reshape(-1)[:, None] == jnp.arange(by_feature.shape[0], dtype=jnp.int32)[None, :])
+        & valid.reshape(-1)[:, None]
+    ).astype(jnp.bfloat16)
+    row_slices = jnp.dot(all_onehot, by_feature, preferred_element_type=jnp.float32).astype(jnp.bfloat16)
     hold_g = jnp.dot(incoming, hold_gate, preferred_element_type=jnp.float32)
     hold_u = jnp.dot(incoming, hold_up, preferred_element_type=jnp.float32)
     partial_score = jnp.sum(jax.nn.silu(hold_g) * hold_u * probe[None, :], axis=1)
@@ -56,6 +61,7 @@
     arrived_weight = lax.all_to_all(picked_weight, "dp", split_axis=0, concat_axis=0, tiled=True)
     row_weight = jnp.sum(arrived_weight.astype(jnp.float32), axis=0)
 
+    row_x, row_slices = lax.optimization_barrier((row_x, row_slices))
     gate = jnp.dot(row_x, full_w[0], preferred_element_type=jnp.float32)
     up = jnp.dot(row_x, full_w[1], preferred_element_type=jnp.float32)
     hidden = (jax.nn.silu(gate) * up).astype(jnp.bfloat16)

time: 269 us -> 278 us (1.033)
  blocking collectives: 61.4 us -> 18.3 us
  waiting for transfers between devices: 126 us -> 168 us
  matrix products: 28.6 us -> 42 us
  starting transfers between devices: 29.1 us -> 22.3 us
  local copies, waits for them, and re-layouts: 5.3 us -> 8.16 us
    all_to_all x1, blocking collectives: 61.4 us -> 18.3 us  [on_device(): lax.all_to_all(picked_weight, 'dp', split_axis=0, concat_axis=0, tiled=True)]
    all_gather x1, waiting for transfers between devices: 35.3 us -> 65.3 us  [on_device(): lax.all_gather(jnp.concatenate([d_gate, d_up], axis=1), 'dp', axis=0, til...]
    all_to_all x1, waiting for transfers between devices: 0.01 us -> 16.3 us  [on_device(): lax.all_to_all(by_feature, 'dp', split_axis=0, concat_axis=0, tiled=True)]
    all_to_all x3, waiting for transfers between devices: 61.6 us -> 47.2 us  [gather_by_a2a(): lax.all_to_all(jnp.broadcast_to(x[None], (parts,) + x.shape), axis_name,...]
    dot_general x0 -> x1, matrix products: none -> 13.2 us  [on_device(): jnp.dot(all_onehot, by_feature, preferred_element_type=jnp.float32)]
    all_gather x1, waiting for transfers between devices: 29 us -> 39.3 us  [on_device(): lax.all_gather(jnp.concatenate([candidates, gate_w, up_w], axis=1), 'dp',...]
    all_to_all x1, starting transfers between devices: 10.9 us -> 3.92 us  [on_device(): lax.all_to_all(by_feature, 'dp', split_axis=0, concat_axis=0, tiled=True)]
    transpose x0 -> x1, local copies, waits for them, and re-layouts: none -> 2.88 us  [gather_by_a2a(): stacked = jnp.moveaxis(stacked, 0, axis)]
  transfers between devices with their start and end apart: 6 -> 6, of which waited for: 5 -> 6; matrix products, arithmetic and copies ran while one was open for 5% -> 11% of each run, Pallas kernels for 0% -> 0%
where the time goes in v6:
time: 278 us; the launch traced here: 277 us
  waiting for transfers between devices  168 us (60%)
  matrix products  42 us (15%)
  starting transfers between devices  22.3 us (8%)
  blocking collectives  18.3 us (7%)
  between operations  14.2 us (5%)
  local copies, waits for them, and re-layouts  8.16 us (3%)
  other arithmetic  3.96 us (1%)
    all_gather x1, waiting for transfers between devices, on_device(): lax.all_gather(jnp.concatenate([d_gate, d_up], axis=1), 'dp', axis=0, til...  65.3 us
    all_to_all x3, waiting for transfers between devices, gather_by_a2a(): lax.all_to_all(jnp.broadcast_to(x[None], (parts,) + x.shape), axis_name,...  47.2 us
    all_gather x1, waiting for transfers between devices, on_device(): lax.all_gather(jnp.concatenate([candidates, gate_w, up_w], axis=1), 'dp',...  39.3 us
    all_to_all x1, blocking collectives, on_device(): lax.all_to_all(picked_weight, 'dp', split_axis=0, concat_axis=0, tiled=True)  18.3 us
    all_to_all x3, starting transfers between devices, gather_by_a2a(): lax.all_to_all(jnp.broadcast_to(x[None], (parts,) + x.shape), axis_name,...  18.1 us
    all_to_all x1, waiting for transfers between devices, on_device(): lax.all_to_all(by_feature, 'dp', split_axis=0, concat_axis=0, tiled=True)  16.3 us
    dot_general x1, matrix products, on_device(): jnp.dot(all_onehot, by_feature, preferred_element_type=jnp.float32)  13.2 us
    dot_general x1, matrix products, on_device(): up = jnp.dot(row_x, full_w[1], preferred_element_type=jnp.float32)  5.93 us
  transfers between devices with their start and end apart: 6, of which 6 were waited for; matrix products, arithmetic and copies ran while one was open for 11% of the time, Pallas kernels for 0%

profile of v6, /device:TPU:1, one launch (start us, length us, event | category | flops | bytes accessed | tf_op | source)
XLA Modules:
  0.0 277.1 jit_solution(11040498959246016723)
XLA Ops:
  7.2 2.3 pad_maximum_fusion
  9.6 1.5 broadcast_in_dim.7
  11.1 7.8 %all-to-all-start.1 = ((bf16[16,256,256]{2,1,0:T(8,128)(2,1)}), bf16[16,256,256]{2,1,0:T(8,128)(2,1)}, u32[]{:S(2)}, u32[]{:S(2)}) async-start(bf16[16,256,256]{2,1,0:T(8,128)(2,1)} %broadcast_in_dim.7), calls=%async_computation.1 | async-start | bytes 4194304 | tf_op jit(solution)/shard_map/all_to_all | solution.py:9
  18.9 31.0 %all-to-all-done.1 = bf16[16,256,256]{2,1,0:T(8,128)(2,1)} async-done(((bf16[16,256,256]{2,1,0:T(8,128)(2,1)}), bf16[16,256,256]{2,1,0:T(8,128)(2,1)}, u32[]{:S(2)}, u32[]{:S(2)}) %all-to-all-start.1) | async-done | bytes 2097184 | tf_op jit(solution)/shard_map/all_to_all | solution.py:9
  49.9 2.9 %copy.22 = bf16[256,16,256]{0,2,1:T(8,128)(2,1)S(1)} copy(bf16[256,16,256]{2,0,1:T(8,128)(2,1)} %bitcast.3) | data formatting | bytes 4194304 | tf_op jit(solution)/shard_map/transpose | solution.py:12
  52.8 3.7 %fusion.45 = f32[256,512]{1,0:T(8,128)S(1)} fusion(bf16[256,4096]{0,1:T(8,128)(2,1)S(1)} %bitcast.20, bf16[4096,512]{1,0:T(8,128)(2,1)} %param.10), kind=kOutput, calls=%fused_computation.54 | convolution fusion | flops 1073741824 | bytes 6815744 | tf_op jit(solution)/shard_map/dot_general | solution.py:53
  56.5 1.4 fusion.34
  57.9 0.6 broadcast_in_dim.8
  58.5 3.8 %all-to-all-start.3 = ((f32[16,1,256]{2,1,0:T(1,128)}), f32[16,1,256]{2,1,0:T(1,128)S(1)}, u32[]{:S(2)}, u32[]{:S(2)}) async-start(f32[16,1,256]{2,1,0:T(1,128)} %broadcast_in_dim.8), calls=%async_computation.3 | async-start | bytes 32768 | tf_op jit(solution)/shard_map/all_to_all | solution.py:9
  62.6 6.2 %all-to-all-done.3 = f32[16,1,256]{2,1,0:T(1,128)S(1)} async-done(((f32[16,1,256]{2,1,0:T(1,128)}), f32[16,1,256]{2,1,0:T(1,128)S(1)}, u32[]{:S(2)}, u32[]{:S(2)}) %all-to-all-start.3) | async-done | bytes 16416 | tf_op jit(solution)/shard_map/all_to_all | solution.py:9
  68.8 0.6 fusion.44
  69.4 2.5 fusion.20
  71.9 0.1 all_to_all.24
  72.0 18.3 %all_to_all.30 = bf16[16,1,192]{2,1,0:T(2,128)(2,1)S(1)} all-to-all(bf16[16,1,192]{2,1,0:T(2,128)(2,1)S(1)} %all_to_all.24), channel_id=1, replica_groups=mesh['dp'=16,'mp'=16] {'dp'}, dimensions={0} | all-to-all | bytes 12288 | tf_op jit(solution)/shard_map/all_to_all | solution.py:61
  90.3 3.9 %all-to-all-start.2 = ((bf16[16,256,256]{2,1,0:T(8,128)(2,1)}), bf16[16,256,256]{2,1,0:T(8,128)(2,1)S(1)}, u32[]{:S(2)}, u32[]{:S(2)}) async-start(bf16[16,256,256]{2,1,0:T(8,128)(2,1)} %all-to-all-done.1), calls=%async_computation.2 | async-start | bytes 4194304 | tf_op jit(solution)/shard_map/all_to_all | solution.py:46
  94.5 39.3 %all-gather.3.cloned.1.call-done = bf16[4096,2048]{1,0:T(8,128)(2,1)} async-done(((bf16[256,2048]{1,0:T(8,128)(2,1)}), bf16[4096,2048]{1,0:T(8,128)(2,1)}) %all-gather.3.cloned.1.call-update) | async-done | bytes 16777232 | tf_op jit(solution)/shard_map/all_gather | solution.py:24
  133.8 2.4 fusion.35
  136.1 16.3 %all-to-all-done.2 = bf16[16,256,256]{2,1,0:T(8,128)(2,1)S(1)} async-done(((bf16[16,256,256]{2,1,0:T(8,128)(2,1)}), bf16[16,256,256]{2,1,0:T(8,128)(2,1)S(1)}, u32[]{:S(2)}, u32[]{:S(2)}) %all-to-all-start.2) | async-done | bytes 2097184 | tf_op jit(solution)/shard_map/all_to_all | solution.py:46
  152.5 1.4 broadcast_in_dim.6
  153.9 0.4 copy-done
  154.3 6.6 %all-to-all-start = ((bf16[16,192,256]{2,1,0:T(8,128)(2,1)}), bf16[16,192,256]{2,1,0:T(8,128)(2,1)S(1)}, u32[]{:S(2)}, u32[]{:S(2)}) async-start(bf16[16,192,256]{2,1,0:T(8,128)(2,1)} %broadcast_in_dim.6), calls=%async_computation | async-start | bytes 3145728 | tf_op jit(solution)/shard_map/all_to_all | solution.py:9
  160.9 0.2 all-gather.5.cloned.1.call-start
  161.2 13.2 %fusion.13 = bf16[3072,256]{1,0:T(8,128)(2,1)} fusion(bf16[4096,256]{1,0:T(8,128)(2,1)} %bitcast.19, s32[3072]{0:T(1024)S(1)} %eq.57, pred[3072]{0:T(1024)(128)(4,1)S(1)} %lt.36), kind=kOutput, calls=%fused_computation.13 | convolution fusion | flops 6468403200 | bytes 3685376 | tf_op jit(solution)/shard_map/dot_general | solution.py:52
  174.4 10.0 %all-to-all-done = bf16[16,192,256]{2,1,0:T(8,128)(2,1)S(1)} async-done(((bf16[16,192,256]{2,1,0:T(8,128)(2,1)}), bf16[16,192,256]{2,1,0:T(8,128)(2,1)S(1)}, u32[]{:S(2)}, u32[]{:S(2)}) %all-to-all-start) | async-done | bytes 1572896 | tf_op jit(solution)/shard_map/all_to_all | solution.py:9
  184.4 0.2 copy.26
  184.6 5.0 %fusion.5 = f32[192,896]{1,0:T(8,128)S(1)} fusion(bf16[192,4096]{1,0:T(8,128)(2,1)S(1)} %bitcast.22, bf16[4096,2048]{1,0:T(8,128)(2,1)} %all-gather.3.cloned.1.call-done), kind=kOutput, calls=%fused_computation.5 | convolution fusion | flops 1409286144 | bytes 9601024 | tf_op jit(solution)/shard_map/dot_general | solution.py:65
  189.6 5.9 %multiply_convert_fusion = (bf16[192,896]{1,0:T(8,128)(2,1)}, bf16[192,896]{1,0:T(8,128)(2,1)S(1)}, bf16[192,896]{1,0:T(8,128)(2,1)S(1)}) fusion(f32[192,896]{1,0:T(8,128)S(1)} %fusion.5, f32[192]{0:T(256)S(1)} %convert_reduce_fusion, bf16[192,896]{1,0:T(8,128)(2,1)S(1)} %copy-done.6, bf16[192,4096]{1,0:T(8,128)(2,1)S(1)} %bitcast.23, ...), kind=kOutput, calls=%fused_computation.33 | convolution fusion | flops 1412382720 | bytes 10978048 | tf_op jit(solution)/shard_map/dot_general | solution.py:66
  195.5 0.9 pad_maximum_fusion.1
  196.4 65.3 %all-gather.5.cloned.1.call-done = bf16[3072,1792]{1,0:T(8,128)(2,1)} async-done(((bf16[192,1792]{1,0:T(8,128)(2,1)}), bf16[3072,1792]{1,0:T(8,128)(2,1)}) %all-gather.5.cloned.1.call-update) | async-done | bytes 11010064 | tf_op jit(solution)/shard_map/all_gather | solution.py:73
  261.7 5.3 %fusion.27 = bf16[256,896]{1,0:T(8,128)(2,1)} fusion(bf16[3072,256]{1,0:T(8,128)(2,1)S(1)} %copy-done.8, bf16[3072,1792]{1,0:T(8,128)(2,1)} %all-gather.5.cloned.1.call-done), kind=kOutput, calls=%fused_computation.25 | convolution fusion | flops 1409515520 | bytes 7536640 | tf_op jit(solution)/shard_map/dot_general | solution.py:75
  267.0 0.6 copy-done.4
  267.6 2.6 fusion.30
  (31 shorter events, 0.6 us)
Async XLA Ops:
  7.2 2.4 copy-start.1
  7.2 126.6 %all-gather.3.cloned.1.call-start = ((), (), s32[]{:S(2)}) async-start(), calls=%async_computation.5 | async-start | bytes 17825792 | tf_op jit(solution)/shard_map/all_gather | solution.py:24
  11.1 7.8 %copy-start.2 = (s32[16,192]{1,0:T(8,128)S(1)}, s32[16,192]{1,0:T(8,128)}, u32[]{:S(2)}) copy-start(s32[16,192]{1,0:T(8,128)} %param.13) | copy-start | bytes 36868
  11.1 38.8 %all-to-all-start.1 = ((bf16[16,256,256]{2,1,0:T(8,128)(2,1)}), bf16[16,256,256]{2,1,0:T(8,128)(2,1)}, u32[]{:S(2)}, u32[]{:S(2)}) async-start(bf16[16,256,256]{2,1,0:T(8,128)(2,1)} %broadcast_in_dim.7), calls=%async_computation.1 | async-start | bytes 4194304 | tf_op jit(solution)/shard_map/all_to_all | solution.py:9
  52.8 3.7 %copy-start.5 = (bf16[4096,512]{1,0:T(8,128)(2,1)S(1)}, bf16[4096,512]{1,0:T(8,128)(2,1)}, u32[]{:S(2)}) copy-start(bf16[4096,512]{1,0:T(8,128)(2,1)} %param.11) | copy-start | bytes 12582916
  52.8 3.7 %copy-start.7 = (f32[512]{0:T(512)S(1)}, f32[512]{0:T(512)}, u32[]{:S(2)}) copy-start(f32[512]{0:T(512)} %param.12) | copy-start | bytes 6148
  56.5 5.8 %copy-start.3 = (s32[16]{0:T(128)S(1)}, s32[16]{0:T(128)}, u32[]{:S(2)}) copy-start(s32[16]{0:T(128)} %param.14) | copy-start | bytes 196
  58.5 10.2 %all-to-all-start.3 = ((f32[16,1,256]{2,1,0:T(1,128)}), f32[16,1,256]{2,1,0:T(1,128)S(1)}, u32[]{:S(2)}, u32[]{:S(2)}) async-start(f32[16,1,256]{2,1,0:T(1,128)} %broadcast_in_dim.8), calls=%async_computation.3 | async-start | bytes 32768 | tf_op jit(solution)/shard_map/all_to_all | solution.py:9
  90.3 62.1 %all-to-all-start.2 = ((bf16[16,256,256]{2,1,0:T(8,128)(2,1)}), bf16[16,256,256]{2,1,0:T(8,128)(2,1)S(1)}, u32[]{:S(2)}, u32[]{:S(2)}) async-start(bf16[16,256,256]{2,1,0:T(8,128)(2,1)} %all-to-all-done.1), calls=%async_computation.2 | async-start | bytes 4194304 | tf_op jit(solution)/shard_map/all_to_all | solution.py:46
  152.5 1.9 copy-start
  154.3 30.1 %all-to-all-start = ((bf16[16,192,256]{2,1,0:T(8,128)(2,1)}), bf16[16,192,256]{2,1,0:T(8,128)(2,1)S(1)}, u32[]{:S(2)}, u32[]{:S(2)}) async-start(bf16[16,192,256]{2,1,0:T(8,128)(2,1)} %broadcast_in_dim.6), calls=%async_computation | async-start | bytes 3145728 | tf_op jit(solution)/shard_map/all_to_all | solution.py:9
  160.9 100.8 %all-gather.5.cloned.1.call-start = ((), (), s32[]{:S(2)}) async-start(), calls=%async_computation.6 | async-start | bytes 11698176 | tf_op jit(solution)/shard_map/all_gather | solution.py:73
  184.6 5.0 %copy-start.6 = (bf16[192,896]{1,0:T(8,128)(2,1)S(1)}, bf16[192,896]{1,0:T(8,128)(2,1)}, u32[]{:S(2)}) copy-start(bf16[192,896]{1,0:T(8,128)(2,1)} %param.17) | copy-start | bytes 1032196
  189.6 72.2 %copy-start.8 = (bf16[3072,256]{1,0:T(8,128)(2,1)S(1)}, bf16[3072,256]{1,0:T(8,128)(2,1)}, u32[]{:S(2)}) copy-start(bf16[3072,256]{1,0:T(8,128)(2,1)} %fusion.13) | copy-start | bytes 4718596
  261.7 5.9 %copy-start.4 = (bf16[3072,1792]{1,0:T(8,128)(2,1)S(1)}, bf16[3072,1792]{1,0:T(8,128)(2,1)}, u32[]{:S(2)}) copy-start(bf16[3072,1792]{1,0:T(8,128)(2,1)} %all-gather.5.cloned.1.call-done) | copy-start | bytes 33030148
Sparse Core Ops, SparseCore 0:
  9.8 123.9 all-gather.2
  196.6 65.1 all-gather.4

commit v7 on v5

--- a/solution.py
+++ b/solution.py
@@ -21,9 +21,9 @@
     slots = chosen.shape[1]
     width = candidates.shape[1]
     ff = gate_w.shape[1]
-    merged = lax.all_gather(jnp.concatenate([candidates, gate_w, up_w], axis=1), "dp", axis=0, tiled=True)
+    merged = lax.all_gather(jnp.concatenate([candidates, gate_w], axis=1), "dp", axis=0, tiled=True)
     all_cands = merged[:, :width]
-    full_w = (merged[:, width:width + ff], merged[:, width + ff:])
+    full_w = (merged[:, width:], lax.all_gather(up_w, "dp", axis=0, tiled=True))
     own_index = lax.axis_index("dp")
     source = chosen // cand_dev
     local_row = (chosen % cand_dev).reshape(-1)

time: 269 us -> 244 us (0.907)
  waiting for transfers between devices: 126 us -> 106 us
  blocking collectives: 61.4 us -> 58.2 us
  starting transfers between devices: 29.1 us -> 26.3 us
    all_gather x1 -> x2, waiting for transfers between devices: 29 us -> 0.81 us  [the longest x1 0.8 us: on_device(): full_w = (merged[:, width:], lax.all_gather(up_w, 'dp', axis=0, tiled=True))]
    all_to_all x1, waiting for transfers between devices: 0.01 us -> 4.94 us  [on_device(): lax.all_to_all(picked_weight, 'dp', split_axis=0, concat_axis=0, tiled=True)]
    all_to_all x1, blocking collectives: 61.4 us -> 58.2 us  [on_device(): lax.all_to_all(row_blocks, 'dp', split_axis=0, concat_axis=0, tiled=True)]
    all_to_all x3, starting transfers between devices: 18.2 us -> 15.2 us  [gather_by_a2a(): lax.all_to_all(jnp.broadcast_to(x[None], (parts,) + x.shape), axis_name,...]
    dot_general x1, matrix products: 5.3 us -> 2.59 us  [on_device(): lax.dot_general(row_slices, incoming[1], contract_rows, preferred_element...]
    dot_general x1, matrix products: 2.59 us -> 5.3 us  [on_device(): lax.dot_general(row_slices, incoming[0], contract_rows, preferred_element...]
  transfers between devices with their start and end apart: 6 -> 7, of which waited for: 5 -> 6; matrix products, arithmetic and copies ran while one was open for 5% -> 9% of each run, Pallas kernels for 0% -> 0%
where the time goes in v7:
time: 244 us
  waiting for transfers between devices  106 us (43%)
  blocking collectives  58.2 us (24%)
  matrix products  29.7 us (12%)
  starting transfers between devices  26.3 us (11%)
  between operations  13.9 us (6%)
  local copies, waits for them, and re-layouts  6.2 us (3%)
  other arithmetic  3.57 us (1%)
    all_to_all x3, waiting for transfers between devices, gather_by_a2a(): lax.all_to_all(jnp.broadcast_to(x[None], (parts,) + x.shape), axis_name,...  61.9 us
    all_to_all x1, blocking collectives, on_device(): lax.all_to_all(row_blocks, 'dp', split_axis=0, concat_axis=0, tiled=True)  58.2 us
    all_gather x1, waiting for transfers between devices, on_device(): lax.all_gather(jnp.concatenate([d_gate, d_up], axis=1), 'dp', axis=0, til...  37.3 us
    all_to_all x3, starting transfers between devices, gather_by_a2a(): lax.all_to_all(jnp.broadcast_to(x[None], (parts,) + x.shape), axis_name,...  15.2 us
    all_to_all x1, starting transfers between devices, on_device(): lax.all_to_all(picked_weight, 'dp', split_axis=0, concat_axis=0, tiled=True)  10.9 us
    dot_general x1, matrix products, on_device(): gate = jnp.dot(row_x, full_w[0], preferred_element_type=jnp.float32)  5.95 us
    dot_general x1, matrix products, on_device(): up = jnp.dot(row_x, full_w[1], preferred_element_type=jnp.float32)  5.92 us
    dot_general x1, matrix products, on_device(): lax.dot_general(row_slices, incoming[0], contract_rows, preferred_element...  5.3 us
  transfers between devices with their start and end apart: 7, of which 6 were waited for; matrix products, arithmetic and copies ran while one was open for 9% of the time, Pallas kernels for 0%

profile of v7, /device:TPU:1, one launch (start us, length us, event | category | flops | bytes accessed | tf_op | source)
XLA Modules:
  0.0 243.6 jit_solution(15453034456665766605)
XLA Ops:
  7.2 1.9 pad_maximum_fusion.1
  9.2 0.7 all-gather.6.cloned.1.call-update
  9.9 1.0 copy.22
  10.9 1.5 broadcast_in_dim.7
  12.5 7.6 %all-to-all-start.2 = ((bf16[16,256,256]{1,2,0:T(8,128)(2,1)}), bf16[16,256,256]{1,2,0:T(8,128)(2,1)S(1)}, u32[]{:S(2)}, u32[]{:S(2)}) async-start(bf16[16,256,256]{1,2,0:T(8,128)(2,1)} %broadcast_in_dim.7), calls=%async_computation.2 | async-start | bytes 4194304 | tf_op jit(solution)/shard_map/all_to_all | solution.py:9
  20.1 0.1 fusion.32
  20.2 30.8 %all-to-all-done.2 = bf16[16,256,256]{1,2,0:T(8,128)(2,1)S(1)} async-done(((bf16[16,256,256]{1,2,0:T(8,128)(2,1)}), bf16[16,256,256]{1,2,0:T(8,128)(2,1)S(1)}, u32[]{:S(2)}, u32[]{:S(2)}) %all-to-all-start.2) | async-done | bytes 2097184 | tf_op jit(solution)/shard_map/all_to_all | solution.py:9
  51.0 3.7 %fusion.35 = f32[256,512]{1,0:T(8,128)S(1)} fusion(bf16[256,4096]{0,1:T(8,128)(2,1)S(1)} %bitcast.20, bf16[4096,512]{1,0:T(8,128)(2,1)} %param.10), kind=kOutput, calls=%fused_computation.46 | convolution fusion | flops 1073741824 | bytes 6815744 | tf_op jit(solution)/shard_map/dot_general | solution.py:48
  54.7 1.4 fusion.24
  56.1 0.6 broadcast_in_dim.8
  56.7 3.9 %all-to-all-start.3 = ((f32[16,1,256]{2,1,0:T(1,128)}), f32[16,1,256]{2,1,0:T(1,128)S(1)}, u32[]{:S(2)}, u32[]{:S(2)}) async-start(f32[16,1,256]{2,1,0:T(1,128)} %broadcast_in_dim.8), calls=%async_computation.3 | async-start | bytes 32768 | tf_op jit(solution)/shard_map/all_to_all | solution.py:9
  60.8 0.1 and.40
  60.9 6.2 %all-to-all-done.3 = f32[16,1,256]{2,1,0:T(1,128)S(1)} async-done(((f32[16,1,256]{2,1,0:T(1,128)}), f32[16,1,256]{2,1,0:T(1,128)S(1)}, u32[]{:S(2)}, u32[]{:S(2)}) %all-to-all-start.3) | async-done | bytes 16416 | tf_op jit(solution)/shard_map/all_to_all | solution.py:9
  67.2 0.6 fusion.34
  67.7 2.5 %fusion.10 = f32[1,3072]{1,0:T(1,128)S(1)} fusion(bf16[256,1]{0,1:T(2,128)(2,1)S(1)} %reshape.45, s32[3072]{0:T(1024)S(1)} %eq.42, pred[3072]{0:T(1024)(128)(4,1)S(1)} %and.40), kind=kOutput, calls=%fused_computation.11 | convolution fusion | flops 3145728 | bytes 28160 | tf_op jit(solution)/shard_map/dot_general | solution.py:53
  70.2 0.7 all_to_all.24
  70.9 10.9 %all-to-all-start.4 = ((bf16[16,1,192]{2,1,0:T(2,128)(2,1)}), bf16[16,1,192]{2,1,0:T(2,128)(2,1)S(1)}, u32[]{:S(2)}, u32[]{:S(2)}) async-start(bf16[16,1,192]{2,1,0:T(2,128)(2,1)} %all_to_all.24), calls=%async_computation.4 | async-start | bytes 32768 | tf_op jit(solution)/shard_map/all_to_all | solution.py:56
  81.9 2.4 fusion.25
  84.3 4.9 %all-to-all-done.4 = bf16[16,1,192]{2,1,0:T(2,128)(2,1)S(1)} async-done(((bf16[16,1,192]{2,1,0:T(2,128)(2,1)}), bf16[16,1,192]{2,1,0:T(2,128)(2,1)S(1)}, u32[]{:S(2)}, u32[]{:S(2)}) %all-to-all-start.4) | async-done | bytes 6176 | tf_op jit(solution)/shard_map/all_to_all | solution.py:56
  89.2 1.3 broadcast_in_dim.6
  90.5 3.7 %all-to-all-start = ((bf16[16,192,256]{2,1,0:T(8,128)(2,1)}), bf16[16,192,256]{2,1,0:T(8,128)(2,1)S(1)}, u32[]{:S(2)}, u32[]{:S(2)}) async-start(bf16[16,192,256]{2,1,0:T(8,128)(2,1)} %broadcast_in_dim.6), calls=%async_computation | async-start | bytes 3145728 | tf_op jit(solution)/shard_map/all_to_all | solution.py:9
  94.4 24.8 %all-to-all-done = bf16[16,192,256]{2,1,0:T(8,128)(2,1)S(1)} async-done(((bf16[16,192,256]{2,1,0:T(8,128)(2,1)}), bf16[16,192,256]{2,1,0:T(8,128)(2,1)S(1)}, u32[]{:S(2)}, u32[]{:S(2)}) %all-to-all-start) | async-done | bytes 1572896 | tf_op jit(solution)/shard_map/all_to_all | solution.py:9
  119.2 0.2 copy.27
  119.4 5.9 %fusion = f32[192,896]{1,0:T(8,128)} fusion(bf16[192,4096]{1,0:T(8,128)(2,1)S(1)} %bitcast.22, bf16[4096,1152]{1,0:T(8,128)(2,1)} %all-gather.4.cloned.1.call-done), kind=kOutput, calls=%fused_computation | convolution fusion | flops 1409286144 | bytes 9601024 | tf_op jit(solution)/shard_map/dot_general | solution.py:59
  125.3 0.8 all-gather.6.cloned.1.call-done
  126.1 5.9 %multiply_convert_fusion = (bf16[192,896]{1,0:T(8,128)(2,1)}, bf16[192,896]{1,0:T(8,128)(2,1)S(1)}, bf16[192,896]{1,0:T(8,128)(2,1)S(1)}) fusion(f32[192,896]{1,0:T(8,128)} %fusion, f32[192]{0:T(256)S(1)} %convert_reduce_fusion, bf16[192,896]{1,0:T(8,128)(2,1)S(1)} %copy-done.4, bf16[192,4096]{1,0:T(8,128)(2,1)S(1)} %bitcast.23, ...), kind=kOutput, calls=%fused_computation.24 | convolution fusion | flops 1412382720 | bytes 10978048 | tf_op jit(solution)/shard_map/dot_general | solution.py:60
  132.0 0.9 pad_maximum_fusion
  133.0 58.2 %all_to_all.30 = bf16[16,192,256]{2,1,0:T(8,128)(2,1)S(1)} all-to-all(bf16[16,192,256]{2,1,0:T(8,128)(2,1)S(1)} %all-to-all-done), channel_id=1, replica_groups=mesh['dp'=16,'mp'=16] {'dp'}, dimensions={0} | all-to-all | bytes 3145728 | tf_op jit(solution)/shard_map/all_to_all | solution.py:44
  191.2 37.3 %all-gather.8.cloned.1.call-done = bf16[3072,1792]{1,0:T(8,128)(2,1)} async-done(((bf16[192,1792]{1,0:T(8,128)(2,1)}), bf16[3072,1792]{1,0:T(8,128)(2,1)}) %all-gather.8.cloned.1.call-update) | async-done | bytes 11010064 | tf_op jit(solution)/shard_map/all_gather | solution.py:67
  228.5 5.3 %fusion.17 = bf16[256,896]{1,0:T(8,128)(2,1)} fusion(bf16[3072,256]{1,0:T(8,128)(2,1)S(1)} %bitcast.24, bf16[3072,1792]{1,0:T(8,128)(2,1)} %all-gather.8.cloned.1.call-done), kind=kOutput, calls=%fused_computation.17 | convolution fusion | flops 1409515520 | bytes 7536640 | tf_op jit(solution)/shard_map/dot_general | solution.py:69
  233.8 0.6 copy-done.2
  234.4 2.6 %fusion.20 = bf16[256,896]{1,0:T(8,128)(2,1)} fusion(bf16[3072,256]{1,0:T(8,128)(2,1)S(1)} %bitcast.25, bf16[3072,1792]{1,0:T(8,128)(2,1)S(1)} %copy-done.2), kind=kOutput, calls=%fused_computation.18 | convolution fusion | flops 1409515520 | bytes 7536640 | tf_op jit(solution)/shard_map/dot_general | solution.py:72
  (25 shorter events, 0.4 us)
Async XLA Ops:
  7.2 74.7 %all-gather.4.cloned.1.call-start = ((), (), s32[]{:S(2)}) async-start(), calls=%async_computation.5 | async-start | bytes 10027008 | tf_op jit(solution)/shard_map/all_gather | solution.py:24
  9.2 117.0 %all-gather.6.cloned.1.call-start = ((), (), s32[]{:S(2)}) async-start(), calls=%async_computation.6 | async-start | bytes 7798784 | tf_op jit(solution)/shard_map/all_gather | solution.py:26
  10.9 9.2 %copy-start = (s32[16,192]{1,0:T(8,128)S(1)}, s32[16,192]{1,0:T(8,128)}, u32[]{:S(2)}) copy-start(s32[16,192]{1,0:T(8,128)} %param.13) | copy-start | bytes 36868
  10.9 9.2 %copy-start.1 = (s32[16]{0:T(128)S(1)}, s32[16]{0:T(128)}, u32[]{:S(2)}) copy-start(s32[16]{0:T(128)} %param.14) | copy-start | bytes 196
  12.5 38.5 %all-to-all-start.2 = ((bf16[16,256,256]{1,2,0:T(8,128)(2,1)}), bf16[16,256,256]{1,2,0:T(8,128)(2,1)S(1)}, u32[]{:S(2)}, u32[]{:S(2)}) async-start(bf16[16,256,256]{1,2,0:T(8,128)(2,1)} %broadcast_in_dim.7), calls=%async_computation.2 | async-start | bytes 4194304 | tf_op jit(solution)/shard_map/all_to_all | solution.py:9
  51.0 3.7 %copy-start.3 = (bf16[4096,512]{1,0:T(8,128)(2,1)S(1)}, bf16[4096,512]{1,0:T(8,128)(2,1)}, u32[]{:S(2)}) copy-start(bf16[4096,512]{1,0:T(8,128)(2,1)} %param.11) | copy-start | bytes 12582916
  51.0 3.7 %copy-start.5 = (f32[512]{0:T(512)S(1)}, f32[512]{0:T(512)}, u32[]{:S(2)}) copy-start(f32[512]{0:T(512)} %param.12) | copy-start | bytes 6148
  56.7 10.4 %all-to-all-start.3 = ((f32[16,1,256]{2,1,0:T(1,128)}), f32[16,1,256]{2,1,0:T(1,128)S(1)}, u32[]{:S(2)}, u32[]{:S(2)}) async-start(f32[16,1,256]{2,1,0:T(1,128)} %broadcast_in_dim.8), calls=%async_computation.3 | async-start | bytes 32768 | tf_op jit(solution)/shard_map/all_to_all | solution.py:9
  70.9 18.3 %all-to-all-start.4 = ((bf16[16,1,192]{2,1,0:T(2,128)(2,1)}), bf16[16,1,192]{2,1,0:T(2,128)(2,1)S(1)}, u32[]{:S(2)}, u32[]{:S(2)}) async-start(bf16[16,1,192]{2,1,0:T(2,128)(2,1)} %all_to_all.24), calls=%async_computation.4 | async-start | bytes 32768 | tf_op jit(solution)/shard_map/all_to_all | solution.py:56
  90.5 28.6 %all-to-all-start = ((bf16[16,192,256]{2,1,0:T(8,128)(2,1)}), bf16[16,192,256]{2,1,0:T(8,128)(2,1)S(1)}, u32[]{:S(2)}, u32[]{:S(2)}) async-start(bf16[16,192,256]{2,1,0:T(8,128)(2,1)} %broadcast_in_dim.6), calls=%async_computation | async-start | bytes 3145728 | tf_op jit(solution)/shard_map/all_to_all | solution.py:9
  94.3 134.3 %all-gather.8.cloned.1.call-start = ((), (), s32[]{:S(2)}) async-start(), calls=%async_computation.7 | async-start | bytes 11698176 | tf_op jit(solution)/shard_map/all_gather | solution.py:67
  119.4 6.8 %copy-start.4 = (bf16[192,896]{1,0:T(8,128)(2,1)S(1)}, bf16[192,896]{1,0:T(8,128)(2,1)}, u32[]{:S(2)}) copy-start(bf16[192,896]{1,0:T(8,128)(2,1)} %param.17) | copy-start | bytes 1032196
  228.5 5.9 %copy-start.2 = (bf16[3072,1792]{1,0:T(8,128)(2,1)S(1)}, bf16[3072,1792]{1,0:T(8,128)(2,1)}, u32[]{:S(2)}) copy-start(bf16[3072,1792]{1,0:T(8,128)(2,1)} %all-gather.8.cloned.1.call-done) | copy-start | bytes 33030148
Sparse Core Ops, SparseCore 0:
  9.8 64.9 all-gather.3
  76.6 49.4 all-gather.5
  133.1 95.3 all-gather.7

commit v8 on v7

--- a/solution.py
+++ b/solution.py
@@ -50,14 +50,16 @@
     partial_score = jnp.sum(jax.nn.silu(hold_g) * hold_u * probe[None, :], axis=1)
     score = jnp.sum(gather_by_a2a(partial_score[None, :], "mp", 0), axis=0)
     cand_weight = jax.nn.sigmoid(score)
+    late_weight, row_x = lax.optimization_barrier((cand_weight, row_x))
     picked_weight = jnp.dot(
-        onehot, cand_weight.astype(jnp.bfloat16)[:, None], preferred_element_type=jnp.float32
+        onehot, late_weight.astype(jnp.bfloat16)[:, None], preferred_element_type=jnp.float32
     ).astype(jnp.bfloat16).reshape(shards, slots)
     arrived_weight = lax.all_to_all(picked_weight, "dp", split_axis=0, concat_axis=0, tiled=True)
     row_weight = jnp.sum(arrived_weight.astype(jnp.float32), axis=0)
 
     gate = jnp.dot(row_x, full_w[0], preferred_element_type=jnp.float32)
-    up = jnp.dot(row_x, full_w[1], preferred_element_type=jnp.float32)
+    row_slices, up_w_full = lax.optimization_barrier((row_slices, full_w[1]))
+    up = jnp.dot(row_x, up_w_full, preferred_element_type=jnp.float32)
     hidden = (jax.nn.silu(gate) * up).astype(jnp.bfloat16)
     back = cotangent.astype(jnp.float32) * row_weight[:, None]
     sig = jax.nn.sigmoid(gate)

time: 244 us -> 254 us (1.041)
  waiting for transfers between devices: 106 us -> 166 us
  blocking collectives: 58.2 us -> 12.9 us
  starting transfers between devices: 26.3 us -> 22.1 us
    all_to_all x1, blocking collectives: 58.2 us -> 12.9 us  [on_device(): lax.all_to_all(picked_weight, 'dp', split_axis=0, concat_axis=0, tiled=True)]
    all_to_all x1, waiting for transfers between devices: 4.94 us -> 32.7 us  [on_device(): lax.all_to_all(row_blocks, 'dp', split_axis=0, concat_axis=0, tiled=True)]
    all_gather x1, waiting for transfers between devices: 37.3 us -> 62.9 us  [on_device(): lax.all_gather(jnp.concatenate([d_gate, d_up], axis=1), 'dp', axis=0, til...]
    all_gather x1, waiting for transfers between devices: 0.01 us -> 14.1 us  [on_device(): lax.all_gather(jnp.concatenate([candidates, gate_w], axis=1), 'dp', axis=...]
    all_to_all x1, starting transfers between devices: 10.9 us -> 3.89 us  [on_device(): lax.all_to_all(row_blocks, 'dp', split_axis=0, concat_axis=0, tiled=True)]
    all_to_all x3, waiting for transfers between devices: 61.9 us -> 55.2 us  [gather_by_a2a(): lax.all_to_all(jnp.broadcast_to(x[None], (parts,) + x.shape), axis_name,...]
    all_to_all x3, starting transfers between devices: 15.2 us -> 18.1 us  [gather_by_a2a(): lax.all_to_all(jnp.broadcast_to(x[None], (parts,) + x.shape), axis_name,...]
    dot_general x1, matrix products: 2.59 us -> 5.3 us  [on_device(): lax.dot_general(row_slices, incoming[1], contract_rows, preferred_element...]
  transfers between devices with their start and end apart: 7 -> 7, of which waited for: 6 -> 5; matrix products, arithmetic and copies ran while one was open for 9% -> 9% of each run, Pallas kernels for 0% -> 0%
where the time goes in v8:
time: 254 us
  waiting for transfers between devices  166 us (65%)
  matrix products  29.5 us (12%)
  starting transfers between devices  22.1 us (9%)
  between operations  13.9 us (5%)
  blocking collectives  12.9 us (5%)
  local copies, waits for them, and re-layouts  7 us (3%)
  other arithmetic  3 us (1%)
    all_gather x1, waiting for transfers between devices, on_device(): lax.all_gather(jnp.concatenate([d_gate, d_up], axis=1), 'dp', axis=0, til...  62.9 us
    all_to_all x3, waiting for transfers between devices, gather_by_a2a(): lax.all_to_all(jnp.broadcast_to(x[None], (parts,) + x.shape), axis_name,...  55.2 us
    all_to_all x1, waiting for transfers between devices, on_device(): lax.all_to_all(row_blocks, 'dp', split_axis=0, concat_axis=0, tiled=True)  32.7 us
    all_to_all x3, starting transfers between devices, gather_by_a2a(): lax.all_to_all(jnp.broadcast_to(x[None], (parts,) + x.shape), axis_name,...  18.1 us
    all_gather x1, waiting for transfers between devices, on_device(): lax.all_gather(jnp.concatenate([candidates, gate_w], axis=1), 'dp', axis=...  14.1 us
    all_to_all x1, blocking collectives, on_device(): lax.all_to_all(picked_weight, 'dp', split_axis=0, concat_axis=0, tiled=True)  12.9 us
    dot_general x1, matrix products, on_device(): up = jnp.dot(row_x, up_w_full, preferred_element_type=jnp.float32)  5.87 us
    dot_general x1, matrix products, on_device(): gate = jnp.dot(row_x, full_w[0], preferred_element_type=jnp.float32)  5.77 us
  transfers between devices with their start and end apart: 7, of which 5 were waited for; matrix products, arithmetic and copies ran while one was open for 9% of the time, Pallas kernels for 0%

profile of v8, /device:TPU:1, one launch (start us, length us, event | category | flops | bytes accessed | tf_op | source)
XLA Modules:
  0.0 254.0 jit_solution(4487285827441276958)
XLA Ops:
  7.2 1.9 pad_maximum_fusion.1
  9.2 0.7 all-gather.6.cloned.1.call-update
  9.9 1.0 copy.22
  10.9 1.5 broadcast_in_dim.7
  12.5 7.6 %all-to-all-start.2 = ((bf16[16,256,256]{1,2,0:T(8,128)(2,1)}), bf16[16,256,256]{1,2,0:T(8,128)(2,1)S(1)}, u32[]{:S(2)}, u32[]{:S(2)}) async-start(bf16[16,256,256]{1,2,0:T(8,128)(2,1)} %broadcast_in_dim.7), calls=%async_computation.2 | async-start | bytes 4194304 | tf_op jit(solution)/shard_map/all_to_all | solution.py:9
  20.1 0.1 fusion.32
  20.2 30.8 %all-to-all-done.2 = bf16[16,256,256]{1,2,0:T(8,128)(2,1)S(1)} async-done(((bf16[16,256,256]{1,2,0:T(8,128)(2,1)}), bf16[16,256,256]{1,2,0:T(8,128)(2,1)S(1)}, u32[]{:S(2)}, u32[]{:S(2)}) %all-to-all-start.2) | async-done | bytes 2097184 | tf_op jit(solution)/shard_map/all_to_all | solution.py:9
  51.0 3.7 %fusion.34 = f32[256,512]{1,0:T(8,128)S(1)} fusion(bf16[256,4096]{0,1:T(8,128)(2,1)S(1)} %bitcast.19, bf16[4096,512]{1,0:T(8,128)(2,1)} %param.10), kind=kOutput, calls=%fused_computation.45 | convolution fusion | flops 1073741824 | bytes 6815744 | tf_op jit(solution)/shard_map/dot_general | solution.py:48
  54.7 1.4 fusion.24
  56.1 0.6 broadcast_in_dim.8
  56.7 3.9 %all-to-all-start.3 = ((f32[16,1,256]{2,1,0:T(1,128)}), f32[16,1,256]{2,1,0:T(1,128)S(1)}, u32[]{:S(2)}, u32[]{:S(2)}) async-start(f32[16,1,256]{2,1,0:T(1,128)} %broadcast_in_dim.8), calls=%async_computation.3 | async-start | bytes 32768 | tf_op jit(solution)/shard_map/all_to_all | solution.py:9
  60.7 14.1 %all-gather.4.cloned.1.call-done = bf16[4096,1152]{1,0:T(8,128)(2,1)} async-done(((bf16[256,1152]{1,0:T(8,128)(2,1)}), bf16[4096,1152]{1,0:T(8,128)(2,1)}) %all-gather.4.cloned.1.call-update) | async-done | bytes 9437200 | tf_op jit(solution)/shard_map/all_gather | solution.py:24
  74.8 2.4 fusion.25
  77.2 1.3 broadcast_in_dim.6
  78.5 6.6 %all-to-all-start = ((bf16[16,192,256]{2,1,0:T(8,128)(2,1)}), bf16[16,192,256]{2,1,0:T(8,128)(2,1)}, u32[]{:S(2)}, u32[]{:S(2)}) async-start(bf16[16,192,256]{2,1,0:T(8,128)(2,1)} %broadcast_in_dim.6), calls=%async_computation | async-start | bytes 3145728 | tf_op jit(solution)/shard_map/all_to_all | solution.py:9
  85.1 0.1 and.40
  85.2 0.1 eq.42
  85.3 24.4 %all-to-all-done = bf16[16,192,256]{2,1,0:T(8,128)(2,1)} async-done(((bf16[16,192,256]{2,1,0:T(8,128)(2,1)}), bf16[16,192,256]{2,1,0:T(8,128)(2,1)}, u32[]{:S(2)}, u32[]{:S(2)}) %all-to-all-start) | async-done | bytes 1572896 | tf_op jit(solution)/shard_map/all_to_all | solution.py:9
  109.7 1.6 copy.27
  111.3 2.5 fusion.10
  113.8 0.1 all_to_all.24
  113.9 12.9 %all_to_all.30 = bf16[16,1,192]{2,1,0:T(2,128)(2,1)S(1)} all-to-all(bf16[16,1,192]{2,1,0:T(2,128)(2,1)S(1)} %all_to_all.24), channel_id=1, replica_groups=mesh['dp'=16,'mp'=16] {'dp'}, dimensions={0} | all-to-all | bytes 12288 | tf_op jit(solution)/shard_map/all_to_all | solution.py:57
  126.8 3.9 %all-to-all-start.1 = ((bf16[16,192,256]{2,1,0:T(8,128)(2,1)}), bf16[16,192,256]{2,1,0:T(8,128)(2,1)S(1)}, u32[]{:S(2)}, u32[]{:S(2)}) async-start(bf16[16,192,256]{2,1,0:T(8,128)(2,1)} %all-to-all-done), calls=%async_computation.1 | async-start | bytes 3145728 | tf_op jit(solution)/shard_map/all_to_all | solution.py:44
  130.7 0.0 all-gather.8.cloned.1.call-start
  130.8 5.8 %fusion = f32[192,896]{1,0:T(8,128)} fusion(bf16[192,4096]{1,0:T(8,128)(2,1)S(1)} %bitcast.23, bf16[4096,1152]{1,0:T(8,128)(2,1)} %all-gather.4.cloned.1.call-done), kind=kOutput, calls=%fused_computation | convolution fusion | flops 1409286144 | bytes 9601024 | tf_op jit(solution)/shard_map/dot_general | solution.py:60
  136.6 32.7 %all-to-all-done.1 = bf16[16,192,256]{2,1,0:T(8,128)(2,1)S(1)} async-done(((bf16[16,192,256]{2,1,0:T(8,128)(2,1)}), bf16[16,192,256]{2,1,0:T(8,128)(2,1)S(1)}, u32[]{:S(2)}, u32[]{:S(2)}) %all-to-all-start.1) | async-done | bytes 1572896 | tf_op jit(solution)/shard_map/all_to_all | solution.py:44
  169.3 5.9 %multiply_convert_fusion = (bf16[192,896]{1,0:T(8,128)(2,1)}, bf16[192,896]{1,0:T(8,128)(2,1)S(1)}, bf16[192,896]{1,0:T(8,128)(2,1)S(1)}) fusion(f32[192,896]{1,0:T(8,128)} %fusion, f32[192]{0:T(256)S(1)} %convert_reduce_fusion, bf16[192,896]{1,0:T(8,128)(2,1)S(1)} %copy-done.5, bf16[192,4096]{1,0:T(8,128)(2,1)S(1)} %bitcast.24, ...), kind=kOutput, calls=%fused_computation.24 | convolution fusion | flops 1412382720 | bytes 10978048 | tf_op jit(solution)/shard_map/dot_general | solution.py:62
  175.2 0.9 pad_maximum_fusion
  176.1 62.9 %all-gather.8.cloned.1.call-done = bf16[3072,1792]{1,0:T(8,128)(2,1)} async-done(((bf16[192,1792]{1,0:T(8,128)(2,1)}), bf16[3072,1792]{1,0:T(8,128)(2,1)}) %all-gather.8.cloned.1.call-update) | async-done | bytes 11010064 | tf_op jit(solution)/shard_map/all_gather | solution.py:69
  238.9 5.3 %fusion.20 = bf16[256,896]{1,0:T(8,128)(2,1)} fusion(bf16[3072,256]{1,0:T(8,128)(2,1)S(1)} %bitcast.21, bf16[3072,1792]{1,0:T(8,128)(2,1)} %all-gather.8.cloned.1.call-done), kind=kOutput, calls=%fused_computation.18 | convolution fusion | flops 1409515520 | bytes 7536640 | tf_op jit(solution)/shard_map/dot_general | solution.py:74
  244.2 0.6 copy-done.3
  244.8 2.6 %fusion.17 = bf16[256,896]{1,0:T(8,128)(2,1)} fusion(bf16[3072,256]{1,0:T(8,128)(2,1)S(1)} %bitcast.22, bf16[3072,1792]{1,0:T(8,128)(2,1)S(1)} %copy-done.3), kind=kOutput, calls=%fused_computation.17 | convolution fusion | flops 1409515520 | bytes 7536640 | tf_op jit(solution)/shard_map/dot_general | solution.py:71
  (28 shorter events, 0.3 us)
Async XLA Ops:
  7.2 67.6 %all-gather.4.cloned.1.call-start = ((), (), s32[]{:S(2)}) async-start(), calls=%async_computation.5 | async-start | bytes 10027008 | tf_op jit(solution)/shard_map/all_gather | solution.py:24
  9.2 127.4 %all-gather.6.cloned.1.call-start = ((), (), s32[]{:S(2)}) async-start(), calls=%async_computation.6 | async-start | bytes 7798784 | tf_op jit(solution)/shard_map/all_gather | solution.py:26
  10.9 9.2 %copy-start = (s32[16,192]{1,0:T(8,128)S(1)}, s32[16,192]{1,0:T(8,128)}, u32[]{:S(2)}) copy-start(s32[16,192]{1,0:T(8,128)} %param.13) | copy-start | bytes 36868
  10.9 9.2 %copy-start.2 = (s32[16]{0:T(128)S(1)}, s32[16]{0:T(128)}, u32[]{:S(2)}) copy-start(s32[16]{0:T(128)} %param.14) | copy-start | bytes 196
  12.5 38.5 %all-to-all-start.2 = ((bf16[16,256,256]{1,2,0:T(8,128)(2,1)}), bf16[16,256,256]{1,2,0:T(8,128)(2,1)S(1)}, u32[]{:S(2)}, u32[]{:S(2)}) async-start(bf16[16,256,256]{1,2,0:T(8,128)(2,1)} %broadcast_in_dim.7), calls=%async_computation.2 | async-start | bytes 4194304 | tf_op jit(solution)/shard_map/all_to_all | solution.py:9
  51.0 3.7 %copy-start.4 = (bf16[4096,512]{1,0:T(8,128)(2,1)S(1)}, bf16[4096,512]{1,0:T(8,128)(2,1)}, u32[]{:S(2)}) copy-start(bf16[4096,512]{1,0:T(8,128)(2,1)} %param.11) | copy-start | bytes 12582916
  51.0 3.7 %copy-start.6 = (f32[512]{0:T(512)S(1)}, f32[512]{0:T(512)}, u32[]{:S(2)}) copy-start(f32[512]{0:T(512)} %param.12) | copy-start | bytes 6148
  56.7 20.5 %all-to-all-start.3 = ((f32[16,1,256]{2,1,0:T(1,128)}), f32[16,1,256]{2,1,0:T(1,128)S(1)}, u32[]{:S(2)}, u32[]{:S(2)}) async-start(f32[16,1,256]{2,1,0:T(1,128)} %broadcast_in_dim.8), calls=%async_computation.3 | async-start | bytes 32768 | tf_op jit(solution)/shard_map/all_to_all | solution.py:9
  78.5 31.2 %all-to-all-start = ((bf16[16,192,256]{2,1,0:T(8,128)(2,1)}), bf16[16,192,256]{2,1,0:T(8,128)(2,1)}, u32[]{:S(2)}, u32[]{:S(2)}) async-start(bf16[16,192,256]{2,1,0:T(8,128)(2,1)} %broadcast_in_dim.6), calls=%async_computation | async-start | bytes 3145728 | tf_op jit(solution)/shard_map/all_to_all | solution.py:9
  85.3 41.5 %copy-start.1 = (f32[256]{0:T(256)}, f32[256]{0:T(256)S(1)}, u32[]{:S(2)}) copy-start(f32[256]{0:T(256)S(1)} %add_divide_fusion.1) | copy-start | bytes 3076
  126.8 42.5 %all-to-all-start.1 = ((bf16[16,192,256]{2,1,0:T(8,128)(2,1)}), bf16[16,192,256]{2,1,0:T(8,128)(2,1)S(1)}, u32[]{:S(2)}, u32[]{:S(2)}) async-start(bf16[16,192,256]{2,1,0:T(8,128)(2,1)} %all-to-all-done), calls=%async_computation.1 | async-start | bytes 3145728 | tf_op jit(solution)/shard_map/all_to_all | solution.py:44
  130.7 38.6 %copy-start.5 = (bf16[192,896]{1,0:T(8,128)(2,1)S(1)}, bf16[192,896]{1,0:T(8,128)(2,1)}, u32[]{:S(2)}) copy-start(bf16[192,896]{1,0:T(8,128)(2,1)} %param.17) | copy-start | bytes 1032196
  130.7 108.2 %all-gather.8.cloned.1.call-start = ((), (), s32[]{:S(2)}) async-start(), calls=%async_computation.7 | async-start | bytes 11698176 | tf_op jit(solution)/shard_map/all_gather | solution.py:69
  238.9 5.9 %copy-start.3 = (bf16[3072,1792]{1,0:T(8,128)(2,1)S(1)}, bf16[3072,1792]{1,0:T(8,128)(2,1)}, u32[]{:S(2)}) copy-start(bf16[3072,1792]{1,0:T(8,128)(2,1)} %all-gather.8.cloned.1.call-done) | copy-start | bytes 33030148
Sparse Core Ops, SparseCore 0:
  9.8 64.9 all-gather.3
  76.6 49.5 all-gather.5
  176.2 62.6 all-gather.7

commit v9 on v7

--- a/solution.py
+++ b/solution.py
@@ -64,7 +64,8 @@
     d_up = (back * gate * sig).astype(jnp.bfloat16)
     d_gate = (back * up * sig * (1.0 + gate * (1.0 - sig))).astype(jnp.bfloat16)
     contract_rows = (((0,), (0,)), ((), ()))
-    both_d = lax.all_gather(jnp.concatenate([d_gate, d_up], axis=1), "dp", axis=0, tiled=True)
+    d_both, row_slices = lax.optimization_barrier((jnp.concatenate([d_gate, d_up], axis=1), row_slices))
+    both_d = lax.all_gather(d_both, "dp", axis=0, tiled=True)
     incoming = (both_d[:, :ff], both_d[:, ff:])
     grad_g = lax.dot_general(
         row_slices, incoming[0], contract_rows, preferred_element_type=jnp.float32

time: 244 us -> 241 us (0.988)
  blocking collectives: 58.2 us -> 25.6 us
  waiting for transfers between devices: 106 us -> 133 us
    all_to_all x1, blocking collectives: 58.2 us -> 25.6 us  [gather_by_a2a(): lax.all_to_all(jnp.broadcast_to(x[None], (parts,) + x.shape), axis_name,...]
    all_gather x1, waiting for transfers between devices: 37.3 us -> 66.8 us  [on_device(): both_d = lax.all_gather(d_both, 'dp', axis=0, tiled=True)]
    all_to_all x3 -> x2, waiting for transfers between devices: 61.9 us -> 37.1 us  [gather_by_a2a(): lax.all_to_all(jnp.broadcast_to(x[None], (parts,) + x.shape), axis_name,...]
    all_to_all x0 -> x1, waiting for transfers between devices: none -> 23.9 us  [on_device(): lax.all_to_all(row_blocks, 'dp', split_axis=0, concat_axis=0, tiled=True)]
    all_to_all x0 -> x1, starting transfers between devices: none -> 5.04 us  [on_device(): lax.all_to_all(row_blocks, 'dp', split_axis=0, concat_axis=0, tiled=True)]
    all_to_all x3 -> x2, starting transfers between devices: 15.2 us -> 11.5 us  [gather_by_a2a(): lax.all_to_all(jnp.broadcast_to(x[None], (parts,) + x.shape), axis_name,...]
    dot_general x1, matrix products: 5.3 us -> 2.59 us  [on_device(): lax.dot_general(row_slices, incoming[0], contract_rows, preferred_element...]
    dot_general x1, matrix products: 2.59 us -> 5.3 us  [on_device(): lax.dot_general(row_slices, incoming[1], contract_rows, preferred_element...]
  transfers between devices with their start and end apart: 7 -> 7, of which waited for: 6 -> 5; matrix products, arithmetic and copies ran while one was open for 9% -> 12% of each run, Pallas kernels for 0% -> 0%
where the time goes in v9:
time: 241 us; the launch traced here: 240 us
  waiting for transfers between devices  133 us (55%)
  matrix products  29.6 us (12%)
  starting transfers between devices  27.6 us (11%)
  blocking collectives  25.6 us (11%)
  between operations  13.9 us (6%)
  local copies, waits for them, and re-layouts  6.43 us (3%)
  other arithmetic  3.57 us (1%)
    all_gather x1, waiting for transfers between devices, on_device(): both_d = lax.all_gather(d_both, 'dp', axis=0, tiled=True)  66.8 us
    all_to_all x2, waiting for transfers between devices, gather_by_a2a(): lax.all_to_all(jnp.broadcast_to(x[None], (parts,) + x.shape), axis_name,...  37.1 us
    all_to_all x1, blocking collectives, gather_by_a2a(): lax.all_to_all(jnp.broadcast_to(x[None], (parts,) + x.shape), axis_name,...  25.6 us
    all_to_all x1, waiting for transfers between devices, on_device(): lax.all_to_all(row_blocks, 'dp', split_axis=0, concat_axis=0, tiled=True)  23.9 us
    all_to_all x2, starting transfers between devices, gather_by_a2a(): lax.all_to_all(jnp.broadcast_to(x[None], (parts,) + x.shape), axis_name,...  11.5 us
    all_to_all x1, starting transfers between devices, on_device(): lax.all_to_all(picked_weight, 'dp', split_axis=0, concat_axis=0, tiled=True)  10.9 us
    dot_general x1, matrix products, on_device(): up = jnp.dot(row_x, full_w[1], preferred_element_type=jnp.float32)  5.92 us
    dot_general x1, matrix products, on_device(): gate = jnp.dot(row_x, full_w[0], preferred_element_type=jnp.float32)  5.9 us
  transfers between devices with their start and end apart: 7, of which 5 were waited for; matrix products, arithmetic and copies ran while one was open for 12% of the time, Pallas kernels for 0%

profile of v9, /device:TPU:1, one launch (start us, length us, event | category | flops | bytes accessed | tf_op | source)
XLA Modules:
  0.0 240.2 jit_solution(6282792678826723846)
XLA Ops:
  7.2 1.9 pad_maximum_fusion.1
  9.2 0.7 all-gather.6.cloned.1.call-update
  9.9 1.0 copy.22
  10.9 1.5 broadcast_in_dim.6
  12.5 7.6 %all-to-all-start = ((bf16[16,256,256]{1,2,0:T(8,128)(2,1)}), bf16[16,256,256]{1,2,0:T(8,128)(2,1)S(1)}, u32[]{:S(2)}, u32[]{:S(2)}) async-start(bf16[16,256,256]{1,2,0:T(8,128)(2,1)} %broadcast_in_dim.6), calls=%async_computation | async-start | bytes 4194304 | tf_op jit(solution)/shard_map/all_to_all | solution.py:9
  20.1 0.1 fusion.32
  20.2 30.8 %all-to-all-done = bf16[16,256,256]{1,2,0:T(8,128)(2,1)S(1)} async-done(((bf16[16,256,256]{1,2,0:T(8,128)(2,1)}), bf16[16,256,256]{1,2,0:T(8,128)(2,1)S(1)}, u32[]{:S(2)}, u32[]{:S(2)}) %all-to-all-start) | async-done | bytes 2097184 | tf_op jit(solution)/shard_map/all_to_all | solution.py:9
  51.0 3.7 %fusion.35 = f32[256,512]{1,0:T(8,128)S(1)} fusion(bf16[256,4096]{0,1:T(8,128)(2,1)S(1)} %bitcast.19, bf16[4096,512]{1,0:T(8,128)(2,1)} %param.10), kind=kOutput, calls=%fused_computation.46 | convolution fusion | flops 1073741824 | bytes 6815744 | tf_op jit(solution)/shard_map/dot_general | solution.py:48
  54.7 1.4 fusion.24
  56.1 0.6 broadcast_in_dim.7
  56.7 3.9 %all-to-all-start.1 = ((f32[16,1,256]{2,1,0:T(1,128)}), f32[16,1,256]{2,1,0:T(1,128)S(1)}, u32[]{:S(2)}, u32[]{:S(2)}) async-start(f32[16,1,256]{2,1,0:T(1,128)} %broadcast_in_dim.7), calls=%async_computation.1 | async-start | bytes 32768 | tf_op jit(solution)/shard_map/all_to_all | solution.py:9
  60.7 0.1 and.37
  60.8 0.1 eq.38
  60.9 6.2 %all-to-all-done.1 = f32[16,1,256]{2,1,0:T(1,128)S(1)} async-done(((f32[16,1,256]{2,1,0:T(1,128)}), f32[16,1,256]{2,1,0:T(1,128)S(1)}, u32[]{:S(2)}, u32[]{:S(2)}) %all-to-all-start.1) | async-done | bytes 16416 | tf_op jit(solution)/shard_map/all_to_all | solution.py:9
  67.2 0.6 fusion.34
  67.7 2.5 %fusion.10 = f32[1,3072]{1,0:T(1,128)S(1)} fusion(bf16[256,1]{0,1:T(2,128)(2,1)S(1)} %reshape.45, s32[3072]{0:T(1024)S(1)} %eq.38, pred[3072]{0:T(1024)(128)(4,1)S(1)} %and.37), kind=kOutput, calls=%fused_computation.11 | convolution fusion | flops 3145728 | bytes 28160 | tf_op jit(solution)/shard_map/dot_general | solution.py:53
  70.2 0.7 all_to_all.24
  70.9 10.9 %all-to-all-start.2 = ((bf16[16,1,192]{2,1,0:T(2,128)(2,1)}), bf16[16,1,192]{2,1,0:T(2,128)(2,1)S(1)}, u32[]{:S(2)}, u32[]{:S(2)}) async-start(bf16[16,1,192]{2,1,0:T(2,128)(2,1)} %all_to_all.24), calls=%async_computation.2 | async-start | bytes 32768 | tf_op jit(solution)/shard_map/all_to_all | solution.py:56
  81.9 2.4 fusion.25
  84.3 4.9 %all-to-all-done.2 = bf16[16,1,192]{2,1,0:T(2,128)(2,1)S(1)} async-done(((bf16[16,1,192]{2,1,0:T(2,128)(2,1)}), bf16[16,1,192]{2,1,0:T(2,128)(2,1)S(1)}, u32[]{:S(2)}, u32[]{:S(2)}) %all-to-all-start.2) | async-done | bytes 6176 | tf_op jit(solution)/shard_map/all_to_all | solution.py:56
  89.2 0.1 broadcast_in_dim.8
  89.4 25.6 %all_to_all.30 = bf16[16,192,256]{2,1,0:T(8,128)(2,1)} all-to-all(bf16[16,192,256]{2,1,0:T(8,128)(2,1)S(1)} %broadcast_in_dim.8), channel_id=1, replica_groups=mesh['dp'=16,'mp'=16] {'mp'}, dimensions={0} | all-to-all | bytes 3145728 | tf_op jit(solution)/shard_map/all_to_all | solution.py:9
  115.0 5.0 %all-to-all-start.4 = ((bf16[16,192,256]{2,1,0:T(8,128)(2,1)}), bf16[16,192,256]{2,1,0:T(8,128)(2,1)S(1)}, u32[]{:S(2)}, u32[]{:S(2)}) async-start(bf16[16,192,256]{2,1,0:T(8,128)(2,1)} %all_to_all.30), calls=%async_computation.4 | async-start | bytes 3145728 | tf_op jit(solution)/shard_map/all_to_all | solution.py:44
  120.1 1.6 copy.27
  121.7 5.9 %fusion = f32[192,896]{1,0:T(8,128)} fusion(bf16[192,4096]{1,0:T(8,128)(2,1)S(1)} %bitcast.23, bf16[4096,1152]{1,0:T(8,128)(2,1)} %all-gather.4.cloned.1.call-done), kind=kOutput, calls=%fused_computation | convolution fusion | flops 1409286144 | bytes 9601024 | tf_op jit(solution)/shard_map/dot_general | solution.py:59
  127.6 5.9 %multiply_convert_fusion = (bf16[192,896]{1,0:T(8,128)(2,1)}, bf16[192,896]{1,0:T(8,128)(2,1)S(1)}, bf16[192,896]{1,0:T(8,128)(2,1)S(1)}) fusion(f32[192,896]{1,0:T(8,128)} %fusion, f32[192]{0:T(256)S(1)} %convert_reduce_fusion, bf16[192,896]{1,0:T(8,128)(2,1)S(1)} %copy-done.4, bf16[192,4096]{1,0:T(8,128)(2,1)S(1)} %bitcast.24, ...), kind=kOutput, calls=%fused_computation.24 | convolution fusion | flops 1412382720 | bytes 10978048 | tf_op jit(solution)/shard_map/dot_general | solution.py:60
  133.5 0.9 pad_maximum_fusion
  134.4 23.9 %all-to-all-done.4 = bf16[16,192,256]{2,1,0:T(8,128)(2,1)S(1)} async-done(((bf16[16,192,256]{2,1,0:T(8,128)(2,1)}), bf16[16,192,256]{2,1,0:T(8,128)(2,1)S(1)}, u32[]{:S(2)}, u32[]{:S(2)}) %all-to-all-start.4) | async-done | bytes 1572896 | tf_op jit(solution)/shard_map/all_to_all | solution.py:44
  158.3 66.8 %all-gather.8.cloned.1.call-done = bf16[3072,1792]{1,0:T(8,128)(2,1)} async-done(((bf16[192,1792]{1,0:T(8,128)(2,1)}), bf16[3072,1792]{1,0:T(8,128)(2,1)}) %all-gather.8.cloned.1.call-update) | async-done | bytes 11010064 | tf_op jit(solution)/shard_map/all_gather | solution.py:68
  225.1 5.3 %fusion.20 = bf16[256,896]{1,0:T(8,128)(2,1)} fusion(bf16[3072,256]{1,0:T(8,128)(2,1)S(1)} %bitcast.21, bf16[3072,1792]{1,0:T(8,128)(2,1)} %all-gather.8.cloned.1.call-done), kind=kOutput, calls=%fused_computation.18 | convolution fusion | flops 1409515520 | bytes 7536640 | tf_op jit(solution)/shard_map/dot_general | solution.py:73
  230.4 0.6 copy-done.2
  231.0 2.6 %fusion.17 = bf16[256,896]{1,0:T(8,128)(2,1)} fusion(bf16[3072,256]{1,0:T(8,128)(2,1)S(1)} %bitcast.22, bf16[3072,1792]{1,0:T(8,128)(2,1)S(1)} %copy-done.2), kind=kOutput, calls=%fused_computation.17 | convolution fusion | flops 1409515520 | bytes 7536640 | tf_op jit(solution)/shard_map/dot_general | solution.py:70
  (25 shorter events, 0.3 us)
Async XLA Ops:
  7.2 74.7 %all-gather.4.cloned.1.call-start = ((), (), s32[]{:S(2)}) async-start(), calls=%async_computation.5 | async-start | bytes 10027008 | tf_op jit(solution)/shard_map/all_gather | solution.py:24
  9.2 118.4 %all-gather.6.cloned.1.call-start = ((), (), s32[]{:S(2)}) async-start(), calls=%async_computation.6 | async-start | bytes 7798784 | tf_op jit(solution)/shard_map/all_gather | solution.py:26
  10.9 9.2 %copy-start = (s32[16,192]{1,0:T(8,128)S(1)}, s32[16,192]{1,0:T(8,128)}, u32[]{:S(2)}) copy-start(s32[16,192]{1,0:T(8,128)} %param.13) | copy-start | bytes 36868
  10.9 9.2 %copy-start.1 = (s32[16]{0:T(128)S(1)}, s32[16]{0:T(128)}, u32[]{:S(2)}) copy-start(s32[16]{0:T(128)} %param.14) | copy-start | bytes 196
  12.5 38.5 %all-to-all-start = ((bf16[16,256,256]{1,2,0:T(8,128)(2,1)}), bf16[16,256,256]{1,2,0:T(8,128)(2,1)S(1)}, u32[]{:S(2)}, u32[]{:S(2)}) async-start(bf16[16,256,256]{1,2,0:T(8,128)(2,1)} %broadcast_in_dim.6), calls=%async_computation | async-start | bytes 4194304 | tf_op jit(solution)/shard_map/all_to_all | solution.py:9
  51.0 3.7 %copy-start.3 = (bf16[4096,512]{1,0:T(8,128)(2,1)S(1)}, bf16[4096,512]{1,0:T(8,128)(2,1)}, u32[]{:S(2)}) copy-start(bf16[4096,512]{1,0:T(8,128)(2,1)} %param.11) | copy-start | bytes 12582916
  51.0 3.7 %copy-start.5 = (f32[512]{0:T(512)S(1)}, f32[512]{0:T(512)}, u32[]{:S(2)}) copy-start(f32[512]{0:T(512)} %param.12) | copy-start | bytes 6148
  56.7 10.4 %all-to-all-start.1 = ((f32[16,1,256]{2,1,0:T(1,128)}), f32[16,1,256]{2,1,0:T(1,128)S(1)}, u32[]{:S(2)}, u32[]{:S(2)}) async-start(f32[16,1,256]{2,1,0:T(1,128)} %broadcast_in_dim.7), calls=%async_computation.1 | async-start | bytes 32768 | tf_op jit(solution)/shard_map/all_to_all | solution.py:9
  70.9 18.3 %all-to-all-start.2 = ((bf16[16,1,192]{2,1,0:T(2,128)(2,1)}), bf16[16,1,192]{2,1,0:T(2,128)(2,1)S(1)}, u32[]{:S(2)}, u32[]{:S(2)}) async-start(bf16[16,1,192]{2,1,0:T(2,128)(2,1)} %all_to_all.24), calls=%async_computation.2 | async-start | bytes 32768 | tf_op jit(solution)/shard_map/all_to_all | solution.py:56
  115.0 43.4 %all-to-all-start.4 = ((bf16[16,192,256]{2,1,0:T(8,128)(2,1)}), bf16[16,192,256]{2,1,0:T(8,128)(2,1)S(1)}, u32[]{:S(2)}, u32[]{:S(2)}) async-start(bf16[16,192,256]{2,1,0:T(8,128)(2,1)} %all_to_all.30), calls=%async_computation.4 | async-start | bytes 3145728 | tf_op jit(solution)/shard_map/all_to_all | solution.py:44
  120.0 105.1 %all-gather.8.cloned.1.call-start = ((), (), s32[]{:S(2)}) async-start(), calls=%async_computation.7 | async-start | bytes 11698176 | tf_op jit(solution)/shard_map/all_gather | solution.py:68
  121.7 5.9 %copy-start.4 = (bf16[192,896]{1,0:T(8,128)(2,1)S(1)}, bf16[192,896]{1,0:T(8,128)(2,1)}, u32[]{:S(2)}) copy-start(bf16[192,896]{1,0:T(8,128)(2,1)} %param.17) | copy-start | bytes 1032196
  225.1 5.9 %copy-start.2 = (bf16[3072,1792]{1,0:T(8,128)(2,1)S(1)}, bf16[3072,1792]{1,0:T(8,128)(2,1)}, u32[]{:S(2)}) copy-start(bf16[3072,1792]{1,0:T(8,128)(2,1)} %all-gather.8.cloned.1.call-done) | copy-start | bytes 33030148
Sparse Core Ops, SparseCore 0:
  9.8 64.9 all-gather.3
  76.6 49.6 all-gather.5
  158.5 66.6 all-gather.7

commit v10 on v9

--- a/solution.py
+++ b/solution.py
@@ -39,10 +39,18 @@
     ).astype(jnp.bfloat16)
     row_slab = jnp.dot(own_onehot, all_cands, preferred_element_type=jnp.float32).astype(jnp.bfloat16)
     row_x = gather_by_a2a(row_slab, "mp", 1)
-    parts = lax.psum(1, "dp")
-    row_blocks = row_x.reshape(row_x.shape[0], parts, -1).transpose(1, 0, 2)
-    row_slices = lax.all_to_all(row_blocks, "dp", split_axis=0, concat_axis=0, tiled=True)
-    row_slices = row_slices.reshape(-1, row_blocks.shape[2])
+    dp_size = lax.psum(1, "dp")
+    mp_size = lax.psum(1, "mp")
+    all_onehot = (
+        (chosen.reshape(-1)[:, None] == jnp.arange(all_cands.shape[0], dtype=jnp.int32)[None, :])
+        & valid.reshape(-1)[:, None]
+    ).astype(jnp.bfloat16)
+    own_slices = jnp.dot(all_onehot, all_cands, preferred_element_type=jnp.float32).astype(jnp.bfloat16)
+    swap = [
+        (a * mp_size + b, b * mp_size + a) for a in range(dp_size) for b in range(mp_size) if a != b
+    ]
+    swapped = lax.ppermute(own_slices, ("dp", "mp"), swap)
+    row_slices = jnp.where(own_index == lax.axis_index("mp"), own_slices, swapped)
 
     incoming = gather_by_a2a(candidates, "mp", 1)
     hold_g = jnp.dot(incoming, hold_gate, preferred_element_type=jnp.float32)

time: 241 us -> 343 us (1.42)
  waiting for transfers between devices: 133 us -> 245 us
  blocking collectives: 25.6 us -> 0 us
  matrix products: 29.6 us -> 40.9 us
    all_gather x1, waiting for transfers between devices: 0.01 us -> 105 us  [on_device(): full_w = (merged[:, width:], lax.all_gather(up_w, 'dp', axis=0, tiled=True))]
    all_to_all x1 -> x0, blocking collectives: 25.6 us -> none  [gather_by_a2a(): lax.all_to_all(jnp.broadcast_to(x[None], (parts,) + x.shape), axis_name,...]
    all_to_all x1 -> x0, waiting for transfers between devices: 23.9 us -> none  [on_device(): lax.all_to_all(row_blocks, 'dp', split_axis=0, concat_axis=0, tiled=True)]
    all_gather x1, waiting for transfers between devices: 66.8 us -> 79.2 us  [on_device(): both_d = lax.all_gather(d_both, 'dp', axis=0, tiled=True)]
    dot_general x0 -> x1, matrix products: none -> 12 us  [on_device(): jnp.dot(all_onehot, all_cands, preferred_element_type=jnp.float32)]
    all_to_all x2 -> x3, waiting for transfers between devices: 37.1 us -> 46.2 us  [gather_by_a2a(): lax.all_to_all(jnp.broadcast_to(x[None], (parts,) + x.shape), axis_name,...]
    ppermute x0 -> x1, waiting for transfers between devices: none -> 7.4 us  [on_device(): swapped = lax.ppermute(own_slices, ('dp', 'mp'), swap)]
    all_to_all x1 -> x0, starting transfers between devices: 5.04 us -> none  [on_device(): lax.all_to_all(row_blocks, 'dp', split_axis=0, concat_axis=0, tiled=True)]
  transfers between devices with their start and end apart: 7 -> 8, of which waited for: 5 -> 7; matrix products, arithmetic and copies ran while one was open for 12% -> 12% of each run, Pallas kernels for 0% -> 0%
where the time goes in v10:
time: 343 us
  waiting for transfers between devices  245 us (71%)
  matrix products  40.9 us (12%)
  starting transfers between devices  30.2 us (9%)
  between operations  13.9 us (4%)
  local copies, waits for them, and re-layouts  7.47 us (2%)
  other arithmetic  5.13 us (1%)
    all_gather x1, waiting for transfers between devices, on_device(): full_w = (merged[:, width:], lax.all_gather(up_w, 'dp', axis=0, tiled=True))  105 us
    all_gather x1, waiting for transfers between devices, on_device(): both_d = lax.all_gather(d_both, 'dp', axis=0, tiled=True)  79.2 us
    all_to_all x3, waiting for transfers between devices, gather_by_a2a(): lax.all_to_all(jnp.broadcast_to(x[None], (parts,) + x.shape), axis_name,...  46.2 us
    all_to_all x3, starting transfers between devices, gather_by_a2a(): lax.all_to_all(jnp.broadcast_to(x[None], (parts,) + x.shape), axis_name,...  15.3 us
    dot_general x1, matrix products, on_device(): jnp.dot(all_onehot, all_cands, preferred_element_type=jnp.float32)  12 us
    all_to_all x1, starting transfers between devices, on_device(): lax.all_to_all(picked_weight, 'dp', split_axis=0, concat_axis=0, tiled=True)  10.9 us
    ppermute x1, waiting for transfers between devices, on_device(): swapped = lax.ppermute(own_slices, ('dp', 'mp'), swap)  7.4 us
    all_to_all x1, waiting for transfers between devices, on_device(): lax.all_to_all(picked_weight, 'dp', split_axis=0, concat_axis=0, tiled=True)  7.14 us
  transfers between devices with their start and end apart: 8, of which 7 were waited for; matrix products, arithmetic and copies ran while one was open for 12% of the time, Pallas kernels for 0%

profile of v10, /device:TPU:1, one launch (start us, length us, event | category | flops | bytes accessed | tf_op | source)
XLA Modules:
  0.0 342.9 jit_solution(3183762719844605361)
XLA Ops:
  7.2 1.9 pad_maximum_fusion.1
  9.2 0.7 all-gather.6.cloned.1.call-update
  9.9 1.0 copy.20
  10.9 1.5 broadcast_in_dim.6
  12.5 7.6 %all-to-all-start = ((bf16[16,256,256]{1,2,0:T(8,128)(2,1)}), bf16[16,256,256]{1,2,0:T(8,128)(2,1)S(1)}, u32[]{:S(2)}, u32[]{:S(2)}) async-start(bf16[16,256,256]{1,2,0:T(8,128)(2,1)} %broadcast_in_dim.6), calls=%async_computation | async-start | bytes 4194304 | tf_op jit(solution)/shard_map/all_to_all | solution.py:9
  20.1 30.9 %all-to-all-done = bf16[16,256,256]{1,2,0:T(8,128)(2,1)S(1)} async-done(((bf16[16,256,256]{1,2,0:T(8,128)(2,1)}), bf16[16,256,256]{1,2,0:T(8,128)(2,1)S(1)}, u32[]{:S(2)}, u32[]{:S(2)}) %all-to-all-start) | async-done | bytes 2097184 | tf_op jit(solution)/shard_map/all_to_all | solution.py:9
  51.0 3.6 %fusion.44 = f32[256,512]{1,0:T(8,128)S(1)} fusion(bf16[256,4096]{0,1:T(8,128)(2,1)S(1)} %bitcast.19, bf16[4096,512]{1,0:T(8,128)(2,1)} %param.10), kind=kOutput, calls=%fused_computation.54 | convolution fusion | flops 1073741824 | bytes 6815744 | tf_op jit(solution)/shard_map/dot_general | solution.py:56
  54.7 1.4 fusion.33
  56.0 0.6 broadcast_in_dim.7
  56.7 4.0 %all-to-all-start.1 = ((f32[16,1,256]{2,1,0:T(1,128)}), f32[16,1,256]{2,1,0:T(1,128)S(1)}, u32[]{:S(2)}, u32[]{:S(2)}) async-start(f32[16,1,256]{2,1,0:T(1,128)} %broadcast_in_dim.7), calls=%async_computation.1 | async-start | bytes 32768 | tf_op jit(solution)/shard_map/all_to_all | solution.py:9
  60.9 6.2 %all-to-all-done.1 = f32[16,1,256]{2,1,0:T(1,128)S(1)} async-done(((f32[16,1,256]{2,1,0:T(1,128)}), f32[16,1,256]{2,1,0:T(1,128)S(1)}, u32[]{:S(2)}, u32[]{:S(2)}) %all-to-all-start.1) | async-done | bytes 16416 | tf_op jit(solution)/shard_map/all_to_all | solution.py:9
  67.7 2.5 fusion.18
  70.2 0.7 all_to_all.20
  70.9 10.9 %all-to-all-start.2 = ((bf16[16,1,192]{2,1,0:T(2,128)(2,1)}), bf16[16,1,192]{2,1,0:T(2,128)(2,1)S(1)}, u32[]{:S(2)}, u32[]{:S(2)}) async-start(bf16[16,1,192]{2,1,0:T(2,128)(2,1)} %all_to_all.20), calls=%async_computation.2 | async-start | bytes 32768 | tf_op jit(solution)/shard_map/all_to_all | solution.py:64
  82.1 7.1 %all-to-all-done.2 = bf16[16,1,192]{2,1,0:T(2,128)(2,1)S(1)} async-done(((bf16[16,1,192]{2,1,0:T(2,128)(2,1)}), bf16[16,1,192]{2,1,0:T(2,128)(2,1)S(1)}, u32[]{:S(2)}, u32[]{:S(2)}) %all-to-all-start.2) | async-done | bytes 6176 | tf_op jit(solution)/shard_map/all_to_all | solution.py:64
  89.3 2.4 fusion.34
  91.6 1.3 broadcast_in_dim.8
  92.9 3.7 %all-to-all-start.3 = ((bf16[16,192,256]{2,1,0:T(8,128)(2,1)}), bf16[16,192,256]{2,1,0:T(8,128)(2,1)S(1)}, u32[]{:S(2)}, u32[]{:S(2)}) async-start(bf16[16,192,256]{2,1,0:T(8,128)(2,1)} %broadcast_in_dim.8), calls=%async_computation.3 | async-start | bytes 3145728 | tf_op jit(solution)/shard_map/all_to_all | solution.py:9
  96.7 12.0 %fusion.11 = bf16[3072,256]{1,0:T(8,128)(2,1)S(1)} fusion(s32[3072]{0:T(1024)S(1)} %eq.67, pred[3072]{0:T(1024)(128)(4,1)S(1)} %lt.37, bf16[4096,1152]{1,0:T(8,128)(2,1)} %all-gather.4.cloned.1.call-done), kind=kOutput, calls=%fused_computation.11 | convolution fusion | flops 6468403200 | bytes 3685376 | tf_op jit(solution)/shard_map/dot_general | solution.py:48
  108.7 3.8 %collective-permute-start = (bf16[3072,256]{1,0:T(8,128)(2,1)S(1)}, bf16[3072,256]{1,0:T(8,128)(2,1)}, u32[]{:S(2)}, u32[]{:S(2)}) collective-permute-start(bf16[3072,256]{1,0:T(8,128)(2,1)S(1)} %fusion.11), channel_id=1, source_target_pairs={{1,16},{2,32},{3,48},{4,64},{5,80},{6,96},{7,112},{8,128},{9,144},... | collective-permute-start | bytes 4718600 | tf_op jit(solution)/shard_map/ppermute | solution.py:52
  112.6 9.1 %all-to-all-done.3 = bf16[16,192,256]{2,1,0:T(8,128)(2,1)S(1)} async-done(((bf16[16,192,256]{2,1,0:T(8,128)(2,1)}), bf16[16,192,256]{2,1,0:T(8,128)(2,1)S(1)}, u32[]{:S(2)}, u32[]{:S(2)}) %all-to-all-start.3) | async-done | bytes 1572896 | tf_op jit(solution)/shard_map/all_to_all | solution.py:9
  121.9 1.1 copy-done
  123.0 4.9 %fusion.5 = f32[192,896]{1,0:T(8,128)S(1)} fusion(bf16[192,4096]{1,0:T(8,128)(2,1)S(1)} %bitcast.21, bf16[4096,1152]{1,0:T(8,128)(2,1)} %all-gather.4.cloned.1.call-done), kind=kOutput, calls=%fused_computation.5 | convolution fusion | flops 1409286144 | bytes 9601024 | tf_op jit(solution)/shard_map/dot_general | solution.py:67
  128.0 104.5 %all-gather.6.cloned.1.call-done = bf16[4096,896]{1,0:T(8,128)(2,1)} async-done(((bf16[256,896]{1,0:T(8,128)(2,1)}), bf16[4096,896]{1,0:T(8,128)(2,1)}) %all-gather.6.cloned.1.call-update) | async-done | bytes 7340048 | tf_op jit(solution)/shard_map/all_gather | solution.py:26
  232.5 6.2 %multiply_convert_fusion = (bf16[192,896]{1,0:T(8,128)(2,1)}, bf16[192,896]{1,0:T(8,128)(2,1)S(1)}, bf16[192,896]{1,0:T(8,128)(2,1)S(1)}) fusion(f32[192,896]{1,0:T(8,128)S(1)} %fusion.5, f32[192]{0:T(256)S(1)} %convert_reduce_fusion, bf16[192,896]{1,0:T(8,128)(2,1)S(1)} %copy-done.5, bf16[192,4096]{1,0:T(8,128)(2,1)} %bitcast.22, ...), kind=kOutput, calls=%fused_computation.32 | convolution fusion | flops 1412382720 | bytes 10978048 | tf_op jit(solution)/shard_map/dot_general | solution.py:68
  238.7 0.9 pad_maximum_fusion
  239.6 7.4 %collective-permute-done = bf16[3072,256]{1,0:T(8,128)(2,1)} collective-permute-done((bf16[3072,256]{1,0:T(8,128)(2,1)S(1)}, bf16[3072,256]{1,0:T(8,128)(2,1)}, u32[]{:S(2)}, u32[]{:S(2)}) %collective-permute-start) | collective-permute-done | bytes 1572896 | tf_op jit(solution)/shard_map/ppermute | solution.py:52
  247.0 1.6 broadcast_select_fusion
  248.6 79.2 %all-gather.8.cloned.1.call-done = bf16[3072,1792]{1,0:T(8,128)(2,1)} async-done(((bf16[192,1792]{1,0:T(8,128)(2,1)}), bf16[3072,1792]{1,0:T(8,128)(2,1)}) %all-gather.8.cloned.1.call-update) | async-done | bytes 11010064 | tf_op jit(solution)/shard_map/all_gather | solution.py:76
  327.9 5.3 %fusion.29 = bf16[256,896]{1,0:T(8,128)(2,1)} fusion(bf16[3072,256]{1,0:T(8,128)(2,1)S(1)} %broadcast_select_fusion, bf16[3072,1792]{1,0:T(8,128)(2,1)} %all-gather.8.cloned.1.call-done), kind=kOutput, calls=%fused_computation.26 | convolution fusion | flops 1409515520 | bytes 7536640 | tf_op jit(solution)/shard_map/dot_general | solution.py:81
  333.2 0.6 copy-done.3
  333.8 2.6 fusion.26
  (32 shorter events, 1.5 us)
Async XLA Ops:
  7.2 82.1 %all-gather.4.cloned.1.call-start = ((), (), s32[]{:S(2)}) async-start(), calls=%async_computation.4 | async-start | bytes 10027008 | tf_op jit(solution)/shard_map/all_gather | solution.py:24
  9.1 223.4 %all-gather.6.cloned.1.call-start = ((), (), s32[]{:S(2)}) async-start(), calls=%async_computation.5 | async-start | bytes 7798784 | tf_op jit(solution)/shard_map/all_gather | solution.py:26
  10.9 9.1 %copy-start.1 = (s32[16,192]{1,0:T(8,128)S(1)}, s32[16,192]{1,0:T(8,128)}, u32[]{:S(2)}) copy-start(s32[16,192]{1,0:T(8,128)} %param.13) | copy-start | bytes 36868
  12.5 38.5 %all-to-all-start = ((bf16[16,256,256]{1,2,0:T(8,128)(2,1)}), bf16[16,256,256]{1,2,0:T(8,128)(2,1)S(1)}, u32[]{:S(2)}, u32[]{:S(2)}) async-start(bf16[16,256,256]{1,2,0:T(8,128)(2,1)} %broadcast_in_dim.6), calls=%async_computation | async-start | bytes 4194304 | tf_op jit(solution)/shard_map/all_to_all | solution.py:9
  51.0 3.6 %copy-start.4 = (bf16[4096,512]{1,0:T(8,128)(2,1)S(1)}, bf16[4096,512]{1,0:T(8,128)(2,1)}, u32[]{:S(2)}) copy-start(bf16[4096,512]{1,0:T(8,128)(2,1)} %param.11) | copy-start | bytes 12582916
  51.0 3.7 %copy-start.6 = (f32[512]{0:T(512)S(1)}, f32[512]{0:T(512)}, u32[]{:S(2)}) copy-start(f32[512]{0:T(512)} %param.12) | copy-start | bytes 6148
  54.7 6.0 %copy-start.2 = (s32[16]{0:T(128)S(1)}, s32[16]{0:T(128)}, u32[]{:S(2)}) copy-start(s32[16]{0:T(128)} %param.14) | copy-start | bytes 196
  56.7 10.4 %all-to-all-start.1 = ((f32[16,1,256]{2,1,0:T(1,128)}), f32[16,1,256]{2,1,0:T(1,128)S(1)}, u32[]{:S(2)}, u32[]{:S(2)}) async-start(f32[16,1,256]{2,1,0:T(1,128)} %broadcast_in_dim.7), calls=%async_computation.1 | async-start | bytes 32768 | tf_op jit(solution)/shard_map/all_to_all | solution.py:9
  70.9 18.3 %all-to-all-start.2 = ((bf16[16,1,192]{2,1,0:T(2,128)(2,1)}), bf16[16,1,192]{2,1,0:T(2,128)(2,1)S(1)}, u32[]{:S(2)}, u32[]{:S(2)}) async-start(bf16[16,1,192]{2,1,0:T(2,128)(2,1)} %all_to_all.20), calls=%async_computation.2 | async-start | bytes 32768 | tf_op jit(solution)/shard_map/all_to_all | solution.py:64
  92.9 28.8 %all-to-all-start.3 = ((bf16[16,192,256]{2,1,0:T(8,128)(2,1)}), bf16[16,192,256]{2,1,0:T(8,128)(2,1)S(1)}, u32[]{:S(2)}, u32[]{:S(2)}) async-start(bf16[16,192,256]{2,1,0:T(8,128)(2,1)} %broadcast_in_dim.8), calls=%async_computation.3 | async-start | bytes 3145728 | tf_op jit(solution)/shard_map/all_to_all | solution.py:9
  96.7 231.2 %all-gather.8.cloned.1.call-start = ((), (), s32[]{:S(2)}) async-start(), calls=%async_computation.6 | async-start | bytes 11698176 | tf_op jit(solution)/shard_map/all_gather | solution.py:76
  108.7 138.3 %collective-permute-start = (bf16[3072,256]{1,0:T(8,128)(2,1)S(1)}, bf16[3072,256]{1,0:T(8,128)(2,1)}, u32[]{:S(2)}, u32[]{:S(2)}) collective-permute-start(bf16[3072,256]{1,0:T(8,128)(2,1)S(1)} %fusion.11), channel_id=1, source_target_pairs={{1,16},{2,32},{3,48},{4,64},{5,80},{6,96},{7,112},{8,128},{9,144},... | collective-permute-start | bytes 4718600 | tf_op jit(solution)/shard_map/ppermute | solution.py:52
  121.9 1.2 copy-start
  123.0 109.5 %copy-start.5 = (bf16[192,896]{1,0:T(8,128)(2,1)S(1)}, bf16[192,896]{1,0:T(8,128)(2,1)}, u32[]{:S(2)}) copy-start(bf16[192,896]{1,0:T(8,128)(2,1)} %param.17) | copy-start | bytes 1032196
  327.9 5.9 %copy-start.3 = (bf16[3072,1792]{1,0:T(8,128)(2,1)S(1)}, bf16[3072,1792]{1,0:T(8,128)(2,1)}, u32[]{:S(2)}) copy-start(bf16[3072,1792]{1,0:T(8,128)(2,1)} %all-gather.8.cloned.1.call-done) | copy-start | bytes 33030148
Sparse Core Ops, SparseCore 0:
  9.8 64.9 all-gather.3
  76.6 155.8 all-gather.5
  248.8 79.0 all-gather.7

commit v11 on v7

--- a/solution.py
+++ b/solution.py
@@ -64,8 +64,9 @@
     d_up = (back * gate * sig).astype(jnp.bfloat16)
     d_gate = (back * up * sig * (1.0 + gate * (1.0 - sig))).astype(jnp.bfloat16)
     contract_rows = (((0,), (0,)), ((), ()))
-    both_d = lax.all_gather(jnp.concatenate([d_gate, d_up], axis=1), "dp", axis=0, tiled=True)
-    incoming = (both_d[:, :ff], both_d[:, ff:])
+    d_both, row_slices = lax.optimization_barrier((jnp.stack([d_gate, d_up]), row_slices))
+    both_d = lax.all_gather(d_both, "dp", axis=1, tiled=True)
+    incoming = (both_d[0], both_d[1])
     grad_g = lax.dot_general(
         row_slices, incoming[0], contract_rows, preferred_element_type=jnp.float32
     )

time: 244 us -> 241 us (0.988)
  blocking collectives: 58.2 us -> 25.6 us
  waiting for transfers between devices: 106 us -> 133 us
    all_to_all x1, blocking collectives: 58.2 us -> 25.6 us  [gather_by_a2a(): lax.all_to_all(jnp.broadcast_to(x[None], (parts,) + x.shape), axis_name,...]
    all_gather x1, waiting for transfers between devices: 37.3 us -> 66.8 us  [on_device(): both_d = lax.all_gather(d_both, 'dp', axis=1, tiled=True)]
    all_to_all x3 -> x2, waiting for transfers between devices: 61.9 us -> 37.1 us  [gather_by_a2a(): lax.all_to_all(jnp.broadcast_to(x[None], (parts,) + x.shape), axis_name,...]
    all_to_all x0 -> x1, waiting for transfers between devices: none -> 23.9 us  [on_device(): lax.all_to_all(row_blocks, 'dp', split_axis=0, concat_axis=0, tiled=True)]
    all_to_all x0 -> x1, starting transfers between devices: none -> 5.04 us  [on_device(): lax.all_to_all(row_blocks, 'dp', split_axis=0, concat_axis=0, tiled=True)]
    all_to_all x3 -> x2, starting transfers between devices: 15.2 us -> 11.5 us  [gather_by_a2a(): lax.all_to_all(jnp.broadcast_to(x[None], (parts,) + x.shape), axis_name,...]
    dot_general x1, matrix products: 2.59 us -> 5.3 us  [on_device(): lax.dot_general(row_slices, incoming[1], contract_rows, preferred_element...]
    dot_general x1, matrix products: 5.3 us -> 2.6 us  [on_device(): lax.dot_general(row_slices, incoming[0], contract_rows, preferred_element...]
  transfers between devices with their start and end apart: 7 -> 7, of which waited for: 6 -> 5; matrix products, arithmetic and copies ran while one was open for 9% -> 12% of each run, Pallas kernels for 0% -> 0%
where the time goes in v11:
time: 241 us; the launch traced here: 240 us
  waiting for transfers between devices  133 us (55%)
  matrix products  29.6 us (12%)
  starting transfers between devices  27.6 us (11%)
  blocking collectives  25.6 us (11%)
  between operations  13.9 us (6%)
  local copies, waits for them, and re-layouts  6.43 us (3%)
  other arithmetic  3.59 us (1%)
    all_gather x1, waiting for transfers between devices, on_device(): both_d = lax.all_gather(d_both, 'dp', axis=1, tiled=True)  66.8 us
    all_to_all x2, waiting for transfers between devices, gather_by_a2a(): lax.all_to_all(jnp.broadcast_to(x[None], (parts,) + x.shape), axis_name,...  37.1 us
    all_to_all x1, blocking collectives, gather_by_a2a(): lax.all_to_all(jnp.broadcast_to(x[None], (parts,) + x.shape), axis_name,...  25.6 us
    all_to_all x1, waiting for transfers between devices, on_device(): lax.all_to_all(row_blocks, 'dp', split_axis=0, concat_axis=0, tiled=True)  23.9 us
    all_to_all x2, starting transfers between devices, gather_by_a2a(): lax.all_to_all(jnp.broadcast_to(x[None], (parts,) + x.shape), axis_name,...  11.5 us
    all_to_all x1, starting transfers between devices, on_device(): lax.all_to_all(picked_weight, 'dp', split_axis=0, concat_axis=0, tiled=True)  10.9 us
    dot_general x1, matrix products, on_device(): up = jnp.dot(row_x, full_w[1], preferred_element_type=jnp.float32)  5.92 us
    dot_general x1, matrix products, on_device(): gate = jnp.dot(row_x, full_w[0], preferred_element_type=jnp.float32)  5.9 us
  transfers between devices with their start and end apart: 7, of which 5 were waited for; matrix products, arithmetic and copies ran while one was open for 12% of the time, Pallas kernels for 0%

profile of v11, /device:TPU:1, one launch (start us, length us, event | category | flops | bytes accessed | tf_op | source)
XLA Modules:
  0.0 240.2 jit_solution(18442236209411644168)
XLA Ops:
  7.2 1.9 pad_maximum_fusion.1
  9.2 0.7 all-gather.6.cloned.1.call-update
  9.9 1.0 copy.22
  10.9 1.5 broadcast_in_dim.6
  12.5 7.6 %all-to-all-start = ((bf16[16,256,256]{1,2,0:T(8,128)(2,1)}), bf16[16,256,256]{1,2,0:T(8,128)(2,1)S(1)}, u32[]{:S(2)}, u32[]{:S(2)}) async-start(bf16[16,256,256]{1,2,0:T(8,128)(2,1)} %broadcast_in_dim.6), calls=%async_computation | async-start | bytes 4194304 | tf_op jit(solution)/shard_map/all_to_all | solution.py:9
  20.1 0.1 fusion.28
  20.2 30.8 %all-to-all-done = bf16[16,256,256]{1,2,0:T(8,128)(2,1)S(1)} async-done(((bf16[16,256,256]{1,2,0:T(8,128)(2,1)}), bf16[16,256,256]{1,2,0:T(8,128)(2,1)S(1)}, u32[]{:S(2)}, u32[]{:S(2)}) %all-to-all-start) | async-done | bytes 2097184 | tf_op jit(solution)/shard_map/all_to_all | solution.py:9
  51.0 3.7 %fusion.31 = f32[256,512]{1,0:T(8,128)S(1)} fusion(bf16[256,4096]{0,1:T(8,128)(2,1)S(1)} %bitcast.33, bf16[4096,512]{1,0:T(8,128)(2,1)} %param.10), kind=kOutput, calls=%fused_computation.48 | convolution fusion | flops 1073741824 | bytes 6815744 | tf_op jit(solution)/shard_map/dot_general | solution.py:48
  54.7 1.4 fusion.18
  56.1 0.6 broadcast_in_dim.7
  56.7 3.9 %all-to-all-start.1 = ((f32[16,1,256]{2,1,0:T(1,128)}), f32[16,1,256]{2,1,0:T(1,128)S(1)}, u32[]{:S(2)}, u32[]{:S(2)}) async-start(f32[16,1,256]{2,1,0:T(1,128)} %broadcast_in_dim.7), calls=%async_computation.1 | async-start | bytes 32768 | tf_op jit(solution)/shard_map/all_to_all | solution.py:9
  60.7 0.1 and.37
  60.8 0.1 eq.38
  60.9 6.2 %all-to-all-done.1 = f32[16,1,256]{2,1,0:T(1,128)S(1)} async-done(((f32[16,1,256]{2,1,0:T(1,128)}), f32[16,1,256]{2,1,0:T(1,128)S(1)}, u32[]{:S(2)}, u32[]{:S(2)}) %all-to-all-start.1) | async-done | bytes 16416 | tf_op jit(solution)/shard_map/all_to_all | solution.py:9
  67.2 0.6 fusion.30
  67.7 2.5 %fusion.8 = f32[1,3072]{1,0:T(1,128)S(1)} fusion(bf16[256,1]{0,1:T(2,128)(2,1)S(1)} %reshape.45, s32[3072]{0:T(1024)S(1)} %eq.38, pred[3072]{0:T(1024)(128)(4,1)S(1)} %and.37), kind=kOutput, calls=%fused_computation.11 | convolution fusion | flops 3145728 | bytes 28160 | tf_op jit(solution)/shard_map/dot_general | solution.py:53
  70.2 0.7 all_to_all.24
  70.9 10.9 %all-to-all-start.2 = ((bf16[16,1,192]{2,1,0:T(2,128)(2,1)}), bf16[16,1,192]{2,1,0:T(2,128)(2,1)S(1)}, u32[]{:S(2)}, u32[]{:S(2)}) async-start(bf16[16,1,192]{2,1,0:T(2,128)(2,1)} %all_to_all.24), calls=%async_computation.2 | async-start | bytes 32768 | tf_op jit(solution)/shard_map/all_to_all | solution.py:56
  81.9 2.4 fusion.19
  84.3 4.9 %all-to-all-done.2 = bf16[16,1,192]{2,1,0:T(2,128)(2,1)S(1)} async-done(((bf16[16,1,192]{2,1,0:T(2,128)(2,1)}), bf16[16,1,192]{2,1,0:T(2,128)(2,1)S(1)}, u32[]{:S(2)}, u32[]{:S(2)}) %all-to-all-start.2) | async-done | bytes 6176 | tf_op jit(solution)/shard_map/all_to_all | solution.py:56
  89.2 0.1 broadcast_in_dim.8
  89.4 25.6 %all_to_all.30 = bf16[16,192,256]{2,1,0:T(8,128)(2,1)} all-to-all(bf16[16,192,256]{2,1,0:T(8,128)(2,1)S(1)} %broadcast_in_dim.8), channel_id=1, replica_groups=mesh['dp'=16,'mp'=16] {'mp'}, dimensions={0} | all-to-all | bytes 3145728 | tf_op jit(solution)/shard_map/all_to_all | solution.py:9
  115.0 5.0 %all-to-all-start.4 = ((bf16[16,192,256]{2,1,0:T(8,128)(2,1)}), bf16[16,192,256]{2,1,0:T(8,128)(2,1)S(1)}, u32[]{:S(2)}, u32[]{:S(2)}) async-start(bf16[16,192,256]{2,1,0:T(8,128)(2,1)} %all_to_all.30), calls=%async_computation.4 | async-start | bytes 3145728 | tf_op jit(solution)/shard_map/all_to_all | solution.py:44
  120.1 1.6 copy.27
  121.7 5.9 %fusion = f32[192,896]{1,0:T(8,128)} fusion(bf16[192,4096]{1,0:T(8,128)(2,1)S(1)} %bitcast.37, bf16[4096,1152]{1,0:T(8,128)(2,1)} %all-gather.4.cloned.1.call-done), kind=kOutput, calls=%fused_computation | convolution fusion | flops 1409286144 | bytes 9601024 | tf_op jit(solution)/shard_map/dot_general | solution.py:59
  127.6 5.9 %multiply_convert_fusion = (bf16[192,896]{1,0:T(8,128)(2,1)}, bf16[1,192,896]{2,1,0:T(8,128)(2,1)S(1)}, bf16[1,192,896]{2,1,0:T(8,128)(2,1)S(1)}) fusion(f32[192,896]{1,0:T(8,128)} %fusion, f32[192]{0:T(256)S(1)} %convert_reduce_fusion, bf16[192,896]{1,0:T(8,128)(2,1)S(1)} %copy-done.4, bf16[192,4096]{1,0:T(8,128)(2,1)S(1)} %bitcast.38, ...), kind=kOutput, calls=%fused_computation.24 | convolution fusion | flops 1412382720 | bytes 10978048 | tf_op jit(solution)/shard_map/dot_general | solution.py:60
  133.5 0.9 pad_maximum_fusion
  134.4 23.9 %all-to-all-done.4 = bf16[16,192,256]{2,1,0:T(8,128)(2,1)S(1)} async-done(((bf16[16,192,256]{2,1,0:T(8,128)(2,1)}), bf16[16,192,256]{2,1,0:T(8,128)(2,1)S(1)}, u32[]{:S(2)}, u32[]{:S(2)}) %all-to-all-start.4) | async-done | bytes 1572896 | tf_op jit(solution)/shard_map/all_to_all | solution.py:44
  158.3 66.8 %all-gather.8.cloned.1.call-done = bf16[2,3072,896]{2,1,0:T(8,128)(2,1)} async-done(((bf16[2,192,896]{2,1,0:T(8,128)(2,1)}), bf16[2,3072,896]{2,1,0:T(8,128)(2,1)}) %all-gather.8.cloned.1.call-update) | async-done | bytes 11010064 | tf_op jit(solution)/shard_map/all_gather | solution.py:68
  225.1 5.3 %fusion.16 = bf16[256,896]{1,0:T(8,128)(2,1)} fusion(bf16[3072,256]{1,0:T(8,128)(2,1)S(1)} %bitcast.35, bf16[2,3072,896]{2,1,0:T(8,128)(2,1)} %all-gather.8.cloned.1.call-done), kind=kOutput, calls=%fused_computation.18 | convolution fusion | flops 1409515520 | bytes 7536640 | tf_op jit(solution)/shard_map/dot_general | solution.py:73
  230.4 0.6 copy-done.2
  231.0 2.6 %fusion.15 = bf16[256,896]{1,0:T(8,128)(2,1)} fusion(bf16[3072,256]{1,0:T(8,128)(2,1)S(1)} %bitcast.36, bf16[2,3072,896]{2,1,0:T(8,128)(2,1)S(1)} %copy-done.2), kind=kOutput, calls=%fused_computation.17 | convolution fusion | flops 1409515520 | bytes 7536640 | tf_op jit(solution)/shard_map/dot_general | solution.py:70
  (25 shorter events, 0.3 us)
Async XLA Ops:
  7.2 74.7 %all-gather.4.cloned.1.call-start = ((), (), s32[]{:S(2)}) async-start(), calls=%async_computation.5 | async-start | bytes 10027008 | tf_op jit(solution)/shard_map/all_gather | solution.py:24
  9.2 118.4 %all-gather.6.cloned.1.call-start = ((), (), s32[]{:S(2)}) async-start(), calls=%async_computation.6 | async-start | bytes 7798784 | tf_op jit(solution)/shard_map/all_gather | solution.py:26
  10.9 9.2 %copy-start = (s32[16,192]{1,0:T(8,128)S(1)}, s32[16,192]{1,0:T(8,128)}, u32[]{:S(2)}) copy-start(s32[16,192]{1,0:T(8,128)} %param.13) | copy-start | bytes 36868
  10.9 9.2 %copy-start.1 = (s32[16]{0:T(128)S(1)}, s32[16]{0:T(128)}, u32[]{:S(2)}) copy-start(s32[16]{0:T(128)} %param.14) | copy-start | bytes 196
  12.5 38.5 %all-to-all-start = ((bf16[16,256,256]{1,2,0:T(8,128)(2,1)}), bf16[16,256,256]{1,2,0:T(8,128)(2,1)S(1)}, u32[]{:S(2)}, u32[]{:S(2)}) async-start(bf16[16,256,256]{1,2,0:T(8,128)(2,1)} %broadcast_in_dim.6), calls=%async_computation | async-start | bytes 4194304 | tf_op jit(solution)/shard_map/all_to_all | solution.py:9
  51.0 3.7 %copy-start.3 = (bf16[4096,512]{1,0:T(8,128)(2,1)S(1)}, bf16[4096,512]{1,0:T(8,128)(2,1)}, u32[]{:S(2)}) copy-start(bf16[4096,512]{1,0:T(8,128)(2,1)} %param.11) | copy-start | bytes 12582916
  51.0 3.7 %copy-start.5 = (f32[512]{0:T(512)S(1)}, f32[512]{0:T(512)}, u32[]{:S(2)}) copy-start(f32[512]{0:T(512)} %param.12) | copy-start | bytes 6148
  56.7 10.4 %all-to-all-start.1 = ((f32[16,1,256]{2,1,0:T(1,128)}), f32[16,1,256]{2,1,0:T(1,128)S(1)}, u32[]{:S(2)}, u32[]{:S(2)}) async-start(f32[16,1,256]{2,1,0:T(1,128)} %broadcast_in_dim.7), calls=%async_computation.1 | async-start | bytes 32768 | tf_op jit(solution)/shard_map/all_to_all | solution.py:9
  70.9 18.3 %all-to-all-start.2 = ((bf16[16,1,192]{2,1,0:T(2,128)(2,1)}), bf16[16,1,192]{2,1,0:T(2,128)(2,1)S(1)}, u32[]{:S(2)}, u32[]{:S(2)}) async-start(bf16[16,1,192]{2,1,0:T(2,128)(2,1)} %all_to_all.24), calls=%async_computation.2 | async-start | bytes 32768 | tf_op jit(solution)/shard_map/all_to_all | solution.py:56
  115.0 43.4 %all-to-all-start.4 = ((bf16[16,192,256]{2,1,0:T(8,128)(2,1)}), bf16[16,192,256]{2,1,0:T(8,128)(2,1)S(1)}, u32[]{:S(2)}, u32[]{:S(2)}) async-start(bf16[16,192,256]{2,1,0:T(8,128)(2,1)} %all_to_all.30), calls=%async_computation.4 | async-start | bytes 3145728 | tf_op jit(solution)/shard_map/all_to_all | solution.py:44
  120.0 105.1 %all-gather.8.cloned.1.call-start = ((), (), s32[]{:S(2)}) async-start(), calls=%async_computation.7 | async-start | bytes 11698176 | tf_op jit(solution)/shard_map/all_gather | solution.py:68
  121.7 5.9 %copy-start.4 = (bf16[192,896]{1,0:T(8,128)(2,1)S(1)}, bf16[192,896]{1,0:T(8,128)(2,1)}, u32[]{:S(2)}) copy-start(bf16[192,896]{1,0:T(8,128)(2,1)} %param.17) | copy-start | bytes 1032196
  225.1 5.9 %copy-start.2 = (bf16[2,3072,896]{2,1,0:T(8,128)(2,1)S(1)}, bf16[2,3072,896]{2,1,0:T(8,128)(2,1)}, u32[]{:S(2)}) copy-start(bf16[2,3072,896]{2,1,0:T(8,128)(2,1)} %all-gather.8.cloned.1.call-done) | copy-start | bytes 33030148
Sparse Core Ops, SparseCore 0:
  9.8 64.9 all-gather.3
  76.6 49.6 all-gather.5
  158.5 66.6 all-gather.7

commit v12 on v9

--- a/solution.py
+++ b/solution.py
@@ -21,9 +21,11 @@
     slots = chosen.shape[1]
     width = candidates.shape[1]
     ff = gate_w.shape[1]
-    merged = lax.all_gather(jnp.concatenate([candidates, gate_w], axis=1), "dp", axis=0, tiled=True)
+    split = ff // 2
+    merged = lax.all_gather(jnp.concatenate([candidates, gate_w[:, :split]], axis=1), "dp", axis=0, tiled=True)
+    rest = lax.all_gather(jnp.concatenate([gate_w[:, split:], up_w], axis=1), "dp", axis=0, tiled=True)
     all_cands = merged[:, :width]
-    full_w = (merged[:, width:], lax.all_gather(up_w, "dp", axis=0, tiled=True))
+    full_w = ((merged[:, width:], rest[:, :ff - split]), rest[:, ff - split:])
     own_index = lax.axis_index("dp")
     source = chosen // cand_dev
     local_row = (chosen % cand_dev).reshape(-1)
@@ -56,7 +58,9 @@
     arrived_weight = lax.all_to_all(picked_weight, "dp", split_axis=0, concat_axis=0, tiled=True)
     row_weight = jnp.sum(arrived_weight.astype(jnp.float32), axis=0)
 
-    gate = jnp.dot(row_x, full_w[0], preferred_element_type=jnp.float32)
+    gate = jnp.concatenate(
+        [jnp.dot(row_x, part, preferred_element_type=jnp.float32) for part in full_w[0]], axis=1
+    )
     up = jnp.dot(row_x, full_w[1], preferred_element_type=jnp.float32)
     hidden = (jax.nn.silu(gate) * up).astype(jnp.bfloat16)
     back = cotangent.astype(jnp.float32) * row_weight[:, None]

time: 241 us -> 253 us (1.050)
  waiting for transfers between devices: 133 us -> 141 us
  matrix products: 29.6 us -> 32.6 us
    all_gather x2, waiting for transfers between devices: 0.01 us -> 15.2 us  [the longest x1 15.2 us: on_device(): lax.all_gather(jnp.concatenate([gate_w[:, split:], up_w], axis=1), 'dp',...]
    all_to_all x1, waiting for transfers between devices: 23.9 us -> 9.83 us  [on_device(): lax.all_to_all(row_blocks, 'dp', split_axis=0, concat_axis=0, tiled=True)]
    all_gather x1, waiting for transfers between devices: 66.8 us -> 73.5 us  [on_device(): both_d = lax.all_gather(d_both, 'dp', axis=0, tiled=True)]
    dot_general x1 -> x2, matrix products: 5.9 us -> 7.27 us  [on_device(): jnp.dot(row_x, part, preferred_element_type=jnp.float32)]
  transfers between devices with their start and end apart: 7 -> 7, of which waited for: 5 -> 6; matrix products, arithmetic and copies ran while one was open for 12% -> 13% of each run, Pallas kernels for 0% -> 0%
where the time goes in v12:
time: 253 us
  waiting for transfers between devices  141 us (56%)
  matrix products  32.6 us (13%)
  starting transfers between devices  27.8 us (11%)
  blocking collectives  25.6 us (10%)
  between operations  13.9 us (5%)
  local copies, waits for them, and re-layouts  6.71 us (3%)
  other arithmetic  5.47 us (2%)
    all_gather x1, waiting for transfers between devices, on_device(): both_d = lax.all_gather(d_both, 'dp', axis=0, tiled=True)  73.5 us
    all_to_all x2, waiting for transfers between devices, gather_by_a2a(): lax.all_to_all(jnp.broadcast_to(x[None], (parts,) + x.shape), axis_name,...  37.1 us
    all_to_all x1, blocking collectives, gather_by_a2a(): lax.all_to_all(jnp.broadcast_to(x[None], (parts,) + x.shape), axis_name,...  25.6 us
    all_gather x1, waiting for transfers between devices, on_device(): lax.all_gather(jnp.concatenate([gate_w[:, split:], up_w], axis=1), 'dp',...  15.2 us
    all_to_all x2, starting transfers between devices, gather_by_a2a(): lax.all_to_all(jnp.broadcast_to(x[None], (parts,) + x.shape), axis_name,...  11.5 us
    all_to_all x1, starting transfers between devices, on_device(): lax.all_to_all(picked_weight, 'dp', split_axis=0, concat_axis=0, tiled=True)  10.9 us
    all_to_all x1, waiting for transfers between devices, on_device(): lax.all_to_all(row_blocks, 'dp', split_axis=0, concat_axis=0, tiled=True)  9.83 us
    dot_general x1, matrix products, on_device(): up = jnp.dot(row_x, full_w[1], preferred_element_type=jnp.float32)  7.42 us
  transfers between devices with their start and end apart: 7, of which 6 were waited for; matrix products, arithmetic and copies ran while one was open for 13% of the time, Pallas kernels for 0%

profile of v12, /device:TPU:1, one launch (start us, length us, event | category | flops | bytes accessed | tf_op | source)
XLA Modules:
  0.0 252.8 jit_solution(12523829381281387586)
XLA Ops:
  7.2 1.2 fusion.39
  8.4 1.7 pad_maximum_fusion.3
  10.2 2.1 pad_maximum_fusion
  12.5 1.5 broadcast_in_dim.6
  14.0 7.6 %all-to-all-start = ((bf16[16,256,256]{1,2,0:T(8,128)(2,1)}), bf16[16,256,256]{1,2,0:T(8,128)(2,1)S(1)}, u32[]{:S(2)}, u32[]{:S(2)}) async-start(bf16[16,256,256]{1,2,0:T(8,128)(2,1)} %broadcast_in_dim.6), calls=%async_computation | async-start | bytes 4194304 | tf_op jit(solution)/shard_map/all_to_all | solution.py:9
  21.7 30.8 %all-to-all-done = bf16[16,256,256]{1,2,0:T(8,128)(2,1)S(1)} async-done(((bf16[16,256,256]{1,2,0:T(8,128)(2,1)}), bf16[16,256,256]{1,2,0:T(8,128)(2,1)S(1)}, u32[]{:S(2)}, u32[]{:S(2)}) %all-to-all-start) | async-done | bytes 2097184 | tf_op jit(solution)/shard_map/all_to_all | solution.py:9
  52.6 3.7 %fusion.40 = f32[256,512]{1,0:T(8,128)S(1)} fusion(bf16[256,4096]{0,1:T(8,128)(2,1)S(1)} %bitcast.19, bf16[4096,512]{1,0:T(8,128)(2,1)} %param.10), kind=kOutput, calls=%fused_computation.53 | convolution fusion | flops 1073741824 | bytes 6815744 | tf_op jit(solution)/shard_map/dot_general | solution.py:50
  56.3 1.4 fusion.28
  57.6 0.6 broadcast_in_dim.7
  58.3 4.0 %all-to-all-start.1 = ((f32[16,1,256]{2,1,0:T(1,128)}), f32[16,1,256]{2,1,0:T(1,128)S(1)}, u32[]{:S(2)}, u32[]{:S(2)}) async-start(f32[16,1,256]{2,1,0:T(1,128)} %broadcast_in_dim.7), calls=%async_computation.1 | async-start | bytes 32768 | tf_op jit(solution)/shard_map/all_to_all | solution.py:9
  62.4 6.2 %all-to-all-done.1 = f32[16,1,256]{2,1,0:T(1,128)S(1)} async-done(((f32[16,1,256]{2,1,0:T(1,128)}), f32[16,1,256]{2,1,0:T(1,128)S(1)}, u32[]{:S(2)}, u32[]{:S(2)}) %all-to-all-start.1) | async-done | bytes 16416 | tf_op jit(solution)/shard_map/all_to_all | solution.py:9
  68.7 0.6 fusion.38
  69.3 2.5 fusion.14
  71.8 0.7 all_to_all.24
  72.5 10.9 %all-to-all-start.2 = ((bf16[16,1,192]{2,1,0:T(2,128)(2,1)}), bf16[16,1,192]{2,1,0:T(2,128)(2,1)S(1)}, u32[]{:S(2)}, u32[]{:S(2)}) async-start(bf16[16,1,192]{2,1,0:T(2,128)(2,1)} %all_to_all.24), calls=%async_computation.2 | async-start | bytes 32768 | tf_op jit(solution)/shard_map/all_to_all | solution.py:58
  83.4 2.5 fusion.29
  85.9 5.1 %all-to-all-done.2 = bf16[16,1,192]{2,1,0:T(2,128)(2,1)S(1)} async-done(((bf16[16,1,192]{2,1,0:T(2,128)(2,1)}), bf16[16,1,192]{2,1,0:T(2,128)(2,1)S(1)}, u32[]{:S(2)}, u32[]{:S(2)}) %all-to-all-start.2) | async-done | bytes 6176 | tf_op jit(solution)/shard_map/all_to_all | solution.py:58
  91.0 0.1 broadcast_in_dim.8
  91.1 25.6 %all_to_all.30 = bf16[16,192,256]{2,1,0:T(8,128)(2,1)} all-to-all(bf16[16,192,256]{2,1,0:T(8,128)(2,1)S(1)} %broadcast_in_dim.8), channel_id=1, replica_groups=mesh['dp'=16,'mp'=16] {'mp'}, dimensions={0} | all-to-all | bytes 3145728 | tf_op jit(solution)/shard_map/all_to_all | solution.py:9
  116.7 5.1 %all-to-all-start.4 = ((bf16[16,192,256]{2,1,0:T(8,128)(2,1)}), bf16[16,192,256]{2,1,0:T(8,128)(2,1)S(1)}, u32[]{:S(2)}, u32[]{:S(2)}) async-start(bf16[16,192,256]{2,1,0:T(8,128)(2,1)} %all_to_all.30), calls=%async_computation.4 | async-start | bytes 3145728 | tf_op jit(solution)/shard_map/all_to_all | solution.py:46
  121.7 0.2 all-gather.8.cloned.1.call-start
  122.0 1.6 copy.27
  123.6 4.0 %fusion.8 = f32[192,448]{1,0:T(8,128)} fusion(bf16[192,4096]{1,0:T(8,128)(2,1)S(1)} %bitcast.23, bf16[4096,704]{1,0:T(8,128)(2,1)} %all-gather.4.cloned.1.call-done), kind=kOutput, calls=%fused_computation.8 | convolution fusion | flops 704643072 | bytes 6111232 | tf_op jit(solution)/shard_map/dot_general | solution.py:62
  127.6 15.2 %all-gather.6.cloned.1.call-done = bf16[4096,1344]{1,0:T(8,128)(2,1)} async-done(((bf16[256,1344]{1,0:T(8,128)(2,1)}), bf16[4096,1344]{1,0:T(8,128)(2,1)}) %all-gather.6.cloned.1.call-update) | async-done | bytes 11010064 | tf_op jit(solution)/shard_map/all_gather | solution.py:26
  142.8 3.3 %fusion.6 = f32[192,448]{1,0:T(8,128)S(1)} fusion(bf16[192,4096]{1,0:T(8,128)(2,1)S(1)} %bitcast.24, bf16[4096,1344]{1,0:T(8,128)(2,1)} %all-gather.6.cloned.1.call-done), kind=kOutput, calls=%fused_computation.6 | convolution fusion | flops 704643072 | bytes 6111232 | tf_op jit(solution)/shard_map/dot_general | solution.py:62
  146.1 7.4 %multiply_convert_fusion = (bf16[192,896]{1,0:T(8,128)(2,1)}, bf16[192,896]{1,0:T(8,128)(2,1)S(1)}, bf16[192,896]{1,0:T(8,128)(2,1)S(1)}) fusion(f32[192,448]{1,0:T(8,128)S(1)} %fusion.6, f32[192,448]{1,0:T(8,128)S(1)} %copy-done.7, f32[192]{0:T(256)S(1)} %convert_reduce_fusion, bf16[192,896]{1,0:T(8,128)(2,1)S(1)} %copy-done.5, ...), kind=kOutput, calls=%fused_computation.30 | convolution fusion | flops 1412554752 | bytes 10978048 | tf_op jit(solution)/shard_map/dot_general | solution.py:64
  153.5 0.9 pad_maximum_fusion.2
  154.4 9.8 %all-to-all-done.4 = bf16[16,192,256]{2,1,0:T(8,128)(2,1)S(1)} async-done(((bf16[16,192,256]{2,1,0:T(8,128)(2,1)}), bf16[16,192,256]{2,1,0:T(8,128)(2,1)S(1)}, u32[]{:S(2)}, u32[]{:S(2)}) %all-to-all-start.4) | async-done | bytes 1572896 | tf_op jit(solution)/shard_map/all_to_all | solution.py:46
  164.3 73.5 %all-gather.8.cloned.1.call-done = bf16[3072,1792]{1,0:T(8,128)(2,1)} async-done(((bf16[192,1792]{1,0:T(8,128)(2,1)}), bf16[3072,1792]{1,0:T(8,128)(2,1)}) %all-gather.8.cloned.1.call-update) | async-done | bytes 11010064 | tf_op jit(solution)/shard_map/all_gather | solution.py:72
  237.8 5.3 %fusion.24 = bf16[256,896]{1,0:T(8,128)(2,1)} fusion(bf16[3072,256]{1,0:T(8,128)(2,1)S(1)} %bitcast.21, bf16[3072,1792]{1,0:T(8,128)(2,1)} %all-gather.8.cloned.1.call-done), kind=kOutput, calls=%fused_computation.22 | convolution fusion | flops 1409515520 | bytes 7536640 | tf_op jit(solution)/shard_map/dot_general | solution.py:77
  243.1 0.6 copy-done.3
  243.7 2.6 %fusion.21 = bf16[256,896]{1,0:T(8,128)(2,1)} fusion(bf16[3072,256]{1,0:T(8,128)(2,1)S(1)} %bitcast.22, bf16[3072,1792]{1,0:T(8,128)(2,1)S(1)} %copy-done.3), kind=kOutput, calls=%fused_computation.21 | convolution fusion | flops 1409515520 | bytes 7536640 | tf_op jit(solution)/shard_map/dot_general | solution.py:74
  (32 shorter events, 0.6 us)
Async XLA Ops:
  7.2 5.2 %copy-start = (bf16[256,256]{1,0:T(8,128)(2,1)S(1)}, bf16[256,256]{1,0:T(8,128)(2,1)}, u32[]{:S(2)}) copy-start(bf16[256,256]{1,0:T(8,128)(2,1)} %param.9) | copy-start | bytes 393220
  7.2 76.2 %all-gather.4.cloned.1.call-start = ((), (), s32[]{:S(2)}) async-start(), calls=%async_computation.5 | async-start | bytes 6684672 | tf_op jit(solution)/shard_map/all_gather | solution.py:25
  10.1 132.7 %all-gather.6.cloned.1.call-start = ((), (), s32[]{:S(2)}) async-start(), calls=%async_computation.6 | async-start | bytes 12255232 | tf_op jit(solution)/shard_map/all_gather | solution.py:26
  12.5 9.1 %copy-start.1 = (s32[16,192]{1,0:T(8,128)S(1)}, s32[16,192]{1,0:T(8,128)}, u32[]{:S(2)}) copy-start(s32[16,192]{1,0:T(8,128)} %param.13) | copy-start | bytes 36868
  12.5 9.1 %copy-start.2 = (s32[16]{0:T(128)S(1)}, s32[16]{0:T(128)}, u32[]{:S(2)}) copy-start(s32[16]{0:T(128)} %param.14) | copy-start | bytes 196
  14.0 38.5 %all-to-all-start = ((bf16[16,256,256]{1,2,0:T(8,128)(2,1)}), bf16[16,256,256]{1,2,0:T(8,128)(2,1)S(1)}, u32[]{:S(2)}, u32[]{:S(2)}) async-start(bf16[16,256,256]{1,2,0:T(8,128)(2,1)} %broadcast_in_dim.6), calls=%async_computation | async-start | bytes 4194304 | tf_op jit(solution)/shard_map/all_to_all | solution.py:9
  52.6 3.7 %copy-start.4 = (bf16[4096,512]{1,0:T(8,128)(2,1)S(1)}, bf16[4096,512]{1,0:T(8,128)(2,1)}, u32[]{:S(2)}) copy-start(bf16[4096,512]{1,0:T(8,128)(2,1)} %param.11) | copy-start | bytes 12582916
  52.6 3.7 %copy-start.6 = (f32[512]{0:T(512)S(1)}, f32[512]{0:T(512)}, u32[]{:S(2)}) copy-start(f32[512]{0:T(512)} %param.12) | copy-start | bytes 6148
  58.3 10.4 %all-to-all-start.1 = ((f32[16,1,256]{2,1,0:T(1,128)}), f32[16,1,256]{2,1,0:T(1,128)S(1)}, u32[]{:S(2)}, u32[]{:S(2)}) async-start(f32[16,1,256]{2,1,0:T(1,128)} %broadcast_in_dim.7), calls=%async_computation.1 | async-start | bytes 32768 | tf_op jit(solution)/shard_map/all_to_all | solution.py:9
  72.5 18.5 %all-to-all-start.2 = ((bf16[16,1,192]{2,1,0:T(2,128)(2,1)}), bf16[16,1,192]{2,1,0:T(2,128)(2,1)S(1)}, u32[]{:S(2)}, u32[]{:S(2)}) async-start(bf16[16,1,192]{2,1,0:T(2,128)(2,1)} %all_to_all.24), calls=%async_computation.2 | async-start | bytes 32768 | tf_op jit(solution)/shard_map/all_to_all | solution.py:58
  116.7 47.6 %all-to-all-start.4 = ((bf16[16,192,256]{2,1,0:T(8,128)(2,1)}), bf16[16,192,256]{2,1,0:T(8,128)(2,1)S(1)}, u32[]{:S(2)}, u32[]{:S(2)}) async-start(bf16[16,192,256]{2,1,0:T(8,128)(2,1)} %all_to_all.30), calls=%async_computation.4 | async-start | bytes 3145728 | tf_op jit(solution)/shard_map/all_to_all | solution.py:46
  121.7 116.1 %all-gather.8.cloned.1.call-start = ((), (), s32[]{:S(2)}) async-start(), calls=%async_computation.7 | async-start | bytes 11698176 | tf_op jit(solution)/shard_map/all_gather | solution.py:72
  127.6 18.5 %copy-start.5 = (bf16[192,896]{1,0:T(8,128)(2,1)S(1)}, bf16[192,896]{1,0:T(8,128)(2,1)}, u32[]{:S(2)}) copy-start(bf16[192,896]{1,0:T(8,128)(2,1)} %param.17) | copy-start | bytes 1032196
  142.8 3.3 %copy-start.7 = (f32[192,448]{1,0:T(8,128)S(1)}, f32[192,448]{1,0:T(8,128)}, u32[]{:S(2)}) copy-start(f32[192,448]{1,0:T(8,128)} %fusion.8) | copy-start | bytes 1032196
  237.8 5.9 %copy-start.3 = (bf16[3072,1792]{1,0:T(8,128)(2,1)S(1)}, bf16[3072,1792]{1,0:T(8,128)(2,1)}, u32[]{:S(2)}) copy-start(bf16[3072,1792]{1,0:T(8,128)(2,1)} %all-gather.8.cloned.1.call-done) | copy-start | bytes 33030148
Sparse Core Ops, SparseCore 0:
  10.4 50.2 all-gather.3
  62.5 80.2 all-gather.5
  164.4 73.3 all-gather.7

commit v13 on v9

--- a/solution.py
+++ b/solution.py
@@ -66,14 +66,10 @@
     contract_rows = (((0,), (0,)), ((), ()))
     d_both, row_slices = lax.optimization_barrier((jnp.concatenate([d_gate, d_up], axis=1), row_slices))
     both_d = lax.all_gather(d_both, "dp", axis=0, tiled=True)
-    incoming = (both_d[:, :ff], both_d[:, ff:])
-    grad_g = lax.dot_general(
-        row_slices, incoming[0], contract_rows, preferred_element_type=jnp.float32
-    )
-    grad_u = lax.dot_general(
-        row_slices, incoming[1], contract_rows, preferred_element_type=jnp.float32
-    )
-    return (grad_g.astype(jnp.bfloat16), grad_u.astype(jnp.bfloat16), hidden, cand_weight)
+    grads = lax.dot_general(
+        row_slices, both_d, contract_rows, preferred_element_type=jnp.float32
+    ).astype(jnp.bfloat16)
+    return (grads[:, :ff], grads[:, ff:], hidden, cand_weight)
 
 
 def solution(mesh):

time: 241 us -> 240 us (level)
    dot_general x2 -> x1, matrix products: 7.9 us -> 7.17 us  [on_device(): lax.dot_general(row_slices, both_d, contract_rows, preferred_element_type...]
  transfers between devices with their start and end apart: 7 -> 7, of which waited for: 5 -> 6; matrix products, arithmetic and copies ran while one was open for 12% -> 12% of each run, Pallas kernels for 0% -> 0%
where the time goes in v13:
time: 240 us
  waiting for transfers between devices  134 us (56%)
  matrix products  28.9 us (12%)
  starting transfers between devices  27.7 us (12%)
  blocking collectives  25.6 us (11%)
  between operations  13.9 us (6%)
  local copies, waits for them, and re-layouts  5.97 us (2%)
  other arithmetic  3.59 us (1%)
    all_gather x1, waiting for transfers between devices, on_device(): both_d = lax.all_gather(d_both, 'dp', axis=0, tiled=True)  66.9 us
    all_to_all x2, waiting for transfers between devices, gather_by_a2a(): lax.all_to_all(jnp.broadcast_to(x[None], (parts,) + x.shape), axis_name,...  37.1 us
    all_to_all x1, blocking collectives, gather_by_a2a(): lax.all_to_all(jnp.broadcast_to(x[None], (parts,) + x.shape), axis_name,...  25.6 us
    all_to_all x1, waiting for transfers between devices, on_device(): lax.all_to_all(row_blocks, 'dp', split_axis=0, concat_axis=0, tiled=True)  23.4 us
    all_to_all x2, starting transfers between devices, gather_by_a2a(): lax.all_to_all(jnp.broadcast_to(x[None], (parts,) + x.shape), axis_name,...  11.6 us
    all_to_all x1, starting transfers between devices, on_device(): lax.all_to_all(picked_weight, 'dp', split_axis=0, concat_axis=0, tiled=True)  11 us
    dot_general x1, matrix products, on_device(): lax.dot_general(row_slices, both_d, contract_rows, preferred_element_type...  7.17 us
    dot_general x1, matrix products, on_device(): up = jnp.dot(row_x, full_w[1], preferred_element_type=jnp.float32)  5.92 us
  transfers between devices with their start and end apart: 7, of which 6 were waited for; matrix products, arithmetic and copies ran while one was open for 12% of the time, Pallas kernels for 0%

profile of v13, /device:TPU:1, one launch (start us, length us, event | category | flops | bytes accessed | tf_op | source)
XLA Modules:
  0.0 239.8 jit_solution(12118811220462123746)
XLA Ops:
  7.2 1.9 pad_maximum_fusion.1
  9.2 0.7 all-gather.6.cloned.1.call-update
  10.0 0.1 copy.22
  10.1 1.5 broadcast_in_dim.6
  11.6 7.7 %all-to-all-start = ((bf16[16,256,256]{1,2,0:T(8,128)(2,1)}), bf16[16,256,256]{1,2,0:T(8,128)(2,1)S(1)}, u32[]{:S(2)}, u32[]{:S(2)}) async-start(bf16[16,256,256]{1,2,0:T(8,128)(2,1)} %broadcast_in_dim.6), calls=%async_computation | async-start | bytes 4194304 | tf_op jit(solution)/shard_map/all_to_all | solution.py:9
  19.3 0.1 fusion.22
  19.4 30.8 %all-to-all-done = bf16[16,256,256]{1,2,0:T(8,128)(2,1)S(1)} async-done(((bf16[16,256,256]{1,2,0:T(8,128)(2,1)}), bf16[16,256,256]{1,2,0:T(8,128)(2,1)S(1)}, u32[]{:S(2)}, u32[]{:S(2)}) %all-to-all-start) | async-done | bytes 2097184 | tf_op jit(solution)/shard_map/all_to_all | solution.py:9
  50.3 3.7 %fusion.26 = f32[256,512]{1,0:T(8,128)S(1)} fusion(bf16[256,4096]{0,1:T(8,128)(2,1)S(1)} %bitcast.20, bf16[4096,512]{1,0:T(8,128)(2,1)} %param.10), kind=kOutput, calls=%fused_computation.42 | convolution fusion | flops 1073741824 | bytes 6815744 | tf_op jit(solution)/shard_map/dot_general | solution.py:48
  54.0 1.4 fusion.14
  55.4 0.6 broadcast_in_dim.7
  56.0 3.9 %all-to-all-start.1 = ((f32[16,1,256]{2,1,0:T(1,128)}), f32[16,1,256]{2,1,0:T(1,128)S(1)}, u32[]{:S(2)}, u32[]{:S(2)}) async-start(f32[16,1,256]{2,1,0:T(1,128)} %broadcast_in_dim.7), calls=%async_computation.1 | async-start | bytes 32768 | tf_op jit(solution)/shard_map/all_to_all | solution.py:9
  59.9 0.1 and.37
  60.0 0.1 eq.38
  60.1 6.2 %all-to-all-done.1 = f32[16,1,256]{2,1,0:T(1,128)S(1)} async-done(((f32[16,1,256]{2,1,0:T(1,128)}), f32[16,1,256]{2,1,0:T(1,128)S(1)}, u32[]{:S(2)}, u32[]{:S(2)}) %all-to-all-start.1) | async-done | bytes 16416 | tf_op jit(solution)/shard_map/all_to_all | solution.py:9
  66.3 0.6 fusion.24
  66.9 2.5 %fusion.6 = f32[1,3072]{1,0:T(1,128)S(1)} fusion(bf16[256,1]{0,1:T(2,128)(2,1)S(1)} %reshape.45, s32[3072]{0:T(1024)S(1)} %eq.38, pred[3072]{0:T(1024)(128)(4,1)S(1)} %and.37), kind=kOutput, calls=%fused_computation.7 | convolution fusion | flops 3145728 | bytes 28160 | tf_op jit(solution)/shard_map/dot_general | solution.py:53
  69.4 0.7 all_to_all.24
  70.1 11.0 %all-to-all-start.2 = ((bf16[16,1,192]{2,1,0:T(2,128)(2,1)}), bf16[16,1,192]{2,1,0:T(2,128)(2,1)S(1)}, u32[]{:S(2)}, u32[]{:S(2)}) async-start(bf16[16,1,192]{2,1,0:T(2,128)(2,1)} %all_to_all.24), calls=%async_computation.2 | async-start | bytes 32768 | tf_op jit(solution)/shard_map/all_to_all | solution.py:56
  81.2 2.4 fusion.15
  83.5 4.9 %all-to-all-done.2 = bf16[16,1,192]{2,1,0:T(2,128)(2,1)S(1)} async-done(((bf16[16,1,192]{2,1,0:T(2,128)(2,1)}), bf16[16,1,192]{2,1,0:T(2,128)(2,1)S(1)}, u32[]{:S(2)}, u32[]{:S(2)}) %all-to-all-start.2) | async-done | bytes 6176 | tf_op jit(solution)/shard_map/all_to_all | solution.py:56
  88.5 0.1 broadcast_in_dim.8
  88.6 25.6 %all_to_all.30 = bf16[16,192,256]{2,1,0:T(8,128)(2,1)} all-to-all(bf16[16,192,256]{2,1,0:T(8,128)(2,1)S(1)} %broadcast_in_dim.8), channel_id=1, replica_groups=mesh['dp'=16,'mp'=16] {'mp'}, dimensions={0} | all-to-all | bytes 3145728 | tf_op jit(solution)/shard_map/all_to_all | solution.py:9
  114.2 5.0 %all-to-all-start.4 = ((bf16[16,192,256]{2,1,0:T(8,128)(2,1)}), bf16[16,192,256]{2,1,0:T(8,128)(2,1)S(1)}, u32[]{:S(2)}, u32[]{:S(2)}) async-start(bf16[16,192,256]{2,1,0:T(8,128)(2,1)} %all_to_all.30), calls=%async_computation.4 | async-start | bytes 3145728 | tf_op jit(solution)/shard_map/all_to_all | solution.py:44
  119.3 1.6 copy.27
  121.0 5.9 %fusion = f32[192,896]{1,0:T(8,128)} fusion(bf16[192,4096]{1,0:T(8,128)(2,1)S(1)} %bitcast.22, bf16[4096,1152]{1,0:T(8,128)(2,1)} %all-gather.4.cloned.1.call-done), kind=kOutput, calls=%fused_computation | convolution fusion | flops 1409286144 | bytes 9601024 | tf_op jit(solution)/shard_map/dot_general | solution.py:59
  126.9 1.1 all-gather.6.cloned.1.call-done
  128.0 5.9 %multiply_convert_fusion = (bf16[192,896]{1,0:T(8,128)(2,1)}, bf16[192,896]{1,0:T(8,128)(2,1)S(1)}, bf16[192,896]{1,0:T(8,128)(2,1)S(1)}) fusion(f32[192,896]{1,0:T(8,128)} %fusion, f32[192]{0:T(256)S(1)} %convert_reduce_fusion, bf16[192,896]{1,0:T(8,128)(2,1)S(1)} %copy-done.4, bf16[192,4096]{1,0:T(8,128)(2,1)S(1)} %bitcast.23, ...), kind=kOutput, calls=%fused_computation.19 | convolution fusion | flops 1412382720 | bytes 10978048 | tf_op jit(solution)/shard_map/dot_general | solution.py:60
  133.9 0.9 pad_maximum_fusion
  134.8 23.4 %all-to-all-done.4 = bf16[16,192,256]{2,1,0:T(8,128)(2,1)S(1)} async-done(((bf16[16,192,256]{2,1,0:T(8,128)(2,1)}), bf16[16,192,256]{2,1,0:T(8,128)(2,1)S(1)}, u32[]{:S(2)}, u32[]{:S(2)}) %all-to-all-start.4) | async-done | bytes 1572896 | tf_op jit(solution)/shard_map/all_to_all | solution.py:44
  158.3 66.9 %all-gather.8.cloned.1.call-done = bf16[3072,1792]{1,0:T(8,128)(2,1)} async-done(((bf16[192,1792]{1,0:T(8,128)(2,1)}), bf16[3072,1792]{1,0:T(8,128)(2,1)}) %all-gather.8.cloned.1.call-update) | async-done | bytes 11010064 | tf_op jit(solution)/shard_map/all_gather | solution.py:68
  225.1 7.2 %convolution_convert_fusion = bf16[256,1792]{1,0:T(8,128)(2,1)S(1)} fusion(bf16[3072,256]{1,0:T(8,128)(2,1)S(1)} %bitcast.19, bf16[3072,1792]{1,0:T(8,128)(2,1)} %all-gather.8.cloned.1.call-done), kind=kOutput, calls=%fused_computation.8 | convolution fusion | flops 2819031040 | bytes 13500416 | tf_op jit(solution)/shard_map/dot_general | solution.py:69
  232.3 1.0 fusion.25
  (25 shorter events, 0.3 us)
Async XLA Ops:
  7.2 2.8 %copy-start = (bf16[256,256]{1,0:T(8,128)(2,1)S(1)}, bf16[256,256]{1,0:T(8,128)(2,1)}, u32[]{:S(2)}) copy-start(bf16[256,256]{1,0:T(8,128)(2,1)} %param.9) | copy-start | bytes 393220
  7.2 74.0 %all-gather.4.cloned.1.call-start = ((), (), s32[]{:S(2)}) async-start(), calls=%async_computation.5 | async-start | bytes 10027008 | tf_op jit(solution)/shard_map/all_gather | solution.py:24
  9.2 118.8 %all-gather.6.cloned.1.call-start = ((), (), s32[]{:S(2)}) async-start(), calls=%async_computation.6 | async-start | bytes 7798784 | tf_op jit(solution)/shard_map/all_gather | solution.py:26
  11.6 7.7 %copy-start.1 = (s32[16,192]{1,0:T(8,128)S(1)}, s32[16,192]{1,0:T(8,128)}, u32[]{:S(2)}) copy-start(s32[16,192]{1,0:T(8,128)} %param.13) | copy-start | bytes 36868
  11.6 7.7 %copy-start.2 = (s32[16]{0:T(128)S(1)}, s32[16]{0:T(128)}, u32[]{:S(2)}) copy-start(s32[16]{0:T(128)} %param.14) | copy-start | bytes 196
  11.6 38.7 %all-to-all-start = ((bf16[16,256,256]{1,2,0:T(8,128)(2,1)}), bf16[16,256,256]{1,2,0:T(8,128)(2,1)S(1)}, u32[]{:S(2)}, u32[]{:S(2)}) async-start(bf16[16,256,256]{1,2,0:T(8,128)(2,1)} %broadcast_in_dim.6), calls=%async_computation | async-start | bytes 4194304 | tf_op jit(solution)/shard_map/all_to_all | solution.py:9
  50.3 3.7 %copy-start.3 = (bf16[4096,512]{1,0:T(8,128)(2,1)S(1)}, bf16[4096,512]{1,0:T(8,128)(2,1)}, u32[]{:S(2)}) copy-start(bf16[4096,512]{1,0:T(8,128)(2,1)} %param.11) | copy-start | bytes 12582916
  50.3 3.7 %copy-start.5 = (f32[512]{0:T(512)S(1)}, f32[512]{0:T(512)}, u32[]{:S(2)}) copy-start(f32[512]{0:T(512)} %param.12) | copy-start | bytes 6148
  56.0 10.3 %all-to-all-start.1 = ((f32[16,1,256]{2,1,0:T(1,128)}), f32[16,1,256]{2,1,0:T(1,128)S(1)}, u32[]{:S(2)}, u32[]{:S(2)}) async-start(f32[16,1,256]{2,1,0:T(1,128)} %broadcast_in_dim.7), calls=%async_computation.1 | async-start | bytes 32768 | tf_op jit(solution)/shard_map/all_to_all | solution.py:9
  70.1 18.3 %all-to-all-start.2 = ((bf16[16,1,192]{2,1,0:T(2,128)(2,1)}), bf16[16,1,192]{2,1,0:T(2,128)(2,1)S(1)}, u32[]{:S(2)}, u32[]{:S(2)}) async-start(bf16[16,1,192]{2,1,0:T(2,128)(2,1)} %all_to_all.24), calls=%async_computation.2 | async-start | bytes 32768 | tf_op jit(solution)/shard_map/all_to_all | solution.py:56
  114.2 44.0 %all-to-all-start.4 = ((bf16[16,192,256]{2,1,0:T(8,128)(2,1)}), bf16[16,192,256]{2,1,0:T(8,128)(2,1)S(1)}, u32[]{:S(2)}, u32[]{:S(2)}) async-start(bf16[16,192,256]{2,1,0:T(8,128)(2,1)} %all_to_all.30), calls=%async_computation.4 | async-start | bytes 3145728 | tf_op jit(solution)/shard_map/all_to_all | solution.py:44
  119.3 105.9 %all-gather.8.cloned.1.call-start = ((), (), s32[]{:S(2)}) async-start(), calls=%async_computation.7 | async-start | bytes 11698176 | tf_op jit(solution)/shard_map/all_gather | solution.py:68
  121.0 7.0 %copy-start.4 = (bf16[192,896]{1,0:T(8,128)(2,1)S(1)}, bf16[192,896]{1,0:T(8,128)(2,1)}, u32[]{:S(2)}) copy-start(bf16[192,896]{1,0:T(8,128)(2,1)} %param.17) | copy-start | bytes 1032196
Sparse Core Ops, SparseCore 0:
  9.8 64.9 all-gather.3
  76.7 51.3 all-gather.5
  158.4 66.7 all-gather.7
